TPU v7x, 32 devices: a whole 2x2x4 slice. The times are simulated.
32 devices in a mesh: wide: 16 (over z, x, core), narrow: 2 (over y).
Axes of the slice: x: 2, y: 2, z: 4, core: 2. Of those that a mesh axis runs over, the one named last changes fastest.
Arguments:
- latents: bfloat16 [65536, 1024], P(('wide', 'narrow')), may hold values from -6 to 6
- cotangent: bfloat16 [65536, 1024], P(('wide', 'narrow')), may hold values from -6 to 6
- crop_counts: int32 [16], replicated, may hold values from 1 to 8, as said below
- image_device: int32 [16], replicated, may hold values from 0 to 15, as said below
- query_weight: bfloat16 [1024, 1024], P(None, 'narrow'), may hold values from -0.1875 to 0.1875
- key_weight: bfloat16 [1024, 1024], P(None, 'narrow'), may hold values from -0.1875 to 0.1875
- value_weight: bfloat16 [1024, 1024], P(None, 'narrow'), may hold values from -0.1875 to 0.1875
- out_weight: bfloat16 [1024, 1024], P('narrow'), may hold values from -2 to 2
- up_weight: bfloat16 [1024, 1024], P(None, 'narrow'), may hold values from -0.1875 to 0.1875
- down_weight: bfloat16 [1024, 1024], P('narrow'), may hold values from -0.1875 to 0.1875
- query_bias: bfloat16 [1024], P('narrow'), may hold values from -3 to 3
- value_bias: bfloat16 [1024], P('narrow'), may hold values from -3 to 3
- up_bias: bfloat16 [1024], P('narrow'), may hold values from -3 to 3
- out_bias: float32 [1024], replicated, may hold values from -2 to 2
- down_bias: float32 [1024], replicated, may hold values from -2 to 2
- first_gain: float32 [1024], replicated, may hold values from 0.5 to 1.5
- first_shift: float32 [1024], replicated, may hold values from -1.2 to 1.2
- second_gain: float32 [1024], replicated, may hold values from 0.5 to 1.5
- second_shift: float32 [1024], replicated, may hold values from -1.2 to 1.2
Outputs:
- block_output: bfloat16 [65536, 1024], P(('wide', 'narrow'))
- latents_gradient: float32 [65536, 1024], P(('wide', 'narrow'))
- query_weight_gradient: float32 [1024, 1024], P(None, 'narrow')
- key_weight_gradient: float32 [1024, 1024], P(None, 'narrow')
- value_weight_gradient: float32 [1024, 1024], P(None, 'narrow')
- out_weight_gradient: float32 [1024, 1024], P('narrow')
- up_weight_gradient: float32 [1024, 1024], P(None, 'narrow')
- down_weight_gradient: float32 [1024, 1024], P('narrow')
- query_bias_gradient: float32 [1024], P('narrow')
- value_bias_gradient: float32 [1024], P('narrow')
- up_bias_gradient: float32 [1024], P('narrow')
- out_bias_gradient: float32 [1024], replicated
- down_bias_gradient: float32 [1024], replicated
- first_gain_gradient: float32 [1024], replicated
- first_shift_gradient: float32 [1024], replicated
- second_gain_gradient: float32 [1024], replicated
- second_shift_gradient: float32 [1024], replicated
Inputs may be any that keep to these rules, and one draw needn't show every extreme that they name: `crop_counts`: each image holds 1 to 8 crops; the images of one wide index hold 8 crops or fewer together, and some wide index holds exactly 8. `image_device`: every wide index receives exactly one image.
All inputs are finite; a program needn't handle non-finite values.
Results may differ from a plain program's by a relative error of at most 0.02.
Values may be sent and summed in bfloat16 or wider, within the bound.
No kernel may reach another device: no remote copies, remote signals or barrier semaphores. Data moves between devices by JAX's collectives and lax.ppermute only.
A program may use at most 192 MiB of HBM per device.

v0:
```python
from functools import partial
import math

import jax
import jax.numpy as jnp
from jax import lax
from jax.sharding import PartitionSpec as P

HS = 128
CROP = 512


EPSILON = 1e-05


def normalize(values, gain, shift):
    center = values - jnp.mean(values, axis=-1, keepdims=True)
    inverse = lax.rsqrt(jnp.mean(center * center, axis=-1, keepdims=True) + EPSILON)
    unit = center * inverse
    return (unit * gain + shift, unit, inverse)


def normalize_back(upstream, unit, inverse, gain):
    scaled = upstream * gain
    inner = scaled - jnp.mean(scaled, axis=-1, keepdims=True)
    inner = inner - unit * jnp.mean(scaled * unit, axis=-1, keepdims=True)
    return (inner * inverse, jnp.sum(upstream * unit, axis=0), jnp.sum(upstream, axis=0))


def matmul(left, right):
    return jnp.dot(left, right, preferred_element_type=jnp.float32)


def matmul_left(left, right):
    return lax.dot_general(
        left, right, (((0,), (0,)), ((), ())), preferred_element_type=jnp.float32
    )


def matmul_right(left, right):
    return lax.dot_general(
        left, right, (((1,), (1,)), ((), ())), preferred_element_type=jnp.float32
    )


def crop_shape(array):
    count, width = array.shape
    return array.reshape(count // CROP, CROP, width // HS, HS)


def attend_forward(query, keys, values):
    scale = 1.0 / math.sqrt(HS)

    def one_crop(item):
        crop_query, crop_keys, crop_values = item
        scores = (
            jnp.einsum("qhd,khd->hqk", crop_query, crop_keys, preferred_element_type=jnp.float32)
            * scale
        )
        highest = jnp.max(scores, axis=-1, keepdims=True)
        weights = jnp.exp(scores - highest)
        total = jnp.sum(weights, axis=-1, keepdims=True)
        probs = (weights / total).astype(jnp.bfloat16)
        mixed = jnp.einsum("hqk,khd->qhd", probs, crop_values, preferred_element_type=jnp.float32)
        return (mixed.astype(jnp.bfloat16), (highest + jnp.log(total))[..., 0])

    mixed, logsum = lax.map(one_crop, (crop_shape(query), crop_shape(keys), crop_shape(values)))
    return (mixed.reshape(query.shape), logsum)


def attend_back(query, keys, values, logsum, upstream):
    scale = 1.0 / math.sqrt(HS)

    def one_crop(item):
        crop_query, crop_keys, crop_values, crop_logsum, crop_up = item
        scores = (
            jnp.einsum("qhd,khd->hqk", crop_query, crop_keys, preferred_element_type=jnp.float32)
            * scale
        )
        probs = jnp.exp(scores - crop_logsum[..., None])
        values_raw = jnp.einsum(
            "hqk,qhd->khd", probs.astype(jnp.bfloat16), crop_up, preferred_element_type=jnp.float32
        )
        probs_grad = jnp.einsum(
            "qhd,khd->hqk", crop_up, crop_values, preferred_element_type=jnp.float32
        )
        inner = jnp.sum(probs * probs_grad, axis=-1, keepdims=True)
        scores_grad = (probs * (probs_grad - inner)).astype(jnp.bfloat16)
        query_grad = (
            jnp.einsum("hqk,khd->qhd", scores_grad, crop_keys, preferred_element_type=jnp.float32)
            * scale
        )
        keys_grad = (
            jnp.einsum("hqk,qhd->khd", scores_grad, crop_query, preferred_element_type=jnp.float32)
            * scale
        )
        return (
            query_grad.astype(jnp.bfloat16),
            keys_grad.astype(jnp.bfloat16),
            values_raw.astype(jnp.bfloat16),
        )

    items = (crop_shape(query), crop_shape(keys), crop_shape(values), logsum, crop_shape(upstream))
    query_grad, keys_grad, values_grad = lax.map(one_crop, items)
    return (
        query_grad.reshape(query.shape),
        keys_grad.reshape(query.shape),
        values_grad.reshape(query.shape),
    )


def on_device(
    latents,
    cotangent,
    crop_counts,
    image_device,
    query_weight,
    key_weight,
    value_weight,
    out_weight,
    up_weight,
    down_weight,
    query_bias,
    value_bias,
    up_bias,
    out_bias,
    down_bias,
    first_gain,
    first_shift,
    second_gain,
    second_shift,
):
    count = latents.shape[0]
    owned = jnp.sum(jnp.where(image_device == lax.axis_index("wide"), crop_counts, 0))
    first_row = lax.axis_index("narrow") * count
    crop_index = (first_row + jnp.arange(count, dtype=jnp.int32)) // CROP
    live = (crop_index < owned).astype(jnp.float32)[:, None]
    query_full, key_full, value_full, up_full = (query_weight, key_weight, value_weight, up_weight)
    out_full, down_full = (out_weight, down_weight)
    qbias_full, vbias_full, upbias_full = (query_bias, value_bias, up_bias)
    latent_rows = latents.astype(jnp.float32)
    first_normed, first_unit, first_inverse = normalize(latent_rows, first_gain, first_shift)
    first_all = lax.all_gather(first_normed.astype(jnp.bfloat16), "narrow", axis=0, tiled=True)
    query = (matmul(first_all, query_full) + qbias_full).astype(jnp.bfloat16)
    keys = matmul(first_all, key_full).astype(jnp.bfloat16)
    values = (matmul(first_all, value_full) + vbias_full).astype(jnp.bfloat16)
    attended, logsum = attend_forward(query, keys, values)
    hidden = (
        latent_rows
        + lax.psum_scatter(
            matmul(attended, out_full).astype(jnp.bfloat16),
            "narrow",
            scatter_dimension=0,
            tiled=True,
        ).astype(jnp.float32)
        + out_bias
    )
    second_normed, second_unit, second_inverse = normalize(hidden, second_gain, second_shift)
    second_all = lax.all_gather(second_normed.astype(jnp.bfloat16), "narrow", axis=0, tiled=True)
    before = matmul(second_all, up_full) + upbias_full
    gelu_value, gelu_pull = jax.vjp(partial(jax.nn.gelu, approximate=False), before)
    activated = gelu_value.astype(jnp.bfloat16)
    result = (
        hidden
        + lax.psum_scatter(
            matmul(
                lax.dynamic_slice_in_dim(
                    activated, jnp.int32(0), lax.axis_size("narrow") * count, 0
                ),
                down_full,
            ).astype(jnp.bfloat16),
            "narrow",
            scatter_dimension=0,
            tiled=True,
        ).astype(jnp.float32)
        + down_bias
    )
    block_output = (result * live).astype(jnp.bfloat16)
    top_grad = cotangent.astype(jnp.float32) * live
    down_bias_grad = jnp.sum(top_grad, axis=0)
    top_all = lax.all_gather(top_grad.astype(jnp.bfloat16), "narrow", axis=0, tiled=True)
    down_grad = matmul_left(activated, top_all)
    activated_grad = matmul_right(top_all, down_full)
    before_grad = gelu_pull(activated_grad)[0].astype(jnp.bfloat16)
    upbias_grad = jnp.sum(before_grad.astype(jnp.float32), axis=0)
    up_grad = matmul_left(second_all, before_grad)
    second_grad = lax.psum_scatter(
        matmul_right(before_grad, up_full).astype(jnp.bfloat16),
        "narrow",
        scatter_dimension=0,
        tiled=True,
    ).astype(jnp.float32)
    hidden_part, second_gain_grad, second_shift_grad = normalize_back(
        second_grad, second_unit, second_inverse, second_gain
    )
    hidden_grad = top_grad + hidden_part
    out_bias_grad = jnp.sum(hidden_grad, axis=0)
    hidden_all = lax.all_gather(hidden_grad.astype(jnp.bfloat16), "narrow", axis=0, tiled=True)
    out_grad = matmul_left(attended, hidden_all)
    attended_grad = matmul_right(hidden_all, out_full).astype(jnp.bfloat16)
    query_grad, keys_grad, values_grad = attend_back(query, keys, values, logsum, attended_grad)
    qbias_grad = jnp.sum(query_grad.astype(jnp.float32), axis=0)
    vbias_grad = jnp.sum(values_grad.astype(jnp.float32), axis=0)
    query_wgrad = matmul_left(first_all, query_grad)
    key_wgrad = matmul_left(first_all, keys_grad)
    value_wgrad = matmul_left(first_all, values_grad)
    part = matmul_right(query_grad, query_full)
    part = part + matmul_right(keys_grad, key_full)
    first_grad = lax.psum_scatter(
        (part + matmul_right(values_grad, value_full)).astype(jnp.bfloat16),
        "narrow",
        scatter_dimension=0,
        tiled=True,
    ).astype(jnp.float32)
    input_part, first_gain_grad, first_shift_grad = normalize_back(
        first_grad, first_unit, first_inverse, first_gain
    )
    latents_gradient = hidden_grad + input_part
    matrices = (
        lax.psum(query_wgrad.astype(jnp.bfloat16), "wide").astype(jnp.float32),
        lax.psum(key_wgrad.astype(jnp.bfloat16), "wide").astype(jnp.float32),
        lax.psum(value_wgrad.astype(jnp.bfloat16), "wide").astype(jnp.float32),
        lax.psum(out_grad.astype(jnp.bfloat16), "wide").astype(jnp.float32),
        lax.psum(up_grad.astype(jnp.bfloat16), "wide").astype(jnp.float32),
        lax.psum(down_grad.astype(jnp.bfloat16), "wide").astype(jnp.float32),
        lax.psum(qbias_grad.astype(jnp.bfloat16), "wide").astype(jnp.float32),
        lax.psum(vbias_grad.astype(jnp.bfloat16), "wide").astype(jnp.float32),
        lax.psum(upbias_grad.astype(jnp.bfloat16), "wide").astype(jnp.float32),
    )
    rowwise = lax.psum(
        (
            first_gain_grad,
            first_shift_grad,
            second_gain_grad,
            second_shift_grad,
            out_bias_grad,
            down_bias_grad,
        ),
        ("wide", "narrow"),
    )
    return (
        block_output,
        latents_gradient,
        matrices[0],
        matrices[1],
        matrices[2],
        matrices[3],
        matrices[4],
        matrices[5],
        matrices[6],
        matrices[7],
        matrices[8],
        rowwise[4],
        rowwise[5],
        rowwise[0],
        rowwise[1],
        rowwise[2],
        rowwise[3],
    )


def solution(mesh):
    return jax.shard_map(
        on_device,
        mesh=mesh,
        in_specs=(
            P(("wide", "narrow"), None),
            P(("wide", "narrow"), None),
            P(),
            P(),
            P(None, "narrow"),
            P(None, "narrow"),
            P(None, "narrow"),
            P("narrow", None),
            P(None, "narrow"),
            P("narrow", None),
            P("narrow"),
            P("narrow"),
            P("narrow"),
            P(),
            P(),
            P(),
            P(),
            P(),
            P(),
        ),
        out_specs=(
            P(("wide", "narrow"), None),
            P(("wide", "narrow"), None),
            P(None, "narrow"),
            P(None, "narrow"),
            P(None, "narrow"),
            P("narrow", None),
            P(None, "narrow"),
            P("narrow", None),
            P("narrow"),
            P("narrow"),
            P("narrow"),
            P(),
            P(),
            P(),
            P(),
            P(),
            P(),
        ),
        check_vma=False,
    )
```

profile of v0, /device:TPU:0, one launch (start us, length us, event | category | flops | bytes accessed | tf_op | source)
XLA Modules:
  0.0 1423.9 jit_solution(12782932127262748092)
XLA Ops:
  17.3 106.6 %all-gather.5.cloned.1.call-done = bf16[4096,1024]{1,0:T(8,128)(2,1)} async-done(((bf16[2048,1024]{1,0:T(8,128)(2,1)}), bf16[4096,1024]{1,0:T(8,128)(2,1)}) %all-gather.5.cloned.1.call-update) | async-done | bytes 8388624 | tf_op jit(solution)/shard_map/all_gather | solution.py:143
  123.9 9.4 add_convert_fusion.3
  133.3 7.0 reshape.160
  145.6 9.4 add_convert_fusion.4
  155.0 7.0 reshape.159
  162.0 9.4 convolution_convert_fusion.4
  185.9 53.5 %while.26 = (s32[]{:T(128)}, bf16[8,512,4,128]{1,3,2,0:T(8,128)(2,1)}, f32[8,4,512]{2,1,0:T(4,128)}, bf16[8,512,4,128]{3,2,1,0:T(4,128)(2,1)}, bf16[8,512,4,128]...) while((s32[]{:T(128)}, bf16[8,512,4,128]{1,3,2,0:T(8,128)(2,1)}, f32[8,4,512]{2,1,0:T(4,128)}, ...), condition=%wide.region_5.6_spmd, body=%wide.region_2.5_spmd.sunk | while | flops 546568192 | bytes 16843872 | solution.py:67
  255.2 99.4 %reduce-scatter.5.cloned.1.call-done = bf16[2048,1024]{1,0:T(8,128)(2,1)} async-done(((bf16[4096,1024]{1,0:T(8,128)(2,1)}), bf16[2048,1024]{1,0:T(8,128)(2,1)}) %reduce-scatter.5.cloned.1.call-update) | async-done | bytes 4194320 | tf_op jit(solution)/shard_map/reduce_scatter | solution.py:150
  373.3 97.3 %all-gather.7.cloned.1.call-done = bf16[4096,1024]{1,0:T(8,128)(2,1)} async-done(((bf16[2048,1024]{1,0:T(8,128)(2,1)}), bf16[4096,1024]{1,0:T(8,128)(2,1)}) %all-gather.7.cloned.1.call-update) | async-done | bytes 8388624 | tf_op jit(solution)/shard_map/all_gather | solution.py:159
  470.6 10.3 fusion.90
  480.9 95.1 %all-gather.9.cloned.1.call-done = bf16[4096,1024]{1,0:T(8,128)(2,1)} async-done(((bf16[2048,1024]{1,0:T(8,128)(2,1)}), bf16[4096,1024]{1,0:T(8,128)(2,1)}) %all-gather.9.cloned.1.call-update) | async-done | bytes 8388624 | tf_op jit(solution)/shard_map/all_gather | solution.py:181
  576.0 27.7 %fusion.88 = (bf16[512]{0:T(512)(128)(2,1)}, bf16[4096,512]{1,0:T(8,128)(2,1)S(1)}, f32[4096,512]{1,0:T(8,128)}) fusion(f32[4096,512]{1,0:T(8,128)} %fusion.90, f32[512]{0:T(512)S(1)} %convert_element_type.173, bf16[4096,1024]{1,0:T(8,128)(2,1)} %all-gather.9.cloned.1.call-done, bf16[512,1024]{1,0:T(8,128)(2,1)S(1)} %copy-done), kind=kOutput, calls=%fused_computation.149 | convolution fusion | flops 4450156032 | bytes 30411776 | tf_op jit(solution)/shard_map/dot_general | solution.py:41
  605.6 7.2 convolution_convert_fusion
  613.1 8.0 multiply_convert_fusion.2
  630.0 82.4 %reduce-scatter.9.cloned.1.call-done = bf16[2048,1024]{1,0:T(8,128)(2,1)} async-done(((bf16[4096,1024]{1,0:T(8,128)(2,1)}), bf16[2048,1024]{1,0:T(8,128)(2,1)}) %reduce-scatter.9.cloned.1.call-update) | async-done | bytes 4194320 | tf_op jit(solution)/shard_map/reduce_scatter | solution.py:187
  712.3 8.0 fusion.70
  720.4 94.1 %reduce-scatter.7.cloned.1.call-done = bf16[2048,1024]{1,0:T(8,128)(2,1)} async-done(((bf16[4096,1024]{1,0:T(8,128)(2,1)}), bf16[2048,1024]{1,0:T(8,128)(2,1)}) %reduce-scatter.7.cloned.1.call-update) | async-done | bytes 4194320 | tf_op jit(solution)/shard_map/reduce_scatter | solution.py:165
  814.4 12.4 fusion.86
  833.0 10.3 convolution_convert_fusion.5
  843.2 9.1 convolution_convert_fusion.6
  852.3 84.7 %all-gather.11.cloned.1.call-done = bf16[4096,1024]{1,0:T(8,128)(2,1)} async-done(((bf16[2048,1024]{1,0:T(8,128)(2,1)}), bf16[4096,1024]{1,0:T(8,128)(2,1)}) %all-gather.11.cloned.1.call-update) | async-done | bytes 8388624 | tf_op jit(solution)/shard_map/all_gather | solution.py:198
  937.0 9.5 convolution_convert_fusion.3
  960.8 107.1 %while.27 = (s32[]{:T(128)}, bf16[8,512,4,128]{1,3,2,0:T(8,128)(2,1)}, bf16[8,512,4,128]{1,3,2,0:T(8,128)(2,1)}, bf16[8,512,4,128]{1,3,2,0:T(8,128)(2,1)}, bf16[...) while((s32[]{:T(128)}, ...), condition=%wide.region_16.17_spmd, body=%wide.region_14.16_spmd.sunk | while | flops 1356068864 | bytes 38857848 | solution.py:104
  1084.4 9.6 fusion.92
  1094.0 8.4 convolution_convert_fusion.7
  1119.3 10.8 fusion.91
  1130.1 18.8 %add_convert_fusion = bf16[4096,1024]{1,0:T(8,128)(2,1)} fusion(f32[4096,1024]{1,0:T(8,128)} %fusion.91, f32[4096,1024]{1,0:T(8,128)} %fusion.92, bf16[4096,512]{0,1:T(8,128)(2,1)} %bitcast.159, bf16[1024,512]{1,0:T(8,128)(2,1)S(1)} %copy-done.14), kind=kOutput, calls=%fused_computation.55 | convolution fusion | flops 4307550208 | bytes 47185920 | tf_op jit(solution)/shard_map/dot_general | solution.py:41
  1154.7 34.1 %all-reduce.1 = (bf16[512]{0:T(512)(128)(2,1)S(1)}, bf16[512]{0:T(512)(128)(2,1)S(1)}, bf16[512]{0:T(512)(128)(2,1)S(1)}) all-reduce(bf16[512]{0:T(512)(128)(2,1)S(1)} %bitcast.171, bf16[512]{0:T(512)(128)(2,1)S(1)} %bitcast.170, bf16[512]{0:T(512)(128)(2,1)S(1)} %copy-done.36), channel_id=1, replica_groups=mesh['wide'=16,'narrow'=2] {'wide'}, use_global_device_ids=true, to_apply=%region_27.28 | all-reduce | flops 1536 | bytes 6144 | tf_op jit(solution)/shard_map/psum | solution.py:226
  1190.5 68.9 %all-reduce.5.cloned.1.call-done = (bf16[1024,512]{1,0:T(8,128)(2,1)}, bf16[1024,512]{1,0:T(8,128)(2,1)}, bf16[1024,512]{1,0:T(8,128)(2,1)}, bf16[512,1024]{1,0:...) async-done(((bf16[1024,512]{1,0:T(8,128)(2,1)}, bf16[1024,512]{1,0:T(8,128)(2,1)}, bf16[1024,512]{1,0:T(8,128)(2,1)}, bf16[512,1024]{1,0:T(8,128)(2,1)}, ...) | async-done | bytes 6291472 | tf_op jit(solution)/shard_map/psum | solution.py:220
  1272.9 88.3 %reduce-scatter.11.cloned.1.call-done = bf16[2048,1024]{1,0:T(8,128)(2,1)} async-done(((bf16[4096,1024]{1,0:T(8,128)(2,1)}), bf16[2048,1024]{1,0:T(8,128)(2,1)}) %reduce-scatter.11.cloned.1.call-update) | async-done | bytes 4194320 | tf_op jit(solution)/shard_map/reduce_scatter | solution.py:209
  1367.4 40.0 %all-reduce = (f32[1024]{0:T(1024)}, f32[1024]{0:T(1024)}, f32[1024]{0:T(1024)}, f32[1024]{0:T(1024)}, f32[1024]{0:T(1024)}, /*index=5*/f32[1024]{0:T(1024)}) all-reduce(f32[1024]{0:T(1024)S(1)} %copy-done.28, f32[1024]{0:T(1024)S(1)} %copy-done.29, ...), channel_id=1, replica_groups=mesh['wide'=16,'narrow'=2] {'wide','narrow'}, use_global_device_ids=true, to_apply=%region_33.34 | all-reduce | flops 6144 | bytes 49152 | tf_op jit(solution)/shard_map/psum | solution.py:230
  1407.3 9.5 fusion.61
  (285 shorter events, 315.5 us)
Async XLA Ops:
  7.2 568.8 %copy-start = (bf16[512,1024]{1,0:T(8,128)(2,1)S(1)}, bf16[512,1024]{1,0:T(8,128)(2,1)}, u32[]{:S(2)}) copy-start(bf16[512,1024]{1,0:T(8,128)(2,1)} %param.32) | copy-start | bytes 3145732
  7.2 116.7 %all-gather.5.cloned.1.call-start = ((), (), s32[]{:S(2)}) async-start(), calls=%async_computation.4 | async-start | bytes 12582912 | tf_op jit(solution)/shard_map/all_gather | solution.py:143
  10.3 113.6 %copy-start.44 = (bf16[1024,512]{1,0:T(8,128)(2,1)S(1)}, bf16[1024,512]{1,0:T(8,128)(2,1)}, u32[]{:S(2)}) copy-start(bf16[1024,512]{1,0:T(8,128)(2,1)} %param.27) | copy-start | bytes 3145732
  17.0 337.6 %reduce-scatter.5.cloned.1.call-start = ((), (), s32[]{:S(2)}) async-start(), calls=%async_computation.5 | async-start | bytes 12582912 | tf_op jit(solution)/shard_map/reduce_scatter | solution.py:150
  133.3 12.3 copy-start.13
  255.1 99.5 %copy-start.22 = (f32[1024]{0:T(1024)S(1)}, f32[1024]{0:T(1024)}, u32[]{:S(2)}) copy-start(f32[1024]{0:T(1024)} %param.36) | copy-start | bytes 12292
  255.2 107.5 %copy-start.25 = (f32[1024]{0:T(1024)S(1)}, f32[1024]{0:T(1024)}, u32[]{:S(2)}) copy-start(f32[1024]{0:T(1024)} %param.40) | copy-start | bytes 12292
  255.2 107.5 %copy-start.31 = (f32[1024]{0:T(1024)S(1)}, f32[1024]{0:T(1024)}, u32[]{:S(2)}) copy-start(f32[1024]{0:T(1024)} %param.41) | copy-start | bytes 12292
  255.2 215.4 %all-gather.7.cloned.1.call-start = ((), (), s32[]{:S(2)}) async-start(), calls=%async_computation.6 | async-start | bytes 12582912 | tf_op jit(solution)/shard_map/all_gather | solution.py:159
  366.4 104.2 %copy-start.39 = (bf16[1024,512]{1,0:T(8,128)(2,1)S(1)}, bf16[1024,512]{1,0:T(8,128)(2,1)}, u32[]{:S(2)}) copy-start(bf16[1024,512]{1,0:T(8,128)(2,1)} %param.31) | copy-start | bytes 3145732
  366.5 209.5 %all-gather.9.cloned.1.call-start = ((), (), s32[]{:S(2)}) async-start(), calls=%async_computation.8 | async-start | bytes 12582912 | tf_op jit(solution)/shard_map/all_gather | solution.py:181
  372.7 339.6 %reduce-scatter.9.cloned.1.call-start = ((), (), s32[]{:S(2)}) async-start(), calls=%async_computation.9 | async-start | bytes 12582912 | tf_op jit(solution)/shard_map/reduce_scatter | solution.py:187
  612.8 201.6 %reduce-scatter.7.cloned.1.call-start = ((), (), s32[]{:S(2)}) async-start(), calls=%async_computation.7 | async-start | bytes 12582912 | tf_op jit(solution)/shard_map/reduce_scatter | solution.py:165
  629.9 184.5 %copy-start.32 = (f32[1024]{0:T(1024)S(1)}, f32[1024]{0:T(1024)}, u32[]{:S(2)}) copy-start(f32[1024]{0:T(1024)} %param.37) | copy-start | bytes 12292
  629.9 307.1 %all-gather.11.cloned.1.call-start = ((), (), s32[]{:S(2)}) async-start(), calls=%async_computation.10 | async-start | bytes 12582912 | tf_op jit(solution)/shard_map/all_gather | solution.py:198
  832.9 426.5 %all-reduce.5.cloned.1.call-start = ((), (), s32[]{:S(2)}) async-start(), calls=%async_computation.12 | async-start | bytes 12582912 | tf_op jit(solution)/shard_map/psum | solution.py:220
  843.2 93.8 %copy-start.41 = (bf16[512,1024]{1,0:T(8,128)(2,1)S(1)}, bf16[512,1024]{1,0:T(8,128)(2,1)}, u32[]{:S(2)}) copy-start(bf16[512,1024]{1,0:T(8,128)(2,1)} %param.30) | copy-start | bytes 3145732
  1079.5 33.9 %copy-start.8 = (bf16[64,8,8,512]{3,1,2,0:T(8,128)(2,1)}, bf16[64,8,8,512]{3,1,2,0:T(8,128)(2,1)S(1)}, u32[]{:S(2)}) copy-start(bf16[64,8,8,512]{3,1,2,0:T(8,128)(2,1)S(1)} %copy.81) | copy-start | bytes 12582916
  1084.4 23.5 %copy-start.11 = (bf16[64,8,8,512]{3,1,2,0:T(8,128)(2,1)}, bf16[64,8,8,512]{3,1,2,0:T(8,128)(2,1)S(1)}, u32[]{:S(2)}) copy-start(bf16[64,8,8,512]{3,1,2,0:T(8,128)(2,1)S(1)} %copy.79) | copy-start | bytes 12582916
  1084.4 17.9 %slice-start = ((s8[8388608]{0:T(1024)(128)(4,1)}), s8[4194304]{0:T(1024)(128)(4,1)S(1)}, s32[]{:S(2)}) async-start(s8[8388608]{0:T(1024)(128)(4,1)} %bitcast.172), calls=%async_computation.13 | async-start | bytes 8388608
  1119.3 10.9 copy-start.14
  1119.3 241.9 %reduce-scatter.11.cloned.1.call-start = ((), (), s32[]{:S(2)}) async-start(), calls=%async_computation.11 | async-start | bytes 12582912 | tf_op jit(solution)/shard_map/reduce_scatter | solution.py:209
  1259.4 10.3 copy-start.16
  1259.4 11.9 copy-start.15
  1262.4 98.8 %copy-start.19 = (f32[2048]{0:T(1024)S(1)}, f32[2048]{0:T(1024)}, u32[]{:S(2)}) copy-start(f32[2048]{0:T(1024)} %copy-done.18) | copy-start | bytes 24580
  1262.4 98.8 %copy-start.21 = (f32[2048]{0:T(1024)S(1)}, f32[2048]{0:T(1024)}, u32[]{:S(2)}) copy-start(f32[2048]{0:T(1024)} %copy-done.20) | copy-start | bytes 24580
  1262.4 98.8 %copy-start.24 = (f32[1024]{0:T(1024)S(1)}, f32[1024]{0:T(1024)}, u32[]{:S(2)}) copy-start(f32[1024]{0:T(1024)} %param.38) | copy-start | bytes 12292
  1268.1 99.2 %copy-start.26 = (f32[1024]{0:T(1024)S(1)}, f32[1024]{0:T(1024)}, u32[]{:S(2)}) copy-start(f32[1024]{0:T(1024)} %get-tuple-element.134) | copy-start | bytes 12292
  1268.1 99.2 %copy-start.27 = (f32[1024]{0:T(1024)S(1)}, f32[1024]{0:T(1024)}, u32[]{:S(2)}) copy-start(f32[1024]{0:T(1024)} %get-tuple-element.140) | copy-start | bytes 12292
  1268.1 99.2 %copy-start.28 = (f32[1024]{0:T(1024)S(1)}, f32[1024]{0:T(1024)}, u32[]{:S(2)}) copy-start(f32[1024]{0:T(1024)} %get-tuple-element.187) | copy-start | bytes 12292
  1268.1 99.2 %copy-start.29 = (f32[1024]{0:T(1024)S(1)}, f32[1024]{0:T(1024)}, u32[]{:S(2)}) copy-start(f32[1024]{0:T(1024)} %get-tuple-element.199) | copy-start | bytes 12292
  1367.3 49.5 %copy-start.1 = (bf16[512,1024]{1,0:T(8,128)(2,1)S(1)}, bf16[512,1024]{1,0:T(8,128)(2,1)}, u32[]{:S(2)}) copy-start(bf16[512,1024]{1,0:T(8,128)(2,1)} %param.32) | copy-start | bytes 3145732
  (27 other events, 153.8 us)
Sparse Core Ops, SparseCore 0:
  17.1 106.6 all-gather.4
  255.3 99.3 reduce-scatter.4
  366.6 103.9 all-gather.6
  472.0 103.9 all-gather.8
  613.0 99.3 reduce-scatter.8
  715.1 99.3 reduce-scatter.6
  833.0 103.9 all-gather.10
  1119.4 139.9 all-reduce.4
  1261.7 99.4 reduce-scatter.10
where the time goes:
time: 1430 us; the launch traced here: 1420 us
  waiting for transfers between devices  817 us (57%)
  matrix products  289 us (20%)
  other arithmetic  114 us (8%)
  local copies, waits for them, and re-layouts  113 us (8%)
  blocking collectives  74.1 us (5%)
  between operations  15 us (1%)
    all_gather x1, waiting for transfers between devices, on_device(): lax.all_gather(first_normed.astype(jnp.bfloat16), 'narrow', axis=0, tiled...  107 us
    reduce_scatter x1, waiting for transfers between devices, on_device(): lax.psum_scatter(matmul(attended, out_full).astype(jnp.bfloat16), 'narrow...  99.4 us
    all_gather x1, waiting for transfers between devices, on_device(): lax.all_gather(second_normed.astype(jnp.bfloat16), 'narrow', axis=0, tile...  97.3 us
    all_gather x1, waiting for transfers between devices, on_device(): lax.all_gather(top_grad.astype(jnp.bfloat16), 'narrow', axis=0, tiled=True)  95.1 us
    reduce_scatter x1, waiting for transfers between devices, on_device(): lax.psum_scatter(matmul(lax.dynamic_slice_in_dim(activated, jnp.int32(0),...  94.1 us
    reduce_scatter x1, waiting for transfers between devices, on_device(): lax.psum_scatter((part + matmul_right(values_grad, value_full)).astype(jn...  88.3 us
    all_gather x1, waiting for transfers between devices, on_device(): lax.all_gather(hidden_grad.astype(jnp.bfloat16), 'narrow', axis=0, tiled=...  84.7 us
    dot_general x6, matrix products, matmul_right(): lax.dot_general(left, right, (((1,), (1,)), ((), ())), preferred_element_...  83.6 us
  transfers between devices with their start and end apart: 9, of which 9 were waited for; matrix products, arithmetic and copies ran while one was open for 8% of the time, Pallas kernels for 0%

commit v1 on v0

v1 whole, which is shorter than its diff:
```python
from functools import partial
import math

import jax
import jax.numpy as jnp
from jax import lax
from jax.sharding import PartitionSpec as P

HS = 128
CROP = 512


EPSILON = 1e-05


def normalize(values, gain, shift):
    center = values - jnp.mean(values, axis=-1, keepdims=True)
    inverse = lax.rsqrt(jnp.mean(center * center, axis=-1, keepdims=True) + EPSILON)
    unit = center * inverse
    return (unit * gain + shift, unit, inverse)


def normalize_back(upstream, unit, inverse, gain):
    scaled = upstream * gain
    inner = scaled - jnp.mean(scaled, axis=-1, keepdims=True)
    inner = inner - unit * jnp.mean(scaled * unit, axis=-1, keepdims=True)
    return (inner * inverse, jnp.sum(upstream * unit, axis=0), jnp.sum(upstream, axis=0))


def matmul(left, right):
    return jnp.dot(left, right, preferred_element_type=jnp.float32)


def matmul_left(left, right):
    return lax.dot_general(
        left, right, (((0,), (0,)), ((), ())), preferred_element_type=jnp.float32
    )


def matmul_right(left, right):
    return lax.dot_general(
        left, right, (((1,), (1,)), ((), ())), preferred_element_type=jnp.float32
    )


def heads_of(array):
    count, width = array.shape
    return array.reshape(count // CROP, CROP, width // HS, HS).transpose(0, 2, 1, 3)


def rows_of(array):
    crops, heads, rows, size = array.shape
    return array.transpose(0, 2, 1, 3).reshape(crops * rows, heads * size)


def batched(left, right, left_dim, right_dim):
    return lax.dot_general(
        left,
        right,
        (((left_dim,), (right_dim,)), ((0, 1), (0, 1))),
        preferred_element_type=jnp.float32,
    )


def pair_perm(size, bit):
    return [(i, i ^ bit) for i in range(size)]


class Links:
    def __init__(self):
        self.wide = lax.axis_size("wide")
        self.narrow = lax.axis_size("narrow")
        self.paired = self.narrow == 2 and self.wide == 16
        self.index = lax.axis_index("wide")
        self.core = self.index % 2

    def swap(self, array, bit):
        return lax.ppermute(array, "wide", pair_perm(self.wide, bit))

    def swap_narrow(self, array):
        return lax.ppermute(array, "narrow", [(0, 1), (1, 0)])

    def others(self, weight, axis):
        if not self.paired:
            whole = lax.all_gather(weight, "narrow", axis=0, tiled=False)
            whole = jnp.roll(whole, -lax.axis_index("narrow"), axis=0)[1:]
            return jnp.concatenate([whole[i] for i in range(self.narrow - 1)], axis=axis)
        half = weight.shape[0] // 2
        mine = lax.dynamic_slice_in_dim(weight, self.core * half, half, 0)
        near = self.swap_narrow(mine)
        far = self.swap(near, 1)
        first = jnp.where(self.core == 0, near, far)
        second = jnp.where(self.core == 0, far, near)
        return jnp.concatenate([first, second], axis=0)

    def halves(self, array, bit):
        half = array.shape[0] // 2
        position = (self.index // bit) % 2
        keep = lax.dynamic_slice_in_dim(array, position * half, half, 0)
        give = lax.dynamic_slice_in_dim(array, (1 - position) * half, half, 0)
        return keep, give

    def add(self, left, right):
        return (left.astype(jnp.float32) + right.astype(jnp.float32)).astype(jnp.bfloat16)

    def join(self, mine, other, bit):
        position = (self.index // bit) % 2
        first = jnp.where(position == 0, mine, other)
        second = jnp.where(position == 0, other, mine)
        return jnp.concatenate([first, second], axis=0)

    def reduce_matrix(self, own, other, axis):
        own = own.astype(jnp.bfloat16)
        other = other.astype(jnp.bfloat16)
        if not self.paired:
            width = own.shape[axis]
            parts = jnp.stack(
                [own]
                + [
                    lax.slice_in_dim(other, i * width, (i + 1) * width, axis=axis)
                    for i in range(self.narrow - 1)
                ]
            )
            parts = jnp.roll(parts, lax.axis_index("narrow"), axis=0)
            mine = lax.psum_scatter(parts, "narrow", scatter_dimension=0, tiled=True)[0]
            return lax.psum(mine, "wide").astype(jnp.float32)
        keep_own, give_own = self.halves(own, 1)
        keep_other, give_other = self.halves(other, 1)
        keep_other = self.add(keep_other, self.swap(give_other, 1))
        keep = self.add(keep_own, self.swap(give_own, 1))
        keep = self.add(keep, self.swap_narrow(keep_other))
        for bit in (2, 4, 8):
            keep, give = self.halves(keep, bit)
            keep = self.add(keep, self.swap(give, bit))
        for bit in (8, 4, 2, 1):
            keep = self.join(keep, self.swap(keep, bit), bit)
        return keep.astype(jnp.float32)

    def reduce_all(self, rows):
        if not self.paired:
            return lax.psum(rows, ("wide", "narrow"))
        rows = rows + self.swap(rows, 1)
        rows = rows + self.swap_narrow(rows)
        for bit in (2, 4, 8):
            rows = rows + self.swap(rows, bit)
        return rows


def on_device(
    latents,
    cotangent,
    crop_counts,
    image_device,
    query_weight,
    key_weight,
    value_weight,
    out_weight,
    up_weight,
    down_weight,
    query_bias,
    value_bias,
    up_bias,
    out_bias,
    down_bias,
    first_gain,
    first_shift,
    second_gain,
    second_shift,
):
    links = Links()
    count = latents.shape[0]
    narrow = links.narrow
    owned = jnp.sum(jnp.where(image_device == lax.axis_index("wide"), crop_counts, 0))
    first_row = lax.axis_index("narrow") * count
    crop_index = (first_row + jnp.arange(count, dtype=jnp.int32)) // CROP
    live = (crop_index < owned).astype(jnp.float32)[:, None]
    biases = jnp.stack([query_bias, value_bias, up_bias])
    biases = lax.all_gather(biases, "narrow", axis=0)
    biases = jnp.roll(biases, -lax.axis_index("narrow"), axis=0)
    biases = biases.transpose(1, 0, 2).reshape(3, -1).astype(jnp.float32)
    units = query_weight.shape[1]
    query_full = jnp.concatenate([query_weight, links.others(query_weight, 1)], axis=1)
    key_full = jnp.concatenate([key_weight, links.others(key_weight, 1)], axis=1)
    value_full = jnp.concatenate([value_weight, links.others(value_weight, 1)], axis=1)
    out_full = jnp.concatenate([out_weight, links.others(out_weight, 0)], axis=0)
    up_full = jnp.concatenate([up_weight, links.others(up_weight, 1)], axis=1)
    down_full = jnp.concatenate([down_weight, links.others(down_weight, 0)], axis=0)
    scale = 1.0 / math.sqrt(HS)

    latent_rows = latents.astype(jnp.float32)
    first_normed, first_unit, first_inverse = normalize(latent_rows, first_gain, first_shift)
    first_all = first_normed.astype(jnp.bfloat16)
    query = heads_of((matmul(first_all, query_full) + biases[0]).astype(jnp.bfloat16))
    keys = heads_of(matmul(first_all, key_full).astype(jnp.bfloat16))
    values = heads_of((matmul(first_all, value_full) + biases[1]).astype(jnp.bfloat16))
    scores = batched(query, keys, 3, 3) * scale
    probs = jax.nn.softmax(scores, axis=-1)
    probs_low = probs.astype(jnp.bfloat16)
    attended = rows_of(batched(probs_low, values, 3, 2).astype(jnp.bfloat16))
    hidden = latent_rows + matmul(attended, out_full) + out_bias
    second_normed, second_unit, second_inverse = normalize(hidden, second_gain, second_shift)
    second_all = second_normed.astype(jnp.bfloat16)
    before = matmul(second_all, up_full) + biases[2]
    gelu_value, gelu_pull = jax.vjp(partial(jax.nn.gelu, approximate=False), before)
    activated = gelu_value.astype(jnp.bfloat16)
    result = hidden + matmul(activated, down_full) + down_bias
    block_output = (result * live).astype(jnp.bfloat16)
    top_grad = cotangent.astype(jnp.float32) * live
    down_bias_grad = jnp.sum(top_grad, axis=0)
    top_all = top_grad.astype(jnp.bfloat16)
    down_grad = matmul_left(activated, top_all)
    activated_grad = matmul_right(top_all, down_full)
    before_grad = gelu_pull(activated_grad)[0].astype(jnp.bfloat16)
    upbias_grad = jnp.sum(before_grad.astype(jnp.float32), axis=0)
    up_grad = matmul_left(second_all, before_grad)
    second_grad = matmul_right(before_grad, up_full)
    hidden_part, second_gain_grad, second_shift_grad = normalize_back(
        second_grad, second_unit, second_inverse, second_gain
    )
    hidden_grad = top_grad + hidden_part
    out_bias_grad = jnp.sum(hidden_grad, axis=0)
    hidden_all = hidden_grad.astype(jnp.bfloat16)
    out_grad = matmul_left(attended, hidden_all)
    attended_grad = heads_of(matmul_right(hidden_all, out_full).astype(jnp.bfloat16))
    values_raw = batched(probs_low, attended_grad, 2, 2)
    probs_grad = batched(attended_grad, values, 3, 3)
    inner = jnp.sum(probs * probs_grad, axis=-1, keepdims=True)
    scores_grad = (probs * (probs_grad - inner)).astype(jnp.bfloat16)
    query_grad = rows_of((batched(scores_grad, keys, 3, 2) * scale).astype(jnp.bfloat16))
    keys_grad = rows_of((batched(scores_grad, query, 2, 2) * scale).astype(jnp.bfloat16))
    values_grad = rows_of(values_raw.astype(jnp.bfloat16))
    qbias_grad = jnp.sum(query_grad.astype(jnp.float32), axis=0)
    vbias_grad = jnp.sum(values_grad.astype(jnp.float32), axis=0)
    query_wgrad = matmul_left(first_all, query_grad)
    key_wgrad = matmul_left(first_all, keys_grad)
    value_wgrad = matmul_left(first_all, values_grad)
    part = matmul_right(query_grad, query_full)
    part = part + matmul_right(keys_grad, key_full)
    first_grad = part + matmul_right(values_grad, value_full)
    input_part, first_gain_grad, first_shift_grad = normalize_back(
        first_grad, first_unit, first_inverse, first_gain
    )
    latents_gradient = hidden_grad + input_part

    def shared_units(vector):
        if narrow == 2:
            swapped = jnp.concatenate([vector[units:], vector[:units]])
            return jnp.where(lax.axis_index("narrow") == 0, vector, swapped)
        return jnp.roll(vector.reshape(narrow, units), lax.axis_index("narrow"), axis=0).reshape(-1)

    rows = jnp.stack(
        [
            first_gain_grad,
            first_shift_grad,
            second_gain_grad,
            second_shift_grad,
            out_bias_grad,
            down_bias_grad,
            shared_units(qbias_grad),
            shared_units(vbias_grad),
            shared_units(upbias_grad),
        ]
    )
    rowwise = links.reduce_all(rows)
    own = lax.dynamic_slice_in_dim(rowwise[6:], lax.axis_index("narrow") * units, units, 1)
    matrices = (
        links.reduce_matrix(query_wgrad[:, :units], query_wgrad[:, units:], 1),
        links.reduce_matrix(key_wgrad[:, :units], key_wgrad[:, units:], 1),
        links.reduce_matrix(value_wgrad[:, :units], value_wgrad[:, units:], 1),
        links.reduce_matrix(out_grad[:units], out_grad[units:], 0),
        links.reduce_matrix(up_grad[:, :units], up_grad[:, units:], 1),
        links.reduce_matrix(down_grad[:units], down_grad[units:], 0),
    )
    return (
        block_output,
        latents_gradient,
        *matrices,
        own[0],
        own[1],
        own[2],
        rowwise[4],
        rowwise[5],
        rowwise[0],
        rowwise[1],
        rowwise[2],
        rowwise[3],
    )


def solution(mesh):
    rows = P(("wide", "narrow"), None)
    columns = P(None, "narrow")
    units = P("narrow", None)
    vector = P("narrow")
    whole = P()
    return jax.shard_map(
        on_device,
        mesh=mesh,
        in_specs=(
            rows,
            rows,
            whole,
            whole,
            columns,
            columns,
            columns,
            units,
            columns,
            units,
            vector,
            vector,
            vector,
            whole,
            whole,
            whole,
            whole,
            whole,
            whole,
        ),
        out_specs=(
            rows,
            rows,
            columns,
            columns,
            columns,
            units,
            columns,
            units,
            vector,
            vector,
            vector,
            whole,
            whole,
            whole,
            whole,
            whole,
            whole,
        ),
        check_vma=False,
    )
```

time: 1430 us -> 725 us (0.51)
  waiting for transfers between devices: 817 us -> 125 us
  starting transfers between devices: 1.22 us -> 62.7 us
  blocking collectives: 74.1 us -> 44.4 us
  matrix products: 289 us -> 262 us
  local copies, waits for them, and re-layouts: 113 us -> 95.9 us
    all_gather x4 -> x0, waiting for transfers between devices: 384 us -> none  [the longest x1 107 us: on_device(): lax.all_gather(first_normed.astype(jnp.bfloat16), 'narrow', axis=0, tiled...]
    reduce_scatter x4 -> x0, waiting for transfers between devices: 364 us -> none  [the longest x1 99.4 us: on_device(): lax.psum_scatter(matmul(attended, out_full).astype(jnp.bfloat16), 'narrow...]
    ppermute x0 -> x77, waiting for transfers between devices: none -> 125 us  [the longest x13 63 us: swap_narrow(): return lax.ppermute(array, 'narrow', [(0, 1), (1, 0)])]
    psum x2 -> x0, blocking collectives: 74.1 us -> none  [the longest x1 40 us: on_device(): lax.psum((first_gain_grad, first_shift_grad, second_gain_grad, second_shi...]
    psum x1 -> x0, waiting for transfers between devices: 68.9 us -> none  [on_device(): lax.psum(query_wgrad.astype(jnp.bfloat16), 'wide').astype(jnp.float32)]
    ppermute x0 -> x77, starting transfers between devices: none -> 62.7 us  [the longest x64 45 us: swap(): return lax.ppermute(array, 'wide', pair_perm(self.wide, bit))]
    all_gather x0 -> x1, blocking collectives: none -> 44.4 us  [on_device(): biases = lax.all_gather(biases, 'narrow', axis=0)]
    sub x0 -> x1, other arithmetic: none -> 35.4 us  [on_device(): probs = jax.nn.softmax(scores, axis=-1)]
  transfers between devices with their start and end apart: 9 -> 77, of which waited for: 9 -> 35; matrix products, arithmetic and copies ran while one was open for 8% -> 37% of each run, Pallas kernels for 0% -> 0%
where the time goes in v1:
time: 725 us; the launch traced here: 721 us
  matrix products  262 us (36%)
  other arithmetic  127 us (18%)
  waiting for transfers between devices  125 us (17%)
  local copies, waits for them, and re-layouts  95.9 us (13%)
  starting transfers between devices  62.7 us (9%)
  blocking collectives  44.4 us (6%)
    dot_general x6, matrix products, batched(): lax.dot_general(left, right, (((left_dim,), (right_dim,)), ((0, 1), (0, 1...  98.5 us
    dot_general x6, matrix products, matmul_right(): lax.dot_general(left, right, (((1,), (1,)), ((), ())), preferred_element_...  64.9 us
    ppermute x13, waiting for transfers between devices, swap_narrow(): return lax.ppermute(array, 'narrow', [(0, 1), (1, 0)])  63 us
    dot_general x6, matrix products, matmul(): return jnp.dot(left, right, preferred_element_type=jnp.float32)  62.1 us
    ppermute x64, waiting for transfers between devices, swap(): return lax.ppermute(array, 'wide', pair_perm(self.wide, bit))  62 us
    unnamed x194, local copies, waits for them, and re-layouts  45.6 us
    ppermute x64, starting transfers between devices, swap(): return lax.ppermute(array, 'wide', pair_perm(self.wide, bit))  45 us
    all_gather x1, blocking collectives, on_device(): biases = lax.all_gather(biases, 'narrow', axis=0)  44.4 us
  transfers between devices with their start and end apart: 77, of which 35 were waited for; matrix products, arithmetic and copies ran while one was open for 37% of the time, Pallas kernels for 0%

profile of v1, /device:TPU:0, one launch (start us, length us, event | category | flops | bytes accessed | tf_op | source)
XLA Modules:
  0.0 720.6 jit_solution(2542267815018079838)
XLA Ops:
  18.4 44.4 %all-gather.1 = bf16[2,3,512]{2,1,0:T(4,128)(2,1)S(1)} all-gather(bf16[1,3,512]{2,1,0:T(4,128)(2,1)S(1)} %maximum_bitcast_fusion), channel_id=2, replica_groups=mesh['wide'=16,'narrow'=2] {'narrow'}, dimensions={0}, use_global_device_ids=true | all-gather | bytes 9216 | tf_op jit(solution)/shard_map/all_gather | solution.py:178
  74.1 6.6 copy.79
  89.0 9.1 %collective-permute-done = bf16[512,512]{1,0:T(8,128)(2,1)S(1)} collective-permute-done((bf16[512,512]{1,0:T(8,128)(2,1)}, bf16[512,512]{1,0:T(8,128)(2,1)S(1)}, u32[]{:S(2)}, u32[]{:S(2)}) %collective-permute-start) | collective-permute-done | bytes 524320 | tf_op jit(solution)/shard_map/ppermute | solution.py:81
  98.8 8.0 %fusion.33 = bf16[256,8,8,128]{3,1,2,0:T(8,128)(2,1)S(1)} fusion(f32[1024]{0:T(1024)S(1)} %bitcast.185, bf16[512,512]{1,0:T(8,128)(2,1)S(1)} %get-tuple-element.115, bf16[512,512]{1,0:T(8,128)(2,1)S(1)} %get-tuple-element.114, bf16[1024,512]{1,0:T(8,128)(2,1)} %param.25, bf16[2048,1024]{0,1:T(8,128)(2,1)} %copy.72, f32[1024]{0:T(1024)S(1)} %copy-done.87, ...), kind=kOutput, calls=%fused_computation.68 | convolution fusion | flops 4318035968 | bytes 10514432 | tf_op jit(solution)/shard_map/dot_general | solution.py:31
  127.4 19.3 %fusion.59 = f32[4,8,512,512]{2,3,1,0:T(8,128)} fusion(bf16[4,512,8,128]{3,2,1,0:T(8,128)(2,1)} %bitcast.147, bf16[4,512,8,128]{3,2,1,0:T(8,128)(2,1)} %bitcast.145), kind=kOutput, calls=%fused_computation.94 | convolution fusion | flops 2147483648 | bytes 41943040 | tf_op jit(solution)/shard_map/dot_general | solution.py:57
  146.6 35.4 %fusion.163 = (f32[4,8,512]{2,1,0:T(8,128)S(1)}, f32[4,8,512,512]{2,3,1,0:T(8,128)}) fusion(f32[4,8,512,512]{2,3,1,0:T(8,128)} %fusion.59), kind=kOutput, calls=%fused_computation.349 | output fusion | flops 33554944 | bytes 67174400 | tf_op jit(solution)/shard_map/sub | solution.py:197
  182.0 12.8 %convert_bitcast_fusion.2 = bf16[4,512,8,128]{3,1,2,0:T(8,128)(2,1)S(1)} fusion(bf16[4,512,8,128]{3,2,1,0:T(8,128)(2,1)S(1)} %bitcast.150, f32[4,8,512,512]{2,3,1,0:T(8,128)} %get-tuple-element.171, f32[4,8,512]{2,1,0:T(8,128)S(1)} %get-tuple-element.170), kind=kOutput, calls=%fused_computation.101 | convolution fusion | flops 2166358016 | bytes 42008576 | tf_op jit(solution)/shard_map/dot_general | solution.py:57
  208.3 28.9 %multiply_convert_fusion.4 = (bf16[2048,1024]{1,0:T(8,128)(2,1)}, f32[2048,1024]{1,0:T(8,128)}, f32[2048,1024]{1,0:T(8,128)}) fusion(f32[1024]{0:T(1024)S(1)} %bitcast.182, bf16[2048,1024]{0,1:T(8,128)(2,1)S(1)} %add_convert_fusion.1, bf16[512,512]{1,0:T(8,128)(2,1)S(1)} %get-tuple-element.107, bf16[512,512]{1,0:T(8,128)(2,1)S(1)} %get-tuple-element.106, ...), kind=kOutput, calls=%fused_computation.42 | convolution fusion | flops 4439670784 | bytes 27267072 | tf_op jit(solution)/shard_map/dot_general | solution.py:31
  238.6 15.6 %convert_reduce_fusion.1 = (f32[1024]{0:T(1024)}, bf16[2048,1024]{1,0:T(8,128)(2,1)}) fusion(f32[2048,1024]{1,0:T(8,128)} %get-tuple-element.78, bf16[256,1024]{1,0:T(8,128)(2,1)S(1)} %get-tuple-element.105, bf16[256,1024]{1,0:T(8,128)(2,1)S(1)} %get-tuple-element.104, bf16[512,1024]{1,0:T(8,128)(2,1)S(1)} %copy-done.65, ...), kind=kOutput, calls=%fused_computation.28 | convolution fusion | flops 4343200768 | bytes 27279360 | tf_op jit(solution)/shard_map/dot_general | solution.py:41
  254.1 8.1 %convolution_convert_fusion = bf16[1024,1024]{1,0:T(8,128)(2,1)} fusion(bf16[2048,1024]{0,1:T(8,128)(2,1)S(1)} %add_convert_fusion.1, bf16[2048,1024]{1,0:T(8,128)(2,1)} %get-tuple-element.182), kind=kOutput, calls=%fused_computation.133 | convolution fusion | flops 4296015872 | bytes 10485760 | tf_op jit(solution)/shard_map/dot_general | solution.py:35
  262.2 9.7 %fusion.165 = (f32[1024]{0:T(1024)}, f32[2048,1024]{1,0:T(8,128)}) fusion(bf16[2048,1024]{1,0:T(8,128)(2,1)S(1)} %copy-done.89, bf16[512,512]{1,0:T(8,128)(2,1)S(1)} %get-tuple-element.107, bf16[512,512]{1,0:T(8,128)(2,1)S(1)} %get-tuple-element.106, bf16[1024,512]{1,0:T(8,128)(2,1)S(1)} %copy-done.58), kind=kOutput, calls=%fused_computation.351 | convolution fusion | flops 4303354880 | bytes 14684160 | tf_op jit(solution)/shard_map/dot_general | solution.py:41
  271.9 9.1 %copy.80 = f32[2048,1024]{0,1:T(8,128)} copy(f32[2048,1024]{1,0:T(8,128)} %get-tuple-element.185) | data formatting | bytes 16777216 | tf_op jit(solution)/shard_map/dot_general | solution.py:41
  281.1 8.1 %multiply_reduce_fusion.2 = (f32[1024]{0:T(1024)}, f32[2048]{0:T(1024)S(1)}, f32[2048]{0:T(1024)S(1)}) fusion(f32[2048,1024]{0,1:T(8,128)} %copy.80, f32[2048,1024]{0,1:T(8,128)} %copy-done, f32[2048]{0:T(1024)S(1)} %add_rsqrt_fusion, f32[2048]{0:T(1024)S(1)} %broadcast_multiply_fusion.4, f32[1024]{0:T(1024)S(1)} %copy-done.69), kind=kLoop, calls=%fused_computation.31 | loop fusion | flops 16772096 | bytes 16818176 | tf_op jit(solution)/shard_map/reduce_sum | solution.py:27
  290.5 7.4 %fusion.149 = (f32[1024]{0:T(1024)}, f32[2048,1024]{0,1:T(8,128)S(1)}, f32[1024]{0:T(1024)}) fusion(f32[2048]{0:T(1024)S(1)} %get-tuple-element.186, f32[2048]{0:T(1024)S(1)} %add_rsqrt_fusion, f32[2048,1024]{0,1:T(8,128)} %copy-done, f32[2048]{0:T(1024)S(1)} %broadcast_multiply_fusion.4, f32[2048]{0:T(1024)S(1)} %get-tuple-element.187, ...), kind=kLoop, calls=%fused_computation.336 | loop fusion | flops 25163776 | bytes 29413376 | tf_op jit(solution)/shard_map/reduce_sum | solution.py:221
  313.2 17.4 %convert_reduce_fusion.2 = (f32[8,128]{1,0:T(8,128)}, bf16[4,512,8,128]{3,1,2,0:T(8,128)(2,1)}) fusion(bf16[4,512,8,128]{3,2,1,0:T(8,128)(2,1)} %bitcast.155, f32[4,8,512,512]{2,3,1,0:T(8,128)} %get-tuple-element.171, f32[4,8,512]{2,1,0:T(8,128)S(1)} %copy-done.57), kind=kOutput, calls=%fused_computation.29 | convolution fusion | flops 2170551296 | bytes 42012672 | tf_op jit(solution)/shard_map/dot_general | solution.py:57
  330.6 25.1 %multiply_reduce_fusion = (f32[4,8,512]{2,1,0:T(8,128)S(1)}, f32[4,8,512,512]{2,3,1,0:T(8,128)}) fusion(f32[4,8,512,512]{2,3,1,0:T(8,128)} %get-tuple-element.171, f32[4,8,512]{2,1,0:T(8,128)S(1)} %copy-done.57, bf16[4,512,8,128]{3,2,1,0:T(8,128)(2,1)} %bitcast.149, bf16[4,512,8,128]{3,2,1,0:T(8,128)(2,1)} %bitcast.156), kind=kOutput, calls=%fused_computation.2 | convolution fusion | flops 2172633088 | bytes 75628544 | tf_op jit(solution)/shard_map/dot_general | solution.py:57
  355.7 28.0 %multiply_convert_fusion = bf16[4,8,512,512]{2,3,1,0:T(8,128)(2,1)} fusion(f32[4,8,512,512]{2,3,1,0:T(8,128)} %get-tuple-element.176, f32[4,8,512]{2,1,0:T(8,128)S(1)} %get-tuple-element.175, f32[4,8,512,512]{2,3,1,0:T(8,128)} %get-tuple-element.171, f32[4,8,512]{2,1,0:T(8,128)S(1)} %copy-done.57), kind=kLoop, calls=%fused_computation.1 | loop fusion | flops 33554432 | bytes 84017152 | tf_op jit(solution)/shard_map/convert_element_type | solution.py:228
  383.7 13.5 %fusion.35 = bf16[4,512,8,128]{3,1,2,0:T(8,128)(2,1)} fusion(bf16[4,8,512,512]{2,3,1,0:T(8,128)(2,1)} %multiply_convert_fusion, bf16[4,512,8,128]{3,2,1,0:T(8,128)(2,1)} %bitcast.146), kind=kOutput, calls=%fused_computation.70 | convolution fusion | flops 2151677952 | bytes 25165824 | tf_op jit(solution)/shard_map/dot_general | solution.py:57
  397.2 10.4 %convert_reduce_fusion.3 = (f32[8,128]{1,0:T(8,128)S(1)}, bf16[4,512,8,128]{3,1,2,0:T(8,128)(2,1)S(1)}) fusion(bf16[4,8,512,512]{2,3,1,0:T(8,128)(2,1)} %multiply_convert_fusion, bf16[4,512,8,128]{3,2,1,0:T(8,128)(2,1)} %bitcast.148), kind=kOutput, calls=%fused_computation.30 | convolution fusion | flops 2155871232 | bytes 25169920 | tf_op jit(solution)/shard_map/dot_general | solution.py:57
  416.5 10.2 %fusion.46 = f32[2048,1024]{0,1:T(8,128)} fusion(bf16[256,8,8,128]{3,2,1,0:T(8,128)(2,1)S(1)} %bitcast.158, bf16[512,512]{1,0:T(8,128)(2,1)S(1)} %copy-done.40, bf16[512,512]{1,0:T(8,128)(2,1)S(1)} %copy-done.38, bf16[1024,512]{1,0:T(8,128)(2,1)S(1)} %copy-done.62), kind=kOutput, calls=%fused_computation.81 | convolution fusion | flops 4301258752 | bytes 14680064 | tf_op jit(solution)/shard_map/dot_general | solution.py:41
  435.6 10.1 %fusion.42 = f32[2048,1024]{0,1:T(8,128)} fusion(bf16[256,8,8,128]{3,2,1,0:T(8,128)(2,1)S(1)} %bitcast.160, bf16[512,512]{1,0:T(8,128)(2,1)S(1)} %copy-done.44, bf16[512,512]{1,0:T(8,128)(2,1)S(1)} %copy-done.42, bf16[1024,512]{1,0:T(8,128)(2,1)S(1)} %copy-done.64), kind=kOutput, calls=%fused_computation.77 | convolution fusion | flops 4301258752 | bytes 14680064 | tf_op jit(solution)/shard_map/dot_general | solution.py:41
  454.9 8.7 %multiply_convert_fusion.3 = bf16[2048,1024]{0,1:T(8,128)(2,1)} fusion(f32[2048,1024]{0,1:T(8,128)S(1)} %bitcast.144, f32[2048]{0:T(1024)S(1)} %copy-done.73, f32[1024]{0:T(1024)S(1)} %copy-done.86, bf16[2048,1024]{1,0:T(8,128)(2,1)} %get-tuple-element.77, bf16[256,1024]{1,0:T(8,128)(2,1)S(1)} %copy-done.48, bf16[256,1024]{1,0:T(8,128)(2,1)S(1)} %copy-done.46, ...), kind=kOutput, calls=%fused_computation.41 | convolution fusion | flops 4309647360 | bytes 18886656 | tf_op jit(solution)/shard_map/dot_general | solution.py:31
  463.7 6.9 copy.90
  489.4 13.0 %fusion.17 = (f32[1024]{0:T(1024)S(1)}, f32[2048]{0:T(1024)S(1)}, f32[2048]{0:T(1024)S(1)}, f32[1024]{0:T(1024)S(1)}, f32[2048,1024]{0,1:T(8,128)}) fusion(bf16[2048,1024]{0,1:T(8,128)(2,1)S(1)} %copy-done.5, f32[2048]{0:T(1024)S(1)} %copy-done.71, f32[2048]{0:T(1024)S(1)} %copy-done.68, f32[1024]{0:T(1024)S(1)} %copy-done.81, ...), kind=kOutput, calls=%fused_computation.24 | convolution fusion | flops 4326418432 | bytes 35696640 | tf_op jit(solution)/shard_map/dot_general | solution.py:41
  502.7 11.5 %fusion.16 = f32[2048,1024]{0,1:T(8,128)} fusion(f32[2048,1024]{0,1:T(8,128)} %copy-done.6, bf16[2048,1024]{0,1:T(8,128)(2,1)} %copy.72, f32[2048,1024]{0,1:T(8,128)} %get-tuple-element.183, f32[2048]{0:T(1024)S(1)} %broadcast_multiply_fusion, f32[2048]{0:T(1024)S(1)} %broadcast_multiply_fusion.1, f32[1024]{0:T(1024)S(1)} %copy-done.81, ...), kind=kLoop, calls=%fused_computation.23 | loop fusion | flops 18874368 | bytes 29396992 | tf_op jit(solution)/shard_map/add | solution.py:243
  531.8 9.4 %copy.91 = f32[2048,1024]{1,0:T(8,128)} copy(f32[2048,1024]{0,1:T(8,128)} %fusion.16) | data formatting | bytes 16777216
  553.2 9.5 %collective-permute-done.54 = bf16[512,512]{1,0:T(8,128)(2,1)S(1)} collective-permute-done((bf16[512,512]{1,0:T(8,128)(2,1)S(1)}, bf16[512,512]{1,0:T(8,128)(2,1)S(1)}, u32[]{:S(2)}, u32[]{:S(2)}) %collective-permute-start.54) | collective-permute-done | bytes 524320 | tf_op jit(solution)/shard_map/ppermute | solution.py:81
  565.6 8.4 %collective-permute-done.64 = bf16[256,1024]{1,0:T(8,128)(2,1)S(1)} collective-permute-done((bf16[256,1024]{1,0:T(8,128)(2,1)S(1)}, bf16[256,1024]{1,0:T(8,128)(2,1)S(1)}, u32[]{:S(2)}, u32[]{:S(2)}) %collective-permute-start.64) | collective-permute-done | bytes 524320 | tf_op jit(solution)/shard_map/ppermute | solution.py:81
  577.0 8.3 %collective-permute-done.44 = bf16[256,1024]{1,0:T(8,128)(2,1)S(1)} collective-permute-done((bf16[256,1024]{1,0:T(8,128)(2,1)S(1)}, bf16[256,1024]{1,0:T(8,128)(2,1)S(1)}, u32[]{:S(2)}, u32[]{:S(2)}) %collective-permute-start.44) | collective-permute-done | bytes 524320 | tf_op jit(solution)/shard_map/ppermute | solution.py:81
  587.6 8.8 %collective-permute-done.34 = bf16[512,512]{1,0:T(8,128)(2,1)S(1)} collective-permute-done((bf16[512,512]{1,0:T(8,128)(2,1)S(1)}, bf16[512,512]{1,0:T(8,128)(2,1)S(1)}, u32[]{:S(2)}, u32[]{:S(2)}) %collective-permute-start.34) | collective-permute-done | bytes 524320 | tf_op jit(solution)/shard_map/ppermute | solution.py:81
  598.9 8.9 %collective-permute-done.24 = bf16[512,512]{1,0:T(8,128)(2,1)S(1)} collective-permute-done((bf16[512,512]{1,0:T(8,128)(2,1)S(1)}, bf16[512,512]{1,0:T(8,128)(2,1)S(1)}, u32[]{:S(2)}, u32[]{:S(2)}) %collective-permute-start.24) | collective-permute-done | bytes 524320 | tf_op jit(solution)/shard_map/ppermute | solution.py:81
  610.0 7.9 %collective-permute-done.14 = bf16[512,512]{1,0:T(8,128)(2,1)S(1)} collective-permute-done((bf16[512,512]{1,0:T(8,128)(2,1)S(1)}, bf16[512,512]{1,0:T(8,128)(2,1)S(1)}, u32[]{:S(2)}, u32[]{:S(2)}) %collective-permute-start.14) | collective-permute-done | bytes 524320 | tf_op jit(solution)/shard_map/ppermute | solution.py:81
  (512 shorter events, 279.1 us)
Async XLA Ops:
  2.5 82.3 %collective-permute-start.10 = (bf16[256,1024]{1,0:T(8,128)(2,1)}, bf16[256,1024]{1,0:T(8,128)(2,1)}, u32[]{:S(2)}, u32[]{:S(2)}) collective-permute-start(bf16[256,1024]{1,0:T(8,128)(2,1)} %constant_dynamic-slice_fusion.32), channel_id=1, source_target_pairs={{0,1},{1,0},{2,3},{3,2},{4,5},{5,4},{6,7},{7,6},{8,9},{9,8},{10,11... | collective-permute-start | bytes 1572872 | tf_op jit(solution)/shard_map/ppermute | solution.py:81
  7.4 80.5 %collective-permute-start.8 = (bf16[512,512]{1,0:T(8,128)(2,1)}, bf16[512,512]{1,0:T(8,128)(2,1)S(1)}, u32[]{:S(2)}, u32[]{:S(2)}) collective-permute-start(bf16[512,512]{1,0:T(8,128)(2,1)} %constant_dynamic-slice_fusion.33), channel_id=1, source_target_pairs={{0,1},{1,0},{2,3},{3,2},{4,5},{5,4},{6,7},{7,6},{8,9},{9,8},{10,11... | collective-permute-start | bytes 1572872 | tf_op jit(solution)/shard_map/ppermute | solution.py:81
  8.5 80.0 %collective-permute-start.6 = (bf16[256,1024]{1,0:T(8,128)(2,1)S(1)}, bf16[256,1024]{1,0:T(8,128)(2,1)S(1)}, u32[]{:S(2)}, u32[]{:S(2)}) collective-permute-start(bf16[256,1024]{1,0:T(8,128)(2,1)S(1)} %constant_dynamic-slice_fusion.34), channel_id=1, source_target_pairs={{0,1},{1,0},{2,3},{3,2},{4,5},{5,4},{6,7},{7,6},{8,9},{9,8},{10,11... | collective-permute-start | bytes 1572872 | tf_op jit(solution)/shard_map/ppermute | solution.py:81
  12.5 74.2 %collective-permute-start.4 = (bf16[512,512]{1,0:T(8,128)(2,1)}, bf16[512,512]{1,0:T(8,128)(2,1)S(1)}, u32[]{:S(2)}, u32[]{:S(2)}) collective-permute-start(bf16[512,512]{1,0:T(8,128)(2,1)} %constant_dynamic-slice_fusion.35), channel_id=1, source_target_pairs={{0,1},{1,0},{2,3},{3,2},{4,5},{5,4},{6,7},{7,6},{8,9},{9,8},{10,11... | collective-permute-start | bytes 1572872 | tf_op jit(solution)/shard_map/ppermute | solution.py:81
  14.3 74.2 %collective-permute-start.2 = (bf16[512,512]{1,0:T(8,128)(2,1)}, bf16[512,512]{1,0:T(8,128)(2,1)S(1)}, u32[]{:S(2)}, u32[]{:S(2)}) collective-permute-start(bf16[512,512]{1,0:T(8,128)(2,1)} %constant_dynamic-slice_fusion.36), channel_id=1, source_target_pairs={{0,1},{1,0},{2,3},{3,2},{4,5},{5,4},{6,7},{7,6},{8,9},{9,8},{10,11... | collective-permute-start | bytes 1572872 | tf_op jit(solution)/shard_map/ppermute | solution.py:81
  87.9 149.3 %collective-permute-start.11 = (bf16[256,1024]{1,0:T(8,128)(2,1)}, bf16[256,1024]{1,0:T(8,128)(2,1)}, u32[]{:S(2)}, u32[]{:S(2)}) collective-permute-start(bf16[256,1024]{1,0:T(8,128)(2,1)} %collective-permute-done.10), channel_id=1, source_target_pairs={{0,2},{2,0},{4,6},{6,4},{8,10},{10,8},{12,14},{14,12},{16,18},{18,... | collective-permute-start | bytes 1572872 | tf_op jit(solution)/shard_map/ppermute | solution.py:78
  88.5 119.7 %collective-permute-start.9 = (bf16[512,512]{1,0:T(8,128)(2,1)S(1)}, bf16[512,512]{1,0:T(8,128)(2,1)S(1)}, u32[]{:S(2)}, u32[]{:S(2)}) collective-permute-start(bf16[512,512]{1,0:T(8,128)(2,1)S(1)} %collective-permute-done.8), channel_id=1, source_target_pairs={{0,2},{2,0},{4,6},{6,4},{8,10},{10,8},{12,14},{14,12},{16,18},{18,... | collective-permute-start | bytes 1572872 | tf_op jit(solution)/shard_map/ppermute | solution.py:78
  88.6 109.0 %collective-permute-start.7 = (bf16[256,1024]{1,0:T(8,128)(2,1)S(1)}, bf16[256,1024]{1,0:T(8,128)(2,1)}, u32[]{:S(2)}, u32[]{:S(2)}) collective-permute-start(bf16[256,1024]{1,0:T(8,128)(2,1)S(1)} %collective-permute-done.6), channel_id=1, source_target_pairs={{0,2},{2,0},{4,6},{6,4},{8,10},{10,8},{12,14},{14,12},{16,18},{18,... | collective-permute-start | bytes 1572872 | tf_op jit(solution)/shard_map/ppermute | solution.py:78
  98.1 20.8 %collective-permute-start.3 = (bf16[512,512]{1,0:T(8,128)(2,1)S(1)}, bf16[512,512]{1,0:T(8,128)(2,1)S(1)}, u32[]{:S(2)}, u32[]{:S(2)}) collective-permute-start(bf16[512,512]{1,0:T(8,128)(2,1)S(1)} %collective-permute-done.2), channel_id=1, source_target_pairs={{0,2},{2,0},{4,6},{6,4},{8,10},{10,8},{12,14},{14,12},{16,18},{18,... | collective-permute-start | bytes 1572872 | tf_op jit(solution)/shard_map/ppermute | solution.py:78
  448.6 94.1 %collective-permute-start.53 = (bf16[512,512]{1,0:T(8,128)(2,1)}, bf16[512,512]{1,0:T(8,128)(2,1)}, u32[]{:S(2)}, u32[]{:S(2)}) collective-permute-start(bf16[512,512]{1,0:T(8,128)(2,1)} %constant_dynamic-slice_fusion.10), channel_id=1, source_target_pairs={{0,2},{2,0},{4,6},{6,4},{8,10},{10,8},{12,14},{14,12},{16,18},{18,... | collective-permute-start | bytes 1572872 | tf_op jit(solution)/shard_map/ppermute | solution.py:78
  448.6 104.1 %collective-permute-start.52 = (bf16[512,512]{1,0:T(8,128)(2,1)}, bf16[512,512]{1,0:T(8,128)(2,1)}, u32[]{:S(2)}, u32[]{:S(2)}) collective-permute-start(bf16[512,512]{1,0:T(8,128)(2,1)} %constant_dynamic-slice_fusion.11), channel_id=1, source_target_pairs={{0,2},{2,0},{4,6},{6,4},{8,10},{10,8},{12,14},{14,12},{16,18},{18,... | collective-permute-start | bytes 1572872 | tf_op jit(solution)/shard_map/ppermute | solution.py:78
  474.2 70.4 %collective-permute-start.63 = (bf16[256,1024]{1,0:T(8,128)(2,1)}, bf16[256,1024]{1,0:T(8,128)(2,1)}, u32[]{:S(2)}, u32[]{:S(2)}) collective-permute-start(bf16[256,1024]{1,0:T(8,128)(2,1)} %constant_dynamic-slice_fusion.5), channel_id=1, source_target_pairs={{0,2},{2,0},{4,6},{6,4},{8,10},{10,8},{12,14},{14,12},{16,18},{18,... | collective-permute-start | bytes 1572872 | tf_op jit(solution)/shard_map/ppermute | solution.py:78
  474.2 91.4 %collective-permute-start.62 = (bf16[256,1024]{1,0:T(8,128)(2,1)}, bf16[256,1024]{1,0:T(8,128)(2,1)}, u32[]{:S(2)}, u32[]{:S(2)}) collective-permute-start(bf16[256,1024]{1,0:T(8,128)(2,1)} %constant_dynamic-slice_fusion.6), channel_id=1, source_target_pairs={{0,2},{2,0},{4,6},{6,4},{8,10},{10,8},{12,14},{14,12},{16,18},{18,... | collective-permute-start | bytes 1572872 | tf_op jit(solution)/shard_map/ppermute | solution.py:78
  550.7 23.3 %collective-permute-start.64 = (bf16[256,1024]{1,0:T(8,128)(2,1)S(1)}, bf16[256,1024]{1,0:T(8,128)(2,1)S(1)}, u32[]{:S(2)}, u32[]{:S(2)}) collective-permute-start(bf16[256,1024]{1,0:T(8,128)(2,1)S(1)} %add_convert_fusion.5), channel_id=1, source_target_pairs={{0,1},{1,0},{2,3},{3,2},{4,5},{5,4},{6,7},{7,6},{8,9},{9,8},{10,11... | collective-permute-start | bytes 1572872 | tf_op jit(solution)/shard_map/ppermute | solution.py:81
  552.4 24.4 %collective-permute-start.42 = (bf16[256,1024]{1,0:T(8,128)(2,1)}, bf16[256,1024]{1,0:T(8,128)(2,1)S(1)}, u32[]{:S(2)}, u32[]{:S(2)}) collective-permute-start(bf16[256,1024]{1,0:T(8,128)(2,1)} %constant_dynamic-slice_fusion.16), channel_id=1, source_target_pairs={{0,2},{2,0},{4,6},{6,4},{8,10},{10,8},{12,14},{14,12},{16,18},{18,... | collective-permute-start | bytes 1572872 | tf_op jit(solution)/shard_map/ppermute | solution.py:78
  552.7 34.4 %collective-permute-start.32 = (bf16[512,512]{1,0:T(8,128)(2,1)S(1)}, bf16[512,512]{1,0:T(8,128)(2,1)S(1)}, u32[]{:S(2)}, u32[]{:S(2)}) collective-permute-start(bf16[512,512]{1,0:T(8,128)(2,1)S(1)} %copy-done.53), channel_id=1, source_target_pairs={{0,2},{2,0},{4,6},{6,4},{8,10},{10,8},{12,14},{14,12},{16,18},{18,... | collective-permute-start | bytes 1572872 | tf_op jit(solution)/shard_map/ppermute | solution.py:78
  562.8 22.5 %collective-permute-start.44 = (bf16[256,1024]{1,0:T(8,128)(2,1)S(1)}, bf16[256,1024]{1,0:T(8,128)(2,1)S(1)}, u32[]{:S(2)}, u32[]{:S(2)}) collective-permute-start(bf16[256,1024]{1,0:T(8,128)(2,1)S(1)} %add_convert_fusion.11), channel_id=1, source_target_pairs={{0,1},{1,0},{2,3},{3,2},{4,5},{5,4},{6,7},{7,6},{8,9},{9,8},{10,11... | collective-permute-start | bytes 1572872 | tf_op jit(solution)/shard_map/ppermute | solution.py:81
  565.6 32.7 %collective-permute-start.22 = (bf16[512,512]{1,0:T(8,128)(2,1)S(1)}, bf16[512,512]{1,0:T(8,128)(2,1)S(1)}, u32[]{:S(2)}, u32[]{:S(2)}) collective-permute-start(bf16[512,512]{1,0:T(8,128)(2,1)S(1)} %copy-done.54), channel_id=1, source_target_pairs={{0,2},{2,0},{4,6},{6,4},{8,10},{10,8},{12,14},{14,12},{16,18},{18,... | collective-permute-start | bytes 1572872 | tf_op jit(solution)/shard_map/ppermute | solution.py:78
  574.0 22.5 %collective-permute-start.34 = (bf16[512,512]{1,0:T(8,128)(2,1)S(1)}, bf16[512,512]{1,0:T(8,128)(2,1)S(1)}, u32[]{:S(2)}, u32[]{:S(2)}) collective-permute-start(bf16[512,512]{1,0:T(8,128)(2,1)S(1)} %add_convert_fusion.14), channel_id=1, source_target_pairs={{0,1},{1,0},{2,3},{3,2},{4,5},{5,4},{6,7},{7,6},{8,9},{9,8},{10,11... | collective-permute-start | bytes 1572872 | tf_op jit(solution)/shard_map/ppermute | solution.py:81
  576.9 32.5 %collective-permute-start.12 = (bf16[512,512]{1,0:T(8,128)(2,1)S(1)}, bf16[512,512]{1,0:T(8,128)(2,1)S(1)}, u32[]{:S(2)}, u32[]{:S(2)}) collective-permute-start(bf16[512,512]{1,0:T(8,128)(2,1)S(1)} %copy-done.55), channel_id=1, source_target_pairs={{0,2},{2,0},{4,6},{6,4},{8,10},{10,8},{12,14},{14,12},{16,18},{18,... | collective-permute-start | bytes 1572872 | tf_op jit(solution)/shard_map/ppermute | solution.py:78
  585.2 22.5 %collective-permute-start.24 = (bf16[512,512]{1,0:T(8,128)(2,1)S(1)}, bf16[512,512]{1,0:T(8,128)(2,1)S(1)}, u32[]{:S(2)}, u32[]{:S(2)}) collective-permute-start(bf16[512,512]{1,0:T(8,128)(2,1)S(1)} %add_convert_fusion.17), channel_id=1, source_target_pairs={{0,1},{1,0},{2,3},{3,2},{4,5},{5,4},{6,7},{7,6},{8,9},{9,8},{10,11... | collective-permute-start | bytes 1572872 | tf_op jit(solution)/shard_map/ppermute | solution.py:81
  587.1 30.9 %collective-permute-start.14 = (bf16[512,512]{1,0:T(8,128)(2,1)S(1)}, bf16[512,512]{1,0:T(8,128)(2,1)S(1)}, u32[]{:S(2)}, u32[]{:S(2)}) collective-permute-start(bf16[512,512]{1,0:T(8,128)(2,1)S(1)} %add_convert_fusion.20), channel_id=1, source_target_pairs={{0,1},{1,0},{2,3},{3,2},{4,5},{5,4},{6,7},{7,6},{8,9},{9,8},{10,11... | collective-permute-start | bytes 1572872 | tf_op jit(solution)/shard_map/ppermute | solution.py:81
  596.5 23.3 %collective-permute-start.55 = (bf16[256,512]{1,0:T(8,128)(2,1)S(1)}, bf16[256,512]{1,0:T(8,128)(2,1)S(1)}, u32[]{:S(2)}, u32[]{:S(2)}) collective-permute-start(bf16[256,512]{1,0:T(8,128)(2,1)S(1)} %constant_dynamic-slice_fusion.9), channel_id=1, source_target_pairs={{0,4},{2,6},{4,0},{6,2},{8,12},{10,14},{12,8},{14,10},{16,20},{18,... | collective-permute-start | bytes 786440 | tf_op jit(solution)/shard_map/ppermute | solution.py:78
  598.2 22.2 %collective-permute-start.65 = (bf16[128,1024]{1,0:T(8,128)(2,1)S(1)}, bf16[128,1024]{1,0:T(8,128)(2,1)S(1)}, u32[]{:S(2)}, u32[]{:S(2)}) collective-permute-start(bf16[128,1024]{1,0:T(8,128)(2,1)S(1)} %constant_dynamic-slice_fusion.4), channel_id=1, source_target_pairs={{0,4},{2,6},{4,0},{6,2},{8,12},{10,14},{12,8},{14,10},{16,20},{18,... | collective-permute-start | bytes 786440 | tf_op jit(solution)/shard_map/ppermute | solution.py:78
  633.7 16.9 %collective-permute-start.67 = (bf16[32,1024]{1,0:T(8,128)(2,1)S(1)}, bf16[32,1024]{1,0:T(8,128)(2,1)S(1)}, u32[]{:S(2)}, u32[]{:S(2)}) collective-permute-start(bf16[32,1024]{1,0:T(8,128)(2,1)S(1)} %constant_dynamic-slice_fusion.2), channel_id=1, source_target_pairs={{0,16},{2,18},{4,20},{6,22},{8,24},{10,26},{12,28},{14,30},{16,0},... | collective-permute-start | bytes 196616 | tf_op jit(solution)/shard_map/ppermute | solution.py:78
  636.5 15.5 %collective-permute-start.47 = (bf16[32,1024]{1,0:T(8,128)(2,1)S(1)}, bf16[32,1024]{1,0:T(8,128)(2,1)S(1)}, u32[]{:S(2)}, u32[]{:S(2)}) collective-permute-start(bf16[32,1024]{1,0:T(8,128)(2,1)S(1)} %constant_dynamic-slice_fusion.12), channel_id=1, source_target_pairs={{0,16},{2,18},{4,20},{6,22},{8,24},{10,26},{12,28},{14,30},{16,0},... | collective-permute-start | bytes 196616 | tf_op jit(solution)/shard_map/ppermute | solution.py:78
  641.4 16.9 %collective-permute-start.27 = (bf16[64,512]{1,0:T(8,128)(2,1)S(1)}, bf16[64,512]{1,0:T(8,128)(2,1)S(1)}, u32[]{:S(2)}, u32[]{:S(2)}) collective-permute-start(bf16[64,512]{1,0:T(8,128)(2,1)S(1)} %constant_dynamic-slice_fusion.22), channel_id=1, source_target_pairs={{0,16},{2,18},{4,20},{6,22},{8,24},{10,26},{12,28},{14,30},{16,0},... | collective-permute-start | bytes 196616 | tf_op jit(solution)/shard_map/ppermute | solution.py:78
  683.0 17.6 %collective-permute-start.40 = (bf16[256,512]{1,0:T(8,128)(2,1)S(1)}, bf16[256,512]{1,0:T(8,128)(2,1)S(1)}, u32[]{:S(2)}, u32[]{:S(2)}) collective-permute-start(bf16[256,512]{1,0:T(8,128)(2,1)S(1)} %pad_maximum_fusion.14), channel_id=1, source_target_pairs={{0,4},{2,6},{4,0},{6,2},{8,12},{10,14},{12,8},{14,10},{16,20},{18,... | collective-permute-start | bytes 786440 | tf_op jit(solution)/shard_map/ppermute | solution.py:78
  684.7 21.2 %collective-permute-start.30 = (bf16[256,512]{1,0:T(8,128)(2,1)S(1)}, bf16[256,512]{1,0:T(8,128)(2,1)S(1)}, u32[]{:S(2)}, u32[]{:S(2)}) collective-permute-start(bf16[256,512]{1,0:T(8,128)(2,1)S(1)} %pad_maximum_fusion.13), channel_id=1, source_target_pairs={{0,4},{2,6},{4,0},{6,2},{8,12},{10,14},{12,8},{14,10},{16,20},{18,... | collective-permute-start | bytes 786440 | tf_op jit(solution)/shard_map/ppermute | solution.py:78
  686.3 22.4 %collective-permute-start.20 = (bf16[256,512]{1,0:T(8,128)(2,1)S(1)}, bf16[256,512]{1,0:T(8,128)(2,1)S(1)}, u32[]{:S(2)}, u32[]{:S(2)}) collective-permute-start(bf16[256,512]{1,0:T(8,128)(2,1)S(1)} %pad_maximum_fusion.12), channel_id=1, source_target_pairs={{0,4},{2,6},{4,0},{6,2},{8,12},{10,14},{12,8},{14,10},{16,20},{18,... | collective-permute-start | bytes 786440 | tf_op jit(solution)/shard_map/ppermute | solution.py:78
  689.4 19.5 %collective-permute-start.61 = (bf16[512,512]{1,0:T(8,128)(2,1)S(1)}, bf16[512,512]{1,0:T(8,128)(2,1)S(1)}, u32[]{:S(2)}, u32[]{:S(2)}) collective-permute-start(bf16[512,512]{1,0:T(8,128)(2,1)S(1)} %pad_maximum_fusion.10), channel_id=1, source_target_pairs={{0,2},{2,0},{4,6},{6,4},{8,10},{10,8},{12,14},{14,12},{16,18},{18,... | collective-permute-start | bytes 1572872 | tf_op jit(solution)/shard_map/ppermute | solution.py:78
  695.0 16.2 %collective-permute-start.71 = (bf16[256,1024]{1,0:T(8,128)(2,1)S(1)}, bf16[256,1024]{1,0:T(8,128)(2,1)S(1)}, u32[]{:S(2)}, u32[]{:S(2)}) collective-permute-start(bf16[256,1024]{1,0:T(8,128)(2,1)S(1)} %pad_maximum_fusion.11), channel_id=1, source_target_pairs={{0,2},{2,0},{4,6},{6,4},{8,10},{10,8},{12,14},{14,12},{16,18},{18,... | collective-permute-start | bytes 1572872 | tf_op jit(solution)/shard_map/ppermute | solution.py:78
  (138 other events, 1517.6 us)

commit v2 on v1

v2 whole, which is shorter than its diff:
```python
from functools import partial
import math

import jax
import jax.numpy as jnp
from jax import lax
from jax.experimental import pallas as pl
from jax.experimental.pallas import tpu as pltpu
from jax.sharding import PartitionSpec as P

HS = 128
CROP = 512


EPSILON = 1e-05


def dot(left, right, left_dim, right_dim):
    return lax.dot_general(
        left,
        right,
        (((left_dim,), (right_dim,)), ((), ())),
        preferred_element_type=jnp.float32,
    )


def unit_rows(rows):
    center = rows - jnp.mean(rows, axis=-1, keepdims=True)
    inverse = lax.rsqrt(jnp.mean(center * center, axis=-1, keepdims=True) + EPSILON)
    return center * inverse, inverse


def unit_rows_back(scaled, unit, inverse):
    inner = scaled - jnp.mean(scaled, axis=-1, keepdims=True)
    return (inner - unit * jnp.mean(scaled * unit, axis=-1, keepdims=True)) * inverse


def low(array):
    return array.astype(jnp.bfloat16)


def attend_kernel(first, live_ref, source_ref, *refs):
    if first:
        gain_ref, shift_ref, *refs = refs
    query_weight, key_weight, value_weight, query_bias, value_bias, *refs = refs
    if first:
        normed_ref, *refs = refs
    query_ref, keys_ref, values_ref, weights_ref, attended_ref, inverse_ref = refs

    @pl.when(pl.program_id(0) < live_ref[0])
    def _():
        if first:
            unit, _ = unit_rows(source_ref[...].astype(jnp.float32))
            normed_ref[...] = low(unit * gain_ref[...] + shift_ref[...])
            normed = normed_ref[...]
        else:
            normed = source_ref[...]
        query_ref[...] = low(dot(normed, query_weight[...], 1, 0) + query_bias[...])
        keys_ref[...] = low(dot(normed, key_weight[...], 1, 0))
        values_ref[...] = low(dot(normed, value_weight[...], 1, 0) + value_bias[...])
        ones = jnp.ones((CROP, HS), jnp.bfloat16)
        for head in range(query_ref.shape[1] // HS):
            columns = pl.ds(head * HS, HS)
            scores = dot(query_ref[:, columns], keys_ref[:, columns], 1, 1)
            highest = jnp.max(scores, axis=-1, keepdims=True)
            weights = low(jnp.exp2((scores - highest) * (math.log2(math.e) / math.sqrt(HS))))
            weights_ref[head] = weights
            extended = jnp.concatenate([values_ref[:, columns], ones], axis=1)
            mixed = dot(weights, extended, 1, 0)
            inverse = 1.0 / mixed[:, HS:]
            inverse_ref[:, columns] = inverse
            attended_ref[:, columns] = low(mixed[:, :HS] * inverse)


def gelu_pair(before):
    lower = 0.5 + 0.5 * lax.erf(before * math.sqrt(0.5))
    density = jnp.exp2(before * before * (-0.5 * math.log2(math.e)))
    slope = lower + before * density * (1.0 / math.sqrt(2.0 * math.pi))
    return before * lower, slope


def feed_kernel(
    crops,
    live_ref,
    latents_ref,
    cotangent_ref,
    attended_refs,
    out_weights,
    up_weights,
    down_weights,
    up_biases,
    out_bias,
    down_bias,
    gain,
    shift,
    output_ref,
    hidden_grad_ref,
    attended_grads,
    out_grads,
    up_grads,
    down_grads,
    up_bias_grads,
    vectors_ref,
    out_sums,
    up_sums,
    down_sums,
):
    step = pl.program_id(0)

    @pl.when(step == 0)
    def _():
        for sums in (*out_sums, *up_sums, *down_sums, *up_bias_grads, vectors_ref):
            sums[...] = jnp.zeros_like(sums)

    @pl.when(step >= live_ref[0])
    def _():
        output_ref[...] = jnp.zeros_like(output_ref)
        hidden_grad_ref[...] = jnp.zeros_like(hidden_grad_ref)

    @pl.when(step < live_ref[0])
    def _():
        hidden = latents_ref[...].astype(jnp.float32) + out_bias[...]
        for part in range(2):
            hidden = hidden + dot(attended_refs[part][...], out_weights[part][...], 1, 0)
        unit, inverse = unit_rows(hidden)
        normed = low(unit * gain[...] + shift[...])
        top = cotangent_ref[...]
        result = hidden + down_bias[...]
        second_grad = jnp.zeros(hidden.shape, jnp.float32)
        for part in range(2):
            before = dot(normed, up_weights[part][...], 1, 0) + up_biases[part][...]
            value, slope = gelu_pair(before)
            activated = low(value)
            result = result + dot(activated, down_weights[part][...], 1, 0)
            down_sums[part][...] += dot(activated, top, 0, 0)
            activated_grad = dot(top, down_weights[part][...], 1, 1)
            before_grad = low(activated_grad * slope)
            up_bias_grads[part][...] += jnp.sum(
                before_grad.astype(jnp.float32), axis=0, keepdims=True
            )
            up_sums[part][...] += dot(normed, before_grad, 0, 0)
            second_grad = second_grad + dot(before_grad, up_weights[part][...], 1, 1)
        output_ref[...] = low(result)
        top_grad = top.astype(jnp.float32)
        hidden_grad = top_grad + unit_rows_back(second_grad * gain[...], unit, inverse)
        hidden_grad_ref[...] = hidden_grad
        hidden_low = low(hidden_grad)
        for part in range(2):
            out_sums[part][...] += dot(attended_refs[part][...], hidden_low, 0, 0)
            attended_grads[part][...] = low(dot(hidden_low, out_weights[part][...], 1, 1))
        for row, term in enumerate((second_grad * unit, second_grad, hidden_grad, top_grad)):
            vectors_ref[row : row + 1] += jnp.sum(term, axis=0, keepdims=True)

    @pl.when(step == crops - 1)
    def _():
        for part in range(2):
            out_grads[part][...] = low(out_sums[part][...])
            up_grads[part][...] = low(up_sums[part][...])
            down_grads[part][...] = low(down_sums[part][...])


def attend_back_kernel(
    crops,
    live_ref,
    normed_ref,
    queries,
    keys,
    values,
    weights,
    inverses,
    attended,
    attended_grads,
    matrices,
    query_grads,
    keys_grads,
    values_grads,
    matrix_grads,
    bias_grads,
    gain_terms,
    shift_terms,
    matrix_sums,
):
    step = pl.program_id(0)
    scale = 1.0 / math.sqrt(HS)

    @pl.when(step == 0)
    def _():
        for part in range(2):
            bias_grads[part][...] = jnp.zeros_like(bias_grads[part])
            for kind in range(3):
                matrix_sums[kind][part][...] = jnp.zeros_like(matrix_sums[kind][part])

    @pl.when(step < live_ref[0])
    def _():
        normed = normed_ref[...]
        for part in range(2):
            for head in range(queries[part].shape[1] // HS):
                columns = pl.ds(head * HS, HS)
                inner = attended_grads[part][:, columns].astype(jnp.float32)
                inner = inner * inverses[part][:, columns]
                upstream = low(inner)
                total = jnp.sum(
                    inner * attended[part][:, columns].astype(jnp.float32), axis=1, keepdims=True
                )
                head_weights = weights[part][head]
                values_grads[part][:, columns] = low(dot(head_weights, upstream, 0, 0))
                probs_grad = dot(upstream, values[part][:, columns], 1, 1)
                scores_grad = low(head_weights.astype(jnp.float32) * (probs_grad - total))
                query_grads[part][:, columns] = low(
                    dot(scores_grad, keys[part][:, columns], 1, 0) * scale
                )
                keys_grads[part][:, columns] = low(
                    dot(scores_grad, queries[part][:, columns], 0, 0) * scale
                )
            for kind, grads in enumerate((query_grads, keys_grads, values_grads)):
                grad = grads[part][...]
                matrix_sums[kind][part][...] += dot(normed, grad, 0, 0)
                bias_grads[part][kind : kind + 1] += jnp.sum(
                    grad.astype(jnp.float32), axis=0, keepdims=True
                )

    @pl.when(step == crops - 1)
    def _():
        gain_terms[...] = jnp.zeros_like(gain_terms)
        shift_terms[...] = jnp.zeros_like(shift_terms)
        for part in range(2):
            for kind in range(3):
                matrix = matrices[kind][part]
                sums = matrix_sums[kind][part]
                matrix_grads[kind][part][...] = low(sums[...])
                for start in range(0, matrix.shape[1], HS):
                    columns = pl.ds(start, HS)
                    gain_terms[...] += sums[:, columns] * matrix[:, columns].astype(jnp.float32)
                bias = bias_grads[part][kind : kind + 1]
                rough = low(bias)
                fine = low(bias - rough.astype(jnp.float32))
                shift_terms[...] += dot(
                    jnp.concatenate([rough, fine] + [jnp.zeros_like(rough)] * 6, axis=0),
                    matrix[...],
                    1,
                    1,
                )


def latents_kernel(
    live_ref, latents_ref, hidden_grad_ref, grads, matrices, gain_ref, output_ref
):
    @pl.when(pl.program_id(0) >= live_ref[0])
    def _():
        output_ref[...] = jnp.zeros_like(output_ref)

    @pl.when(pl.program_id(0) < live_ref[0])
    def _():
        unit, inverse = unit_rows(latents_ref[...].astype(jnp.float32))
        upstream = jnp.zeros(output_ref.shape, jnp.float32)
        for kind in range(3):
            for grad, matrix in zip(grads[kind], matrices[kind]):
                upstream = upstream + dot(grad[...], matrix[...], 1, 1)
        output_ref[...] = hidden_grad_ref[...] + unit_rows_back(
            upstream * gain_ref[...], unit, inverse
        )


VMEM_LIMIT = 66_000_000


def row_block(width, column=0):
    return pl.BlockSpec((CROP, width), lambda i, live: (i, column))


def fixed(rows, width, column=0):
    return pl.BlockSpec((rows, width), lambda i, live: (0, column), pipeline_mode=pl.Buffered(1))


def shaped(shape, dtype=jnp.bfloat16):
    return jax.ShapeDtypeStruct(shape, dtype)


def run(kernel, name, crops, in_specs, out_specs, out_shape, flops, moved, scratch=()):
    return pl.pallas_call(
        kernel,
        name=name,
        out_shape=out_shape,
        grid_spec=pltpu.PrefetchScalarGridSpec(
            num_scalar_prefetch=1,
            grid=(crops,),
            in_specs=in_specs,
            out_specs=out_specs,
            scratch_shapes=scratch,
        ),
        compiler_params=pltpu.CompilerParams(
            dimension_semantics=("arbitrary",), vmem_limit_bytes=VMEM_LIMIT
        ),
        cost_estimate=pl.CostEstimate(flops=flops, bytes_accessed=moved, transcendentals=0),
    )


def attend(live, source, norm, matrices, biases):
    count, width = source.shape
    crops = count // CROP
    units = matrices[0].shape[1]
    heads = units // HS
    first = norm is not None
    vector = fixed(1, units)
    outs = (row_block(width),) * first + (
        row_block(units),
        row_block(units),
        row_block(units),
        pl.BlockSpec((None, heads, CROP, CROP), lambda i, live: (i, 0, 0, 0)),
        row_block(units),
        row_block(units),
    )
    rows = shaped((count, units))
    shapes = (shaped((count, width)),) * first + (
        rows,
        rows,
        rows,
        shaped((crops, heads, CROP, CROP)),
        rows,
        shaped((count, units), jnp.float32),
    )
    return run(
        partial(attend_kernel, first),
        "attend_first" if first else "attend_rest",
        crops,
        (row_block(width),)
        + (fixed(1, width),) * (2 * first)
        + (fixed(width, units),) * 3
        + (vector,) * 2,
        outs,
        shapes,
        2 * count * units * (3 * width + 2 * CROP),
        count * (units * (12 + 2 * CROP // HS) + 4 * width),
    )(live, source, *(norm or ()), *matrices, *biases)


def feed(live, latents, cotangent, attended, outs, ups, downs, up_biases, vectors):
    count, width = latents.shape
    crops = count // CROP
    units = [array.shape[1] for array in attended]
    both = lambda make: tuple(make(size) for size in units)
    row_in = both(row_block)
    tall = both(lambda size: fixed(size, width))
    flat = both(lambda size: fixed(width, size))
    thin = both(lambda size: fixed(1, size))
    vector = fixed(1, width)
    sums = lambda dtype: (
        both(lambda size: dtype((size, width))),
        both(lambda size: dtype((width, size))),
        both(lambda size: dtype((size, width))),
    )
    return run(
        partial(feed_kernel, crops),
        "feed",
        crops,
        (row_block(width), row_block(width), row_in, tall, flat, tall, thin)
        + (vector,) * 4,
        (row_block(width), row_block(width), row_in, tall, flat, tall, thin, fixed(8, width)),
        (
            shaped((count, width)),
            shaped((count, width), jnp.float32),
            both(lambda size: shaped((count, size))),
            *sums(shaped),
            both(lambda size: shaped((1, size), jnp.float32)),
            shaped((8, width), jnp.float32),
        ),
        2 * count * width * width * 9,
        count * width * 14,
        sums(lambda shape: pltpu.VMEM(shape, jnp.float32)),
    )(live, latents, cotangent, attended, outs, ups, downs, up_biases, *vectors)


def attend_back(live, normed, saved, attended_grads, matrices, widths, phase):
    count, width = normed.shape
    crops = count // CROP
    both = lambda make: tuple(make(size) for size in widths)
    rows = both(lambda size: row_block(size, phase))
    heads = both(
        lambda size: pl.BlockSpec(
            (None, size // HS, CROP, CROP), lambda i, live: (i, phase, 0, 0)
        )
    )
    flat = both(lambda size: fixed(width, size, phase))
    plain = both(lambda size: fixed(width, size))
    queries, keys, values, weights, attended, inverses = saved
    return run(
        partial(attend_back_kernel, crops),
        "attend_back",
        crops,
        (row_block(width), rows, rows, rows, heads, rows, rows, rows, (flat,) * 3),
        (
            both(row_block),
            both(row_block),
            both(row_block),
            (plain,) * 3,
            both(lambda size: fixed(8, size)),
            fixed(width, HS),
            fixed(8, width),
        ),
        (
            both(lambda size: shaped((count, size))),
            both(lambda size: shaped((count, size))),
            both(lambda size: shaped((count, size))),
            (both(lambda size: shaped((width, size))),) * 3,
            both(lambda size: shaped((8, size), jnp.float32)),
            shaped((width, HS), jnp.float32),
            shaped((8, width), jnp.float32),
        ),
        2 * count * sum(widths) * (3 * width + 4 * CROP),
        count * (sum(widths) * (18 + 2 * CROP // HS) + 2 * width),
        ((both(lambda size: pltpu.VMEM((width, size), jnp.float32)),) * 3,),
    )(
        live,
        normed,
        queries,
        keys,
        values,
        weights,
        inverses,
        attended,
        attended_grads,
        matrices,
    )


def latents_back(live, latents, hidden_grad, grads, matrices, gain):
    count, width = latents.shape
    rows = tuple(tuple(row_block(array.shape[1]) for array in kind) for kind in grads)
    flat = tuple(
        tuple(fixed(width, grad.shape[1], column) for grad, (_, column) in zip(*kinds))
        for kinds in zip(grads, matrices)
    )
    return run(
        latents_kernel,
        "latents_back",
        count // CROP,
        (row_block(width), row_block(width), rows, flat, fixed(1, width)),
        row_block(width),
        shaped((count, width), jnp.float32),
        2 * count * width * width * 3,
        count * width * 16,
    )(
        live,
        latents,
        hidden_grad,
        grads,
        tuple(tuple(array for array, _ in kind) for kind in matrices),
        gain,
    )


def pair_perm(size, bit):
    return [(i, i ^ bit) for i in range(size)]


class Links:
    def __init__(self):
        self.wide = lax.axis_size("wide")
        self.narrow = lax.axis_size("narrow")
        self.paired = self.narrow == 2 and self.wide == 16
        self.index = lax.axis_index("wide")
        self.core = self.index % 2

    def swap(self, array, bit):
        return lax.ppermute(array, "wide", pair_perm(self.wide, bit))

    def swap_narrow(self, array):
        return lax.ppermute(array, "narrow", [(0, 1), (1, 0)])

    def others(self, weight, axis):
        if not self.paired:
            whole = lax.all_gather(weight, "narrow", axis=0, tiled=False)
            whole = jnp.roll(whole, -lax.axis_index("narrow"), axis=0)[1:]
            return jnp.concatenate([whole[i] for i in range(self.narrow - 1)], axis=axis)
        half = weight.shape[0] // 2
        mine = lax.dynamic_slice_in_dim(weight, self.core * half, half, 0)
        near = self.swap_narrow(mine)
        far = self.swap(near, 1)
        first = jnp.where(self.core == 0, near, far)
        second = jnp.where(self.core == 0, far, near)
        return jnp.concatenate([first, second], axis=0)

    def halves(self, array, bit):
        half = array.shape[0] // 2
        position = (self.index // bit) % 2
        keep = lax.dynamic_slice_in_dim(array, position * half, half, 0)
        give = lax.dynamic_slice_in_dim(array, (1 - position) * half, half, 0)
        return keep, give

    def add(self, left, right):
        return (left.astype(jnp.float32) + right.astype(jnp.float32)).astype(jnp.bfloat16)

    def join(self, mine, other, bit):
        position = (self.index // bit) % 2
        first = jnp.where(position == 0, mine, other)
        second = jnp.where(position == 0, other, mine)
        return jnp.concatenate([first, second], axis=0)

    def reduce_matrix(self, own, other, axis):
        own = own.astype(jnp.bfloat16)
        other = other.astype(jnp.bfloat16)
        if not self.paired:
            width = own.shape[axis]
            parts = jnp.stack(
                [own]
                + [
                    lax.slice_in_dim(other, i * width, (i + 1) * width, axis=axis)
                    for i in range(self.narrow - 1)
                ]
            )
            parts = jnp.roll(parts, lax.axis_index("narrow"), axis=0)
            mine = lax.psum_scatter(parts, "narrow", scatter_dimension=0, tiled=True)[0]
            return lax.psum(mine, "wide").astype(jnp.float32)
        keep_own, give_own = self.halves(own, 1)
        keep_other, give_other = self.halves(other, 1)
        keep_other = self.add(keep_other, self.swap(give_other, 1))
        keep = self.add(keep_own, self.swap(give_own, 1))
        keep = self.add(keep, self.swap_narrow(keep_other))
        for bit in (2, 4, 8):
            keep, give = self.halves(keep, bit)
            keep = self.add(keep, self.swap(give, bit))
        for bit in (8, 4, 2, 1):
            keep = self.join(keep, self.swap(keep, bit), bit)
        return keep.astype(jnp.float32)

    def reduce_all(self, rows):
        if not self.paired:
            return lax.psum(rows, ("wide", "narrow"))
        rows = rows + self.swap(rows, 1)
        rows = rows + self.swap_narrow(rows)
        for bit in (2, 4, 8):
            rows = rows + self.swap(rows, bit)
        return rows


def on_device(
    latents,
    cotangent,
    crop_counts,
    image_device,
    query_weight,
    key_weight,
    value_weight,
    out_weight,
    up_weight,
    down_weight,
    query_bias,
    value_bias,
    up_bias,
    out_bias,
    down_bias,
    first_gain,
    first_shift,
    second_gain,
    second_shift,
):
    links = Links()
    count = latents.shape[0]
    width = latents.shape[1]
    narrow = links.narrow
    place = lax.axis_index("narrow")
    owned = jnp.sum(jnp.where(image_device == lax.axis_index("wide"), crop_counts, 0))
    live = (owned - place * (count // CROP)).astype(jnp.int32).reshape(1)
    units = query_weight.shape[1]
    biases = jnp.stack([query_bias, value_bias, up_bias])
    if links.paired:
        biases = jnp.concatenate([biases, links.swap_narrow(biases)], axis=1)
    else:
        biases = lax.all_gather(biases, "narrow", axis=0)
        biases = jnp.roll(biases, -place, axis=0).transpose(1, 0, 2).reshape(3, -1)
    biases = biases.astype(jnp.float32)
    both = lambda row: (biases[row : row + 1, :units], biases[row : row + 1, units:])
    query_biases, value_biases, up_biases = both(0), both(1), both(2)
    vector = lambda array: array.reshape(1, -1)
    queries = (query_weight, links.others(query_weight, 1))
    keys = (key_weight, links.others(key_weight, 1))
    values = (value_weight, links.others(value_weight, 1))
    outs = (out_weight, links.others(out_weight, 0))
    ups = (up_weight, links.others(up_weight, 1))
    downs = (down_weight, links.others(down_weight, 0))

    norm = (vector(first_gain), vector(first_shift))
    matrices = (queries, keys, values)
    first, *saved_own = attend(
        live,
        latents,
        norm,
        [kind[0] for kind in matrices],
        (query_biases[0], value_biases[0]),
    )
    saved_rest = attend(
        live,
        first,
        None,
        [kind[1] for kind in matrices],
        (query_biases[1], value_biases[1]),
    )
    saved = tuple(zip(saved_own, saved_rest))
    (
        block_output,
        hidden_grad,
        attended_grads,
        out_grads,
        up_grads,
        down_grads,
        up_bias_grads,
        feed_vectors,
    ) = feed(
        live,
        latents,
        cotangent,
        saved[4],
        outs,
        ups,
        downs,
        up_biases,
        [vector(array) for array in (out_bias, down_bias, second_gain, second_shift)],
    )
    phases = 2 if links.paired else 1
    widths = (units // phases, (width - units) // phases)
    steps = [
        attend_back(live, first, saved, attended_grads, matrices, widths, phase)
        for phase in range(phases)
    ]
    grads = tuple(
        tuple(array for step in steps for array in step[kind]) for kind in range(3)
    )
    parts = tuple(
        tuple((kind[part], phase) for phase in range(phases) for part in range(2))
        for kind in matrices
    )
    latents_gradient = latents_back(live, latents, hidden_grad, grads, parts, norm[0])

    gain_terms = sum(step[5] for step in steps).sum(axis=1)
    first_shift_grad = sum(step[6] for step in steps).sum(axis=0)
    first_gain_grad = (gain_terms - first_shift * first_shift_grad) / first_gain

    def shared_units(own, rest):
        if narrow == 2:
            ahead = place == 0
            return jnp.where(
                ahead, jnp.concatenate([own, rest]), jnp.concatenate([rest, own])
            )
        return jnp.roll(
            jnp.concatenate([own, rest]).reshape(narrow, units), place, axis=0
        ).reshape(-1)

    def bias_row(kind):
        return shared_units(
            jnp.concatenate([step[4][0][kind] for step in steps]),
            jnp.concatenate([step[4][1][kind] for step in steps]),
        )

    rows = jnp.stack(
        [
            first_gain_grad,
            first_shift_grad,
            *(feed_vectors[row] for row in range(4)),
            bias_row(0),
            bias_row(2),
            shared_units(up_bias_grads[0][0], up_bias_grads[1][0]),
        ]
    )
    rowwise = links.reduce_all(rows)
    own = lax.dynamic_slice_in_dim(rowwise[6:], place * units, units, 1)
    wide_grad = lambda kind: links.reduce_matrix(
        jnp.concatenate([step[3][kind][0] for step in steps], axis=1),
        jnp.concatenate([step[3][kind][1] for step in steps], axis=1),
        1,
    )
    return (
        block_output,
        latents_gradient,
        wide_grad(0),
        wide_grad(1),
        wide_grad(2),
        links.reduce_matrix(*out_grads, 0),
        links.reduce_matrix(*up_grads, 1),
        links.reduce_matrix(*down_grads, 0),
        own[0],
        own[1],
        own[2],
        rowwise[4],
        rowwise[5],
        rowwise[0],
        rowwise[1],
        rowwise[2],
        rowwise[3],
    )


def solution(mesh):
    rows = P(("wide", "narrow"), None)
    columns = P(None, "narrow")
    units = P("narrow", None)
    vector = P("narrow")
    whole = P()
    return jax.shard_map(
        on_device,
        mesh=mesh,
        in_specs=(
            rows,
            rows,
            whole,
            whole,
            columns,
            columns,
            columns,
            units,
            columns,
            units,
            vector,
            vector,
            vector,
            whole,
            whole,
            whole,
            whole,
            whole,
            whole,
        ),
        out_specs=(
            rows,
            rows,
            columns,
            columns,
            columns,
            units,
            columns,
            units,
            vector,
            vector,
            vector,
            whole,
            whole,
            whole,
            whole,
            whole,
            whole,
        ),
        check_vma=False,
    )
```

time: 725 us -> 469 us (0.65)
  matrix products: 262 us -> 0 us
  Pallas kernels: 0 us -> 177 us
  other arithmetic: 127 us -> 31.5 us
  local copies, waits for them, and re-layouts: 95.9 us -> 30.4 us
  blocking collectives: 44.4 us -> 0 us
  waiting for transfers between devices: 125 us -> 151 us
    dot_general x24 -> x0, matrix products: 262 us -> none  [the longest x6 98.5 us: batched(): lax.dot_general(left, right, (((left_dim,), (right_dim,)), ((0, 1), (0, 1...]
    pallas_call x0 -> x6, Pallas kernels: none -> 177 us  [the longest x1 57.4 us: feed(): run(partial(feed_kernel, crops), 'feed', crops, (row_block(width), row_bl...]
    all_gather x1 -> x0, blocking collectives: 44.4 us -> none  [on_device(): biases = lax.all_gather(biases, 'narrow', axis=0)]
    unnamed x194 -> x104, local copies, waits for them, and re-layouts: 45.6 us -> 1.7 us
    sub x1 -> x0, other arithmetic: 35.4 us -> none  [on_device(): probs = jax.nn.softmax(scores, axis=-1)]
    ppermute x13 -> x14, waiting for transfers between devices: 63 us -> 96.2 us  [swap_narrow(): return lax.ppermute(array, 'narrow', [(0, 1), (1, 0)])]
    convert_element_type x4 -> x1, other arithmetic: 30.9 us -> 0.6 us  [on_device(): biases = biases.astype(jnp.float32)]
    reduce_sum x5 -> x2, other arithmetic: 22.5 us -> 0.23 us  [the longest x1 0.21 us: on_device(): gain_terms = sum((step[5] for step in steps)).sum(axis=1)]
  transfers between devices with their start and end apart: 77 -> 78, of which waited for: 35 -> 36; matrix products, arithmetic and copies ran while one was open for 37% -> 10% of each run, Pallas kernels for 0% -> 10%
where the time goes in v2:
time: 469 us; the launch traced here: 461 us
  Pallas kernels  177 us (38%)
  waiting for transfers between devices  151 us (32%)
  starting transfers between devices  67.7 us (14%)
  other arithmetic  31.5 us (7%)
  local copies, waits for them, and re-layouts  30.4 us (6%)
    ppermute x14, waiting for transfers between devices, swap_narrow(): return lax.ppermute(array, 'narrow', [(0, 1), (1, 0)])  96.2 us
    pallas_call x1, Pallas kernels, feed(): run(partial(feed_kernel, crops), 'feed', crops, (row_block(width), row_bl...  57.4 us
    pallas_call x2, Pallas kernels, attend_back(): run(partial(attend_back_kernel, crops), 'attend_back', crops, (row_block(...  57.1 us
    ppermute x64, starting transfers between devices, swap(): return lax.ppermute(array, 'wide', pair_perm(self.wide, bit))  55.4 us
    ppermute x64, waiting for transfers between devices, swap(): return lax.ppermute(array, 'wide', pair_perm(self.wide, bit))  55.1 us
    pallas_call x2, Pallas kernels, attend(): run(partial(attend_kernel, first), 'attend_first' if first else 'attend_r...  38.6 us
    pallas_call x1, Pallas kernels, latents_back(): run(latents_kernel, 'latents_back', count // CROP, (row_block(width), row...  23.5 us
    dynamic_slice x30, local copies, waits for them, and re-layouts, halves(): give = lax.dynamic_slice_in_dim(array, (1 - position) * half, half, 0)  12.3 us
  transfers between devices with their start and end apart: 78, of which 36 were waited for; matrix products, arithmetic and copies ran while one was open for 10% of the time, Pallas kernels for 10%

profile of v2, /device:TPU:0, one launch (start us, length us, event | category | flops | bytes accessed | tf_op | source)
XLA Modules:
  0.0 460.7 jit_solution(9177056271952531588)
XLA Ops:
  2.9 3.1 collective-permute-start
  22.1 11.2 %collective-permute-done.3 = bf16[512,512]{1,0:T(8,128)(2,1)} collective-permute-done((bf16[512,512]{1,0:T(8,128)(2,1)S(1)}, bf16[512,512]{1,0:T(8,128)(2,1)}, u32[]{:S(2)}, u32[]{:S(2)}) %collective-permute-start.3) | collective-permute-done | bytes 524320 | tf_op jit(solution)/shard_map/ppermute | solution.py:468
  33.3 20.5 %attend_first.1 = (bf16[2048,1024]{1,0:T(8,128)(2,1)}, bf16[2048,512]{1,0:T(8,128)(2,1)}, bf16[2048,512]{1,0:T(8,128)(2,1)}, bf16[2048,512]{1,0:T(8,128)(2,1)}, ...) custom-call(s32[1]{0:T(128)} %bitcast.live_ref, bf16[2048,1024]{1,0:T(8,128)(2,1)} %latents_ref.3, ...), custom_call_target="tpu_custom_call" | custom-call | flops 8589934592 | bytes 29360128 | tf_op jit(solution)/shard_map/attend_first/pallas_call | solution.py:322
  55.6 11.3 %collective-permute-done.9 = bf16[512,512]{1,0:T(8,128)(2,1)} collective-permute-done((bf16[512,512]{1,0:T(8,128)(2,1)}, bf16[512,512]{1,0:T(8,128)(2,1)}, u32[]{:S(2)}, u32[]{:S(2)}) %collective-permute-start.9) | collective-permute-done | bytes 524320 | tf_op jit(solution)/shard_map/ppermute | solution.py:468
  67.0 9.8 %collective-permute-done.7 = bf16[256,1024]{1,0:T(8,128)(2,1)} collective-permute-done((bf16[256,1024]{1,0:T(8,128)(2,1)}, bf16[256,1024]{1,0:T(8,128)(2,1)}, u32[]{:S(2)}, u32[]{:S(2)}) %collective-permute-start.7) | collective-permute-done | bytes 524320 | tf_op jit(solution)/shard_map/ppermute | solution.py:468
  88.2 18.1 %attend_rest.1 = (bf16[2048,512]{1,0:T(8,128)(2,1)}, bf16[2048,512]{1,0:T(8,128)(2,1)}, bf16[2048,512]{1,0:T(8,128)(2,1)}, bf16[4,4,512,512]{3,2,1,0:T(8,128)(2,...) custom-call(s32[1]{0:T(128)} %bitcast.live_ref, bf16[2048,1024]{1,0:T(8,128)(2,1)} %get-tuple-element.76.source_ref.normed_ref, ...), custom_call_target="tpu_custom_call" | custom-call | flops 8589934592 | bytes 29360128 | tf_op jit(solution)/shard_map/attend_rest/pallas_call | solution.py:322
  106.3 57.4 %feed.1 = (bf16[2048,1024]{1,0:T(8,128)(2,1)}, f32[2048,1024]{1,0:T(8,128)}, bf16[2048,512]{1,0:T(8,128)(2,1)}, bf16[2048,512]{1,0:T(8,128)(2,1)}, bf16[512,1024...) custom-call(s32[1]{0:T(128)} %bitcast.live_ref, ...), custom_call_target="tpu_custom_call" | custom-call | flops 38654705664 | bytes 29360128 | tf_op jit(solution)/shard_map/feed/pallas_call | solution.py:352
  163.7 28.5 %attend_back.3 = (bf16[2048,256]{1,0:T(8,128)(2,1)}, bf16[2048,256]{1,0:T(8,128)(2,1)}, bf16[2048,256]{1,0:T(8,128)(2,1)}, bf16[2048,256]{1,0:T(8,128)(2,1)}, bf...) custom-call(s32[1]{0:T(128)} %bitcast.live_ref, ...), custom_call_target="tpu_custom_call" | custom-call | flops 10737418240 | bytes 31457280 | tf_op jit(solution)/shard_map/attend_back/pallas_call | solution.py:386
  192.2 28.6 %attend_back.2 = (bf16[2048,256]{1,0:T(8,128)(2,1)}, bf16[2048,256]{1,0:T(8,128)(2,1)}, bf16[2048,256]{1,0:T(8,128)(2,1)}, bf16[2048,256]{1,0:T(8,128)(2,1)}, bf...) custom-call(s32[1]{0:T(128)} %bitcast.live_ref, ...), custom_call_target="tpu_custom_call" | custom-call | flops 10737418240 | bytes 31457280 | tf_op jit(solution)/shard_map/attend_back/pallas_call | solution.py:386
  238.2 23.5 %latents_back.1 = f32[2048,1024]{1,0:T(8,128)} custom-call(s32[1]{0:T(128)} %bitcast.live_ref, bf16[2048,1024]{1,0:T(8,128)(2,1)} %latents_ref.3, f32[2048,1024]{1,0:T(8,128)} %get-tuple-element.79.hidden_grad_ref, bf16[2048,256]{1,0:T(8,128)(2,1)} %get-tuple-element.92.grads_0__0_, bf16[2048,256]{1,0:T(8,128)(2,1)} %get-tuple-element.93.grads_0__1_, ...), custom_call_target="tpu_custom_call" | custom-call | flops 12884901888 | bytes 33554432 | tf_op jit(solution)/shard_map/latents_back/pallas_call | solution.py:433
  264.9 3.4 collective-permute-done.74
  269.9 2.7 collective-permute-done.75
  274.3 2.6 collective-permute-done.76
  279.2 3.0 collective-permute-done.77
  290.8 11.5 %collective-permute-done.65 = bf16[256,1024]{1,0:T(8,128)(2,1)S(1)} collective-permute-done((bf16[256,1024]{1,0:T(8,128)(2,1)S(1)}, bf16[256,1024]{1,0:T(8,128)(2,1)S(1)}, u32[]{:S(2)}, u32[]{:S(2)}) %collective-permute-start.65) | collective-permute-done | bytes 524320 | tf_op jit(solution)/shard_map/ppermute | solution.py:468
  304.0 9.5 %collective-permute-done.55 = bf16[512,512]{1,0:T(8,128)(2,1)S(1)} collective-permute-done((bf16[512,512]{1,0:T(8,128)(2,1)S(1)}, bf16[512,512]{1,0:T(8,128)(2,1)S(1)}, u32[]{:S(2)}, u32[]{:S(2)}) %collective-permute-start.55) | collective-permute-done | bytes 524320 | tf_op jit(solution)/shard_map/ppermute | solution.py:468
  314.2 10.6 %collective-permute-done.45 = bf16[256,1024]{1,0:T(8,128)(2,1)S(1)} collective-permute-done((bf16[256,1024]{1,0:T(8,128)(2,1)S(1)}, bf16[256,1024]{1,0:T(8,128)(2,1)S(1)}, u32[]{:S(2)}, u32[]{:S(2)}) %collective-permute-start.45) | collective-permute-done | bytes 524320 | tf_op jit(solution)/shard_map/ppermute | solution.py:468
  327.2 8.8 %collective-permute-done.15 = bf16[512,512]{1,0:T(8,128)(2,1)S(1)} collective-permute-done((bf16[512,512]{1,0:T(8,128)(2,1)S(1)}, bf16[512,512]{1,0:T(8,128)(2,1)S(1)}, u32[]{:S(2)}, u32[]{:S(2)}) %collective-permute-start.15) | collective-permute-done | bytes 524320 | tf_op jit(solution)/shard_map/ppermute | solution.py:468
  338.4 8.8 %collective-permute-done.25 = bf16[512,512]{1,0:T(8,128)(2,1)S(1)} collective-permute-done((bf16[512,512]{1,0:T(8,128)(2,1)S(1)}, bf16[512,512]{1,0:T(8,128)(2,1)S(1)}, u32[]{:S(2)}, u32[]{:S(2)}) %collective-permute-start.25) | collective-permute-done | bytes 524320 | tf_op jit(solution)/shard_map/ppermute | solution.py:468
  349.6 8.1 %collective-permute-done.35 = bf16[512,512]{1,0:T(8,128)(2,1)S(1)} collective-permute-done((bf16[512,512]{1,0:T(8,128)(2,1)S(1)}, bf16[512,512]{1,0:T(8,128)(2,1)S(1)}, u32[]{:S(2)}, u32[]{:S(2)}) %collective-permute-start.35) | collective-permute-done | bytes 524320 | tf_op jit(solution)/shard_map/ppermute | solution.py:468
  364.3 2.6 collective-permute-done.26
  373.2 2.6 collective-permute-start.68
  376.4 2.6 collective-permute-start.48
  383.1 2.5 collective-permute-start.38
  385.6 4.8 %collective-permute-done.58 = bf16[64,512]{1,0:T(8,128)(2,1)S(1)} collective-permute-done((bf16[64,512]{1,0:T(8,128)(2,1)S(1)}, bf16[64,512]{1,0:T(8,128)(2,1)S(1)}, u32[]{:S(2)}, u32[]{:S(2)}) %collective-permute-start.58) | collective-permute-done | bytes 65568 | tf_op jit(solution)/shard_map/ppermute | solution.py:465
  396.6 4.4 collective-permute-done.38
  404.0 3.1 collective-permute-start.70
  427.4 2.6 collective-permute-done.61
  430.1 5.5 %collective-permute-done.51 = bf16[128,1024]{1,0:T(8,128)(2,1)S(1)} collective-permute-done((bf16[128,1024]{1,0:T(8,128)(2,1)S(1)}, bf16[128,1024]{1,0:T(8,128)(2,1)S(1)}, u32[]{:S(2)}, u32[]{:S(2)}) %collective-permute-start.51) | collective-permute-done | bytes 262176 | tf_op jit(solution)/shard_map/ppermute | solution.py:465
  435.8 5.4 %collective-permute-done.21 = bf16[256,512]{1,0:T(8,128)(2,1)S(1)} collective-permute-done((bf16[256,512]{1,0:T(8,128)(2,1)S(1)}, bf16[256,512]{1,0:T(8,128)(2,1)S(1)}, u32[]{:S(2)}, u32[]{:S(2)}) %collective-permute-start.21) | collective-permute-done | bytes 262176 | tf_op jit(solution)/shard_map/ppermute | solution.py:465
  441.4 4.4 collective-permute-done.31
  445.9 2.7 collective-permute-done.41
  (391 shorter events, 133.1 us)
Async XLA Ops:
  2.9 16.1 %collective-permute-start = (bf16[3,512]{1,0:T(4,128)(2,1)S(1)}, bf16[3,512]{1,0:T(4,128)(2,1)S(1)}, u32[]{:S(2)}, u32[]{:S(2)}) collective-permute-start(bf16[3,512]{1,0:T(4,128)(2,1)S(1)} %pad_maximum_fusion.24), channel_id=1, source_target_pairs={{0,1},{1,0},{2,3},{3,2},{4,5},{5,4},{6,7},{7,6},{8,9},{9,8},{10,11... | collective-permute-start | bytes 9224 | tf_op jit(solution)/shard_map/ppermute | solution.py:468
  8.2 25.0 %collective-permute-start.3 = (bf16[512,512]{1,0:T(8,128)(2,1)S(1)}, bf16[512,512]{1,0:T(8,128)(2,1)}, u32[]{:S(2)}, u32[]{:S(2)}) collective-permute-start(bf16[512,512]{1,0:T(8,128)(2,1)S(1)} %constant_dynamic-slice_fusion.35), channel_id=1, source_target_pairs={{0,1},{1,0},{2,3},{3,2},{4,5},{5,4},{6,7},{7,6},{8,9},{9,8},{10,11... | collective-permute-start | bytes 1572872 | tf_op jit(solution)/shard_map/ppermute | solution.py:468
  11.1 42.6 %collective-permute-start.1 = (bf16[512,512]{1,0:T(8,128)(2,1)}, bf16[512,512]{1,0:T(8,128)(2,1)}, u32[]{:S(2)}, u32[]{:S(2)}) collective-permute-start(bf16[512,512]{1,0:T(8,128)(2,1)} %constant_dynamic-slice_fusion.36), channel_id=1, source_target_pairs={{0,1},{1,0},{2,3},{3,2},{4,5},{5,4},{6,7},{7,6},{8,9},{9,8},{10,11... | collective-permute-start | bytes 1572872 | tf_op jit(solution)/shard_map/ppermute | solution.py:468
  12.0 43.6 %collective-permute-start.11 = (bf16[256,1024]{1,0:T(8,128)(2,1)}, bf16[256,1024]{1,0:T(8,128)(2,1)S(1)}, u32[]{:S(2)}, u32[]{:S(2)}) collective-permute-start(bf16[256,1024]{1,0:T(8,128)(2,1)} %constant_dynamic-slice_fusion.31), channel_id=1, source_target_pairs={{0,1},{1,0},{2,3},{3,2},{4,5},{5,4},{6,7},{7,6},{8,9},{9,8},{10,11... | collective-permute-start | bytes 1572872 | tf_op jit(solution)/shard_map/ppermute | solution.py:468
  19.0 47.9 %collective-permute-start.9 = (bf16[512,512]{1,0:T(8,128)(2,1)}, bf16[512,512]{1,0:T(8,128)(2,1)}, u32[]{:S(2)}, u32[]{:S(2)}) collective-permute-start(bf16[512,512]{1,0:T(8,128)(2,1)} %constant_dynamic-slice_fusion.32), channel_id=1, source_target_pairs={{0,1},{1,0},{2,3},{3,2},{4,5},{5,4},{6,7},{7,6},{8,9},{9,8},{10,11... | collective-permute-start | bytes 1572872 | tf_op jit(solution)/shard_map/ppermute | solution.py:468
  22.0 54.8 %collective-permute-start.7 = (bf16[256,1024]{1,0:T(8,128)(2,1)}, bf16[256,1024]{1,0:T(8,128)(2,1)}, u32[]{:S(2)}, u32[]{:S(2)}) collective-permute-start(bf16[256,1024]{1,0:T(8,128)(2,1)} %constant_dynamic-slice_fusion.33), channel_id=1, source_target_pairs={{0,1},{1,0},{2,3},{3,2},{4,5},{5,4},{6,7},{7,6},{8,9},{9,8},{10,11... | collective-permute-start | bytes 1572872 | tf_op jit(solution)/shard_map/ppermute | solution.py:468
  33.3 43.5 %collective-permute-start.6 = (bf16[512,512]{1,0:T(8,128)(2,1)}, bf16[512,512]{1,0:T(8,128)(2,1)}, u32[]{:S(2)}, u32[]{:S(2)}) collective-permute-start(bf16[512,512]{1,0:T(8,128)(2,1)} %collective-permute-done.5), channel_id=1, source_target_pairs={{0,2},{2,0},{4,6},{6,4},{8,10},{10,8},{12,14},{14,12},{16,18},{18,... | collective-permute-start | bytes 1572872 | tf_op jit(solution)/shard_map/ppermute | solution.py:465
  53.8 25.9 %collective-permute-start.4 = (bf16[512,512]{1,0:T(8,128)(2,1)}, bf16[512,512]{1,0:T(8,128)(2,1)S(1)}, u32[]{:S(2)}, u32[]{:S(2)}) collective-permute-start(bf16[512,512]{1,0:T(8,128)(2,1)} %collective-permute-done.3), channel_id=1, source_target_pairs={{0,2},{2,0},{4,6},{6,4},{8,10},{10,8},{12,14},{14,12},{16,18},{18,... | collective-permute-start | bytes 1572872 | tf_op jit(solution)/shard_map/ppermute | solution.py:465
  55.6 25.2 %collective-permute-start.2 = (bf16[512,512]{1,0:T(8,128)(2,1)}, bf16[512,512]{1,0:T(8,128)(2,1)S(1)}, u32[]{:S(2)}, u32[]{:S(2)}) collective-permute-start(bf16[512,512]{1,0:T(8,128)(2,1)} %collective-permute-done.1), channel_id=1, source_target_pairs={{0,2},{2,0},{4,6},{6,4},{8,10},{10,8},{12,14},{14,12},{16,18},{18,... | collective-permute-start | bytes 1572872 | tf_op jit(solution)/shard_map/ppermute | solution.py:465
  67.0 18.6 %collective-permute-start.12 = (bf16[256,1024]{1,0:T(8,128)(2,1)S(1)}, bf16[256,1024]{1,0:T(8,128)(2,1)S(1)}, u32[]{:S(2)}, u32[]{:S(2)}) collective-permute-start(bf16[256,1024]{1,0:T(8,128)(2,1)S(1)} %collective-permute-done.11), channel_id=1, source_target_pairs={{0,2},{2,0},{4,6},{6,4},{8,10},{10,8},{12,14},{14,12},{16,18},{18,... | collective-permute-start | bytes 1572872 | tf_op jit(solution)/shard_map/ppermute | solution.py:465
  228.3 55.2 %collective-permute-start.64 = (bf16[256,1024]{1,0:T(8,128)(2,1)}, bf16[256,1024]{1,0:T(8,128)(2,1)}, u32[]{:S(2)}, u32[]{:S(2)}) collective-permute-start(bf16[256,1024]{1,0:T(8,128)(2,1)} %constant_dynamic-slice_fusion.4), channel_id=1, source_target_pairs={{0,2},{2,0},{4,6},{6,4},{8,10},{10,8},{12,14},{14,12},{16,18},{18,... | collective-permute-start | bytes 1572872 | tf_op jit(solution)/shard_map/ppermute | solution.py:465
  228.3 61.9 %collective-permute-start.63 = (bf16[256,1024]{1,0:T(8,128)(2,1)}, bf16[256,1024]{1,0:T(8,128)(2,1)}, u32[]{:S(2)}, u32[]{:S(2)}) collective-permute-start(bf16[256,1024]{1,0:T(8,128)(2,1)} %constant_dynamic-slice_fusion.5), channel_id=1, source_target_pairs={{0,2},{2,0},{4,6},{6,4},{8,10},{10,8},{12,14},{14,12},{16,18},{18,... | collective-permute-start | bytes 1572872 | tf_op jit(solution)/shard_map/ppermute | solution.py:465
  228.8 56.5 %collective-permute-start.54 = (bf16[512,512]{1,0:T(8,128)(2,1)}, bf16[512,512]{1,0:T(8,128)(2,1)}, u32[]{:S(2)}, u32[]{:S(2)}) collective-permute-start(bf16[512,512]{1,0:T(8,128)(2,1)} %constant_dynamic-slice_fusion.9), channel_id=1, source_target_pairs={{0,2},{2,0},{4,6},{6,4},{8,10},{10,8},{12,14},{14,12},{16,18},{18,... | collective-permute-start | bytes 1572872 | tf_op jit(solution)/shard_map/ppermute | solution.py:465
  228.8 75.1 %collective-permute-start.53 = (bf16[512,512]{1,0:T(8,128)(2,1)}, bf16[512,512]{1,0:T(8,128)(2,1)S(1)}, u32[]{:S(2)}, u32[]{:S(2)}) collective-permute-start(bf16[512,512]{1,0:T(8,128)(2,1)} %constant_dynamic-slice_fusion.10), channel_id=1, source_target_pairs={{0,2},{2,0},{4,6},{6,4},{8,10},{10,8},{12,14},{14,12},{16,18},{18,... | collective-permute-start | bytes 1572872 | tf_op jit(solution)/shard_map/ppermute | solution.py:465
  232.9 30.8 %collective-permute-start.73 = (f32[9,1024]{1,0:T(8,128)S(1)}, f32[9,1024]{1,0:T(8,128)S(1)}, u32[]{:S(2)}, u32[]{:S(2)}) collective-permute-start(f32[9,1024]{1,0:T(8,128)S(1)} %stack.31), channel_id=1, source_target_pairs={{0,2},{2,0},{4,6},{6,4},{8,10},{10,8},{12,14},{14,12},{16,18},{18,... | collective-permute-start | bytes 110600 | tf_op jit(solution)/shard_map/ppermute | solution.py:465
  288.0 25.6 %collective-permute-start.55 = (bf16[512,512]{1,0:T(8,128)(2,1)S(1)}, bf16[512,512]{1,0:T(8,128)(2,1)S(1)}, u32[]{:S(2)}, u32[]{:S(2)}) collective-permute-start(bf16[512,512]{1,0:T(8,128)(2,1)S(1)} %add_convert_fusion.4), channel_id=1, source_target_pairs={{0,1},{1,0},{2,3},{3,2},{4,5},{5,4},{6,7},{7,6},{8,9},{9,8},{10,11... | collective-permute-start | bytes 1572872 | tf_op jit(solution)/shard_map/ppermute | solution.py:468
  290.0 24.1 %collective-permute-start.43 = (bf16[256,1024]{1,0:T(8,128)(2,1)S(1)}, bf16[256,1024]{1,0:T(8,128)(2,1)S(1)}, u32[]{:S(2)}, u32[]{:S(2)}) collective-permute-start(bf16[256,1024]{1,0:T(8,128)(2,1)S(1)} %copy-done.33), channel_id=1, source_target_pairs={{0,2},{2,0},{4,6},{6,4},{8,10},{10,8},{12,14},{14,12},{16,18},{18,... | collective-permute-start | bytes 1572872 | tf_op jit(solution)/shard_map/ppermute | solution.py:465
  290.2 35.2 %collective-permute-start.13 = (bf16[512,512]{1,0:T(8,128)(2,1)S(1)}, bf16[512,512]{1,0:T(8,128)(2,1)S(1)}, u32[]{:S(2)}, u32[]{:S(2)}) collective-permute-start(bf16[512,512]{1,0:T(8,128)(2,1)S(1)} %copy-done.35), channel_id=1, source_target_pairs={{0,2},{2,0},{4,6},{6,4},{8,10},{10,8},{12,14},{14,12},{16,18},{18,... | collective-permute-start | bytes 1572872 | tf_op jit(solution)/shard_map/ppermute | solution.py:465
  302.3 22.5 %collective-permute-start.45 = (bf16[256,1024]{1,0:T(8,128)(2,1)S(1)}, bf16[256,1024]{1,0:T(8,128)(2,1)S(1)}, u32[]{:S(2)}, u32[]{:S(2)}) collective-permute-start(bf16[256,1024]{1,0:T(8,128)(2,1)S(1)} %add_convert_fusion.7), channel_id=1, source_target_pairs={{0,1},{1,0},{2,3},{3,2},{4,5},{5,4},{6,7},{7,6},{8,9},{9,8},{10,11... | collective-permute-start | bytes 1572872 | tf_op jit(solution)/shard_map/ppermute | solution.py:468
  304.0 34.1 %collective-permute-start.23 = (bf16[512,512]{1,0:T(8,128)(2,1)S(1)}, bf16[512,512]{1,0:T(8,128)(2,1)S(1)}, u32[]{:S(2)}, u32[]{:S(2)}) collective-permute-start(bf16[512,512]{1,0:T(8,128)(2,1)S(1)} %copy-done.34), channel_id=1, source_target_pairs={{0,2},{2,0},{4,6},{6,4},{8,10},{10,8},{12,14},{14,12},{16,18},{18,... | collective-permute-start | bytes 1572872 | tf_op jit(solution)/shard_map/ppermute | solution.py:465
  313.6 22.5 %collective-permute-start.15 = (bf16[512,512]{1,0:T(8,128)(2,1)S(1)}, bf16[512,512]{1,0:T(8,128)(2,1)S(1)}, u32[]{:S(2)}, u32[]{:S(2)}) collective-permute-start(bf16[512,512]{1,0:T(8,128)(2,1)S(1)} %add_convert_fusion.16), channel_id=1, source_target_pairs={{0,1},{1,0},{2,3},{3,2},{4,5},{5,4},{6,7},{7,6},{8,9},{9,8},{10,11... | collective-permute-start | bytes 1572872 | tf_op jit(solution)/shard_map/ppermute | solution.py:468
  314.1 35.1 %collective-permute-start.33 = (bf16[512,512]{1,0:T(8,128)(2,1)S(1)}, bf16[512,512]{1,0:T(8,128)(2,1)S(1)}, u32[]{:S(2)}, u32[]{:S(2)}) collective-permute-start(bf16[512,512]{1,0:T(8,128)(2,1)S(1)} %constant_dynamic-slice_fusion.20), channel_id=1, source_target_pairs={{0,2},{2,0},{4,6},{6,4},{8,10},{10,8},{12,14},{14,12},{16,18},{18,... | collective-permute-start | bytes 1572872 | tf_op jit(solution)/shard_map/ppermute | solution.py:465
  324.8 22.5 %collective-permute-start.25 = (bf16[512,512]{1,0:T(8,128)(2,1)S(1)}, bf16[512,512]{1,0:T(8,128)(2,1)S(1)}, u32[]{:S(2)}, u32[]{:S(2)}) collective-permute-start(bf16[512,512]{1,0:T(8,128)(2,1)S(1)} %add_convert_fusion.13), channel_id=1, source_target_pairs={{0,1},{1,0},{2,3},{3,2},{4,5},{5,4},{6,7},{7,6},{8,9},{9,8},{10,11... | collective-permute-start | bytes 1572872 | tf_op jit(solution)/shard_map/ppermute | solution.py:468
  325.4 32.3 %collective-permute-start.35 = (bf16[512,512]{1,0:T(8,128)(2,1)S(1)}, bf16[512,512]{1,0:T(8,128)(2,1)S(1)}, u32[]{:S(2)}, u32[]{:S(2)}) collective-permute-start(bf16[512,512]{1,0:T(8,128)(2,1)S(1)} %add_convert_fusion.10), channel_id=1, source_target_pairs={{0,1},{1,0},{2,3},{3,2},{4,5},{5,4},{6,7},{7,6},{8,9},{9,8},{10,11... | collective-permute-start | bytes 1572872 | tf_op jit(solution)/shard_map/ppermute | solution.py:468
  336.0 23.7 %collective-permute-start.66 = (bf16[128,1024]{1,0:T(8,128)(2,1)S(1)}, bf16[128,1024]{1,0:T(8,128)(2,1)S(1)}, u32[]{:S(2)}, u32[]{:S(2)}) collective-permute-start(bf16[128,1024]{1,0:T(8,128)(2,1)S(1)} %constant_dynamic-slice_fusion.3), channel_id=1, source_target_pairs={{0,4},{2,6},{4,0},{6,2},{8,12},{10,14},{12,8},{14,10},{16,20},{18,... | collective-permute-start | bytes 786440 | tf_op jit(solution)/shard_map/ppermute | solution.py:465
  338.1 22.1 %collective-permute-start.56 = (bf16[256,512]{1,0:T(8,128)(2,1)S(1)}, bf16[256,512]{1,0:T(8,128)(2,1)S(1)}, u32[]{:S(2)}, u32[]{:S(2)}) collective-permute-start(bf16[256,512]{1,0:T(8,128)(2,1)S(1)} %constant_dynamic-slice_fusion.8), channel_id=1, source_target_pairs={{0,4},{2,6},{4,0},{6,2},{8,12},{10,14},{12,8},{14,10},{16,20},{18,... | collective-permute-start | bytes 786440 | tf_op jit(solution)/shard_map/ppermute | solution.py:465
  383.1 17.9 %collective-permute-start.38 = (bf16[64,512]{1,0:T(8,128)(2,1)S(1)}, bf16[64,512]{1,0:T(8,128)(2,1)S(1)}, u32[]{:S(2)}, u32[]{:S(2)}) collective-permute-start(bf16[64,512]{1,0:T(8,128)(2,1)S(1)} %constant_dynamic-slice_fusion.16), channel_id=1, source_target_pairs={{0,16},{2,18},{4,20},{6,22},{8,24},{10,26},{12,28},{14,30},{16,0},... | collective-permute-start | bytes 196616 | tf_op jit(solution)/shard_map/ppermute | solution.py:465
  423.5 17.7 %collective-permute-start.21 = (bf16[256,512]{1,0:T(8,128)(2,1)S(1)}, bf16[256,512]{1,0:T(8,128)(2,1)S(1)}, u32[]{:S(2)}, u32[]{:S(2)}) collective-permute-start(bf16[256,512]{1,0:T(8,128)(2,1)S(1)} %pad_maximum_fusion.12), channel_id=1, source_target_pairs={{0,4},{2,6},{4,0},{6,2},{8,12},{10,14},{12,8},{14,10},{16,20},{18,... | collective-permute-start | bytes 786440 | tf_op jit(solution)/shard_map/ppermute | solution.py:465
  425.0 20.8 %collective-permute-start.31 = (bf16[256,512]{1,0:T(8,128)(2,1)S(1)}, bf16[256,512]{1,0:T(8,128)(2,1)S(1)}, u32[]{:S(2)}, u32[]{:S(2)}) collective-permute-start(bf16[256,512]{1,0:T(8,128)(2,1)S(1)} %pad_maximum_fusion.13), channel_id=1, source_target_pairs={{0,4},{2,6},{4,0},{6,2},{8,12},{10,14},{12,8},{14,10},{16,20},{18,... | collective-permute-start | bytes 786440 | tf_op jit(solution)/shard_map/ppermute | solution.py:465
  426.4 22.2 %collective-permute-start.41 = (bf16[256,512]{1,0:T(8,128)(2,1)S(1)}, bf16[256,512]{1,0:T(8,128)(2,1)S(1)}, u32[]{:S(2)}, u32[]{:S(2)}) collective-permute-start(bf16[256,512]{1,0:T(8,128)(2,1)S(1)} %pad_maximum_fusion.14), channel_id=1, source_target_pairs={{0,4},{2,6},{4,0},{6,2},{8,12},{10,14},{12,8},{14,10},{16,20},{18,... | collective-permute-start | bytes 786440 | tf_op jit(solution)/shard_map/ppermute | solution.py:465
  430.0 23.0 %collective-permute-start.72 = (bf16[256,1024]{1,0:T(8,128)(2,1)S(1)}, bf16[256,1024]{1,0:T(8,128)(2,1)S(1)}, u32[]{:S(2)}, u32[]{:S(2)}) collective-permute-start(bf16[256,1024]{1,0:T(8,128)(2,1)S(1)} %pad_maximum_fusion.11), channel_id=1, source_target_pairs={{0,2},{2,0},{4,6},{6,4},{8,10},{10,8},{12,14},{14,12},{16,18},{18,... | collective-permute-start | bytes 1572872 | tf_op jit(solution)/shard_map/ppermute | solution.py:465
  435.6 15.5 %collective-permute-start.62 = (bf16[512,512]{1,0:T(8,128)(2,1)S(1)}, bf16[512,512]{1,0:T(8,128)(2,1)S(1)}, u32[]{:S(2)}, u32[]{:S(2)}) collective-permute-start(bf16[512,512]{1,0:T(8,128)(2,1)S(1)} %pad_maximum_fusion.10), channel_id=1, source_target_pairs={{0,2},{2,0},{4,6},{6,4},{8,10},{10,8},{12,14},{14,12},{16,18},{18,... | collective-permute-start | bytes 1572872 | tf_op jit(solution)/shard_map/ppermute | solution.py:465
  (95 other events, 916.5 us)

commit v3 on v2

v3 whole, which is shorter than its diff:
```python
from functools import partial
import math

import jax
import jax.numpy as jnp
from jax import lax
from jax.experimental import pallas as pl
from jax.experimental.pallas import tpu as pltpu
from jax.sharding import PartitionSpec as P

HS = 128
CROP = 512


EPSILON = 1e-05


def dot(left, right, left_dim, right_dim):
    return lax.dot_general(
        left,
        right,
        (((left_dim,), (right_dim,)), ((), ())),
        preferred_element_type=jnp.float32,
    )


def unit_rows(rows):
    center = rows - jnp.mean(rows, axis=-1, keepdims=True)
    inverse = lax.rsqrt(jnp.mean(center * center, axis=-1, keepdims=True) + EPSILON)
    return center * inverse, inverse


def unit_rows_back(scaled, unit, inverse):
    inner = scaled - jnp.mean(scaled, axis=-1, keepdims=True)
    return (inner - unit * jnp.mean(scaled * unit, axis=-1, keepdims=True)) * inverse


def low(array):
    return array.astype(jnp.bfloat16)


def attend_kernel(first, live_ref, source_ref, *refs):
    if first:
        gain_ref, shift_ref, *refs = refs
    query_weight, key_weight, value_weight, query_bias, value_bias, *refs = refs
    if first:
        normed_ref, *refs = refs
    query_ref, keys_ref, values_ref, weights_ref, attended_ref, inverse_ref = refs

    @pl.when(pl.program_id(0) < live_ref[0])
    def _():
        if first:
            unit, _ = unit_rows(source_ref[...].astype(jnp.float32))
            normed_ref[...] = low(unit * gain_ref[...] + shift_ref[...])
            normed = normed_ref[...]
        else:
            normed = source_ref[...]
        query_ref[...] = low(dot(normed, query_weight[...], 1, 0) + query_bias[...])
        keys_ref[...] = low(dot(normed, key_weight[...], 1, 0))
        values_ref[...] = low(dot(normed, value_weight[...], 1, 0) + value_bias[...])
        ones = jnp.ones((CROP, HS), jnp.bfloat16)
        for head in range(query_ref.shape[1] // HS):
            columns = pl.ds(head * HS, HS)
            scores = dot(query_ref[:, columns], keys_ref[:, columns], 1, 1)
            highest = jnp.max(scores, axis=-1, keepdims=True)
            weights = low(jnp.exp2((scores - highest) * (math.log2(math.e) / math.sqrt(HS))))
            weights_ref[head] = weights
            extended = jnp.concatenate([values_ref[:, columns], ones], axis=1)
            mixed = dot(weights, extended, 1, 0)
            inverse = 1.0 / mixed[:, HS:]
            inverse_ref[:, columns] = inverse
            attended_ref[:, columns] = low(mixed[:, :HS] * inverse)


def gelu_pair(before):
    lower = 0.5 + 0.5 * lax.erf(before * math.sqrt(0.5))
    density = jnp.exp2(before * before * (-0.5 * math.log2(math.e)))
    slope = lower + before * density * (1.0 / math.sqrt(2.0 * math.pi))
    return before * lower, slope


def feed_kernel(
    crops,
    split,
    live_ref,
    latents_ref,
    cotangent_ref,
    attended_refs,
    out_weights,
    up_weights,
    down_weights,
    up_biases,
    out_bias,
    down_bias,
    gain,
    shift,
    output_ref,
    hidden_grad_ref,
    attended_grads,
    packed,
    up_bias_grads,
    vectors_ref,
    out_sums,
    up_sums,
    down_sums,
):
    step = pl.program_id(0)

    @pl.when(step == 0)
    def _():
        for sums in (*out_sums, *up_sums, *down_sums, *up_bias_grads, vectors_ref):
            sums[...] = jnp.zeros_like(sums)

    @pl.when(step >= live_ref[0])
    def _():
        output_ref[...] = jnp.zeros_like(output_ref)
        hidden_grad_ref[...] = jnp.zeros_like(hidden_grad_ref)

    @pl.when(step < live_ref[0])
    def _():
        hidden = latents_ref[...].astype(jnp.float32) + out_bias[...]
        for part in range(2):
            hidden = hidden + dot(attended_refs[part][...], out_weights[part][...], 1, 0)
        unit, inverse = unit_rows(hidden)
        normed = low(unit * gain[...] + shift[...])
        top = cotangent_ref[...]
        result = hidden + down_bias[...]
        second_grad = jnp.zeros(hidden.shape, jnp.float32)
        for part in range(2):
            before = dot(normed, up_weights[part][...], 1, 0) + up_biases[part][...]
            value, slope = gelu_pair(before)
            activated = low(value)
            result = result + dot(activated, down_weights[part][...], 1, 0)
            down_sums[part][...] += dot(activated, top, 0, 0)
            activated_grad = dot(top, down_weights[part][...], 1, 1)
            before_grad = low(activated_grad * slope)
            up_bias_grads[part][...] += jnp.sum(
                before_grad.astype(jnp.float32), axis=0, keepdims=True
            )
            up_sums[part][...] += dot(normed, before_grad, 0, 0)
            second_grad = second_grad + dot(before_grad, up_weights[part][...], 1, 1)
        output_ref[...] = low(result)
        top_grad = top.astype(jnp.float32)
        hidden_grad = top_grad + unit_rows_back(second_grad * gain[...], unit, inverse)
        hidden_grad_ref[...] = hidden_grad
        hidden_low = low(hidden_grad)
        for part in range(2):
            out_sums[part][...] += dot(attended_refs[part][...], hidden_low, 0, 0)
            attended_grads[part][...] = low(dot(hidden_low, out_weights[part][...], 1, 1))
        for row, term in enumerate((second_grad * unit, second_grad, hidden_grad, top_grad)):
            vectors_ref[row : row + 1] += jnp.sum(term, axis=0, keepdims=True)

    @pl.when(step == crops - 1)
    def _():
        if not split:
            for grads, sums in zip(packed, (down_sums, out_sums, up_sums)):
                for part in range(2):
                    grads[part][...] = low(sums[part][...])
            return
        for group, core in zip(packed, (live_ref[1], 1 - live_ref[1])):
            tall_ref, flat_ref = group
            rows = flat_ref.shape[0] // 2
            short = tall_ref.shape[0] // (4 * PIECES)
            half = tall_ref.shape[1] // 2
            for part in range(2):
                flat_ref[part * rows : (part + 1) * rows] = low(
                    up_sums[part][pl.ds(pl.multiple_of(core * rows, rows), rows), :]
                )
                for piece in range(PIECES):
                    start = core * (PIECES * short) + piece * short
                    source = pl.ds(pl.multiple_of(start, short), short)
                    for side in range(2):
                        base = part * rows + (2 * piece + side) * short
                        across = pl.ds(side * half, half)
                        for index, sums in enumerate((down_sums, out_sums)):
                            tall_ref[base : base + short, index * half : (index + 1) * half] = low(
                                sums[part][source, across]
                            )


def attend_back_kernel(
    crops,
    split,
    live_ref,
    normed_ref,
    queries,
    keys,
    values,
    weights,
    inverses,
    attended,
    attended_grads,
    matrices,
    previous,
    packed_before,
    grads,
    packed,
    bias_grads,
    gain_terms,
    shift_terms,
    joined,
    sums,
):
    step = pl.program_id(0)
    scale = 1.0 / math.sqrt(HS)
    widths = [ref.shape[1] for ref in queries]
    bases = (0, 3 * widths[0])

    @pl.when(step == 0)
    def _():
        sums[...] = jnp.zeros_like(sums)
        for part in range(2):
            bias_grads[part][...] = jnp.zeros_like(bias_grads[part])

    @pl.when(step < live_ref[0])
    def _():
        for part in range(2):
            for head in range(widths[part] // HS):
                columns = pl.ds(head * HS, HS)

                def put(kind, value):
                    value = low(value)
                    grads[kind][part][:, columns] = value
                    joined[:, pl.ds(bases[part] + kind * widths[part] + head * HS, HS)] = value

                inner = attended_grads[part][:, columns].astype(jnp.float32)
                inner = inner * inverses[part][:, columns]
                upstream = low(inner)
                total = jnp.sum(
                    inner * attended[part][:, columns].astype(jnp.float32), axis=1, keepdims=True
                )
                head_weights = weights[part][head]
                put(2, dot(head_weights, upstream, 0, 0))
                probs_grad = dot(upstream, values[part][:, columns], 1, 1)
                scores_grad = low(head_weights.astype(jnp.float32) * (probs_grad - total))
                put(0, dot(scores_grad, keys[part][:, columns], 1, 0) * scale)
                put(1, dot(scores_grad, queries[part][:, columns], 0, 0) * scale)
            for kind in range(3):
                bias_grads[part][kind : kind + 1] += jnp.sum(
                    grads[kind][part][...].astype(jnp.float32), axis=0, keepdims=True
                )
        sums[...] += dot(normed_ref[...], joined[...], 0, 0)

    @pl.when(step == crops - 1)
    def _():
        gain_terms[...] = jnp.zeros_like(gain_terms)
        shift_terms[...] = jnp.zeros_like(shift_terms)
        for part in range(2):
            for kind in range(3):
                matrix = matrices[kind][part]
                base = bases[part] + kind * widths[part]
                for start in range(0, widths[part], HS):
                    gain_terms[...] += sums[:, pl.ds(base + start, HS)] * matrix[
                        :, pl.ds(start, HS)
                    ].astype(jnp.float32)
                bias = bias_grads[part][kind : kind + 1]
                rough = low(bias)
                fine = low(bias - rough.astype(jnp.float32))
                shift_terms[...] += dot(
                    jnp.concatenate([rough, fine] + [jnp.zeros_like(rough)] * 6, axis=0),
                    matrix[...],
                    1,
                    1,
                )
        if not split:
            packed[0][...] = low(sums[...])
            return
        half = sums.shape[0] // 2
        for target, core in zip(packed, (live_ref[1], 1 - live_ref[1])):
            rows = pl.ds(pl.multiple_of(core * half, half), half)
            for part in range(2):
                target[part * half : (part + 1) * half] = low(
                    sums[rows, pl.ds(bases[part], 3 * widths[part])]
                )


def latents_kernel(
    first, live_ref, latents_ref, hidden_grad_ref, grads, matrices, gain_ref, previous, output_ref
):
    crop = pl.program_id(0) + first

    @pl.when(crop >= live_ref[0])
    def _():
        output_ref[...] = jnp.zeros_like(output_ref)

    @pl.when(crop < live_ref[0])
    def _():
        unit, inverse = unit_rows(latents_ref[...].astype(jnp.float32))
        upstream = jnp.zeros(output_ref.shape, jnp.float32)
        for kind in range(3):
            for grad, matrix in zip(grads[kind], matrices[kind]):
                upstream = upstream + dot(grad[...], matrix[...], 1, 1)
        output_ref[...] = hidden_grad_ref[...] + unit_rows_back(
            upstream * gain_ref[...], unit, inverse
        )


def finish_kernel(places_ref, groups, *outputs):
    for half, group in enumerate(groups):
        for index, source in enumerate(group):
            pieces = 16 // len(group)
            size = source.shape[0] // pieces
            width = source.shape[1] // 6
            for piece in range(pieces):
                start = pl.multiple_of(places_ref[index * pieces + piece] * size, size)
                for column in range(6):
                    phase, kind = 2 * half + column // 3, column % 3
                    outputs[kind][pl.ds(start, size), pl.ds(phase * width, width)] = source[
                        piece * size : (piece + 1) * size, pl.ds(column * width, width)
                    ].astype(jnp.float32)


def finish_feed_kernel(places_ref, sources, down_ref, out_ref, up_ref):
    half = up_ref.shape[1]
    for index, source in enumerate(sources):
        pieces = 16 // len(sources)
        size = source.shape[0] // pieces
        short = size // 2
        for piece in range(pieces):
            place = places_ref[index * pieces + piece]
            up_ref[pl.ds(pl.multiple_of(place * size, size), size), :] = source[
                piece * size : (piece + 1) * size, pl.ds(2 * half, half)
            ].astype(jnp.float32)
            rows = pl.ds(pl.multiple_of(place * short, short), short)
            for side in range(2):
                start = piece * size + side * short
                for column, target in enumerate((down_ref, out_ref)):
                    target[rows, pl.ds(side * half, half)] = source[
                        start : start + short, pl.ds(column * half, half)
                    ].astype(jnp.float32)


def rows_kernel(
    place_ref, gains, shifts, biases, feed_vectors, up_biases, gain_ref, shift_ref, rows_ref
):
    gain_terms = gains[0][...]
    shift_terms = shifts[0][...]
    for more in gains[1:]:
        gain_terms = gain_terms + more[...]
    for more in shifts[1:]:
        shift_terms = shift_terms + more[...]
    shift_grad = jnp.sum(shift_terms, axis=0, keepdims=True)
    unscaled = jnp.sum(gain_terms.T, axis=0, keepdims=True)
    rows_ref[...] = jnp.zeros_like(rows_ref)
    rows_ref[0:1] = (unscaled - shift_ref[...] * shift_grad) / gain_ref[...]
    rows_ref[1:2] = shift_grad
    rows_ref[2:6] = feed_vectors[0:4]

    def put(row, own, rest):
        own = jnp.concatenate(own, axis=1)
        rest = jnp.concatenate(rest, axis=1)
        rows_ref[row : row + 1] = jnp.where(
            place_ref[0] == 0,
            jnp.concatenate([own, rest], axis=1),
            jnp.concatenate([rest, own], axis=1),
        )

    for row, kind in ((6, 0), (7, 2)):
        put(row, *([pair[part][kind : kind + 1] for pair in biases] for part in range(2)))
    put(8, *([array[...]] for array in up_biases))


PIECES = 8
VMEM_LIMIT = 66_000_000
COST_SCALE = 8


def row_block(width, column=0):
    return pl.BlockSpec((CROP, width), lambda i, live: (i, column))


def fixed(rows, width, column=0):
    return pl.BlockSpec((rows, width), lambda i, live: (0, column), pipeline_mode=pl.Buffered(1))


def shaped(shape, dtype=jnp.bfloat16):
    return jax.ShapeDtypeStruct(shape, dtype)


def run(
    kernel, name, crops, in_specs, out_specs, out_shape, flops, moved, scratch=(), aliases=None
):
    return pl.pallas_call(
        kernel,
        input_output_aliases=aliases or {},
        name=name,
        out_shape=out_shape,
        grid_spec=pltpu.PrefetchScalarGridSpec(
            num_scalar_prefetch=1,
            grid=(crops,),
            in_specs=in_specs,
            out_specs=out_specs,
            scratch_shapes=scratch,
        ),
        compiler_params=pltpu.CompilerParams(
            dimension_semantics=("arbitrary",), vmem_limit_bytes=VMEM_LIMIT
        ),
        cost_estimate=pl.CostEstimate(
            flops=COST_SCALE * flops, bytes_accessed=COST_SCALE * moved, transcendentals=0
        ),
    )


def attend(live, source, norm, matrices, biases):
    count, width = source.shape
    crops = count // CROP
    units = matrices[0].shape[1]
    heads = units // HS
    first = norm is not None
    vector = fixed(1, units)
    outs = (row_block(width),) * first + (
        row_block(units),
        row_block(units),
        row_block(units),
        pl.BlockSpec((None, heads, CROP, CROP), lambda i, live: (i, 0, 0, 0)),
        row_block(units),
        row_block(units),
    )
    rows = shaped((count, units))
    shapes = (shaped((count, width)),) * first + (
        rows,
        rows,
        rows,
        shaped((crops, heads, CROP, CROP)),
        rows,
        shaped((count, units), jnp.float32),
    )
    return run(
        partial(attend_kernel, first),
        "attend_first" if first else "attend_rest",
        crops,
        (row_block(width),)
        + (fixed(1, width),) * (2 * first)
        + (fixed(width, units),) * 3
        + (vector,) * 2,
        outs,
        shapes,
        2 * count * units * (3 * width + 2 * CROP),
        count * (units * (12 + 2 * CROP // HS) + 4 * width),
    )(live, source, *(norm or ()), *matrices, *biases)


def feed(live, latents, cotangent, attended, outs, ups, downs, up_biases, vectors, split):
    count, width = latents.shape
    crops = count // CROP
    units = [array.shape[1] for array in attended]
    both = lambda make: tuple(make(size) for size in units)
    row_in = both(row_block)
    tall = both(lambda size: fixed(size, width))
    flat = both(lambda size: fixed(width, size))
    thin = both(lambda size: fixed(1, size))
    vector = fixed(1, width)
    sums = lambda dtype: (
        both(lambda size: dtype((size, width))),
        both(lambda size: dtype((width, size))),
        both(lambda size: dtype((size, width))),
    )
    if split:
        packed_specs = ((fixed(width, width), fixed(width, width // 2)),) * 2
        packed_shapes = ((shaped((width, width)), shaped((width, width // 2))),) * 2
    else:
        packed_specs = (tall, tall, flat)
        out_shapes, up_shapes, down_shapes = sums(shaped)
        packed_shapes = (down_shapes, out_shapes, up_shapes)
    return run(
        partial(feed_kernel, crops, split),
        "feed",
        crops,
        (row_block(width), row_block(width), row_in, tall, flat, tall, thin)
        + (vector,) * 4,
        (row_block(width), row_block(width), row_in, packed_specs, thin, fixed(8, width)),
        (
            shaped((count, width)),
            shaped((count, width), jnp.float32),
            both(lambda size: shaped((count, size))),
            packed_shapes,
            both(lambda size: shaped((1, size), jnp.float32)),
            shaped((8, width), jnp.float32),
        ),
        2 * count * width * width * 9,
        count * width * 14,
        sums(lambda shape: pltpu.VMEM(shape, jnp.float32)),
    )(live, latents, cotangent, attended, outs, ups, downs, up_biases, *vectors)


def attend_back(
    live, normed, saved, attended_grads, matrices, widths, phase, previous, packed_before, split
):
    count, width = normed.shape
    crops = count // CROP
    both = lambda make: tuple(make(size) for size in widths)
    units = [array.shape[1] for array in saved[0]]
    rows = both(lambda size: row_block(size, phase))
    heads = both(
        lambda size: pl.BlockSpec(
            (None, size // HS, CROP, CROP), lambda i, live: (i, phase, 0, 0)
        )
    )
    flat = both(lambda size: fixed(width, size, phase))
    queries, keys, values, weights, attended, inverses = saved
    joined = 3 * sum(widths)
    if split:
        packed_specs = (fixed(width, joined // 2, phase % 2),) * 2
        packed_shapes = (shaped((width, joined)),) * 2
    else:
        packed_specs = (fixed(width, joined),)
        packed_shapes = (shaped((width, joined)),)
    operands = (
        live,
        normed,
        queries,
        keys,
        values,
        weights,
        inverses,
        attended,
        attended_grads,
        matrices,
    )
    before = len(jax.tree.leaves(operands))
    carried = len(jax.tree.leaves(previous))
    aliases = {before + i: i for i in range(carried)}
    for i in range(len(packed_before)):
        aliases[before + carried + i] = 6 + i
    untouched = lambda arrays: jax.tree.map(lambda _: pl.BlockSpec(memory_space=pl.ANY), arrays)
    return run(
        partial(attend_back_kernel, crops, split),
        "attend_back",
        crops,
        (row_block(width), rows, rows, rows, heads, rows, rows, rows, (flat,) * 3)
        + (untouched(previous), untouched(packed_before)),
        (
            (rows,) * 3,
            packed_specs,
            both(lambda size: fixed(8, size)),
            fixed(width, HS),
            fixed(8, width),
        ),
        (
            (tuple(shaped((count, size)) for size in units),) * 3,
            packed_shapes,
            both(lambda size: shaped((8, size), jnp.float32)),
            shaped((width, HS), jnp.float32),
            shaped((8, width), jnp.float32),
        ),
        2 * count * sum(widths) * (3 * width + 4 * CROP),
        count * (sum(widths) * (18 + 2 * CROP // HS) + 2 * width),
        (
            pltpu.VMEM((CROP, joined), jnp.bfloat16),
            pltpu.VMEM((width, joined), jnp.float32),
        ),
        aliases,
    )(*operands, previous, packed_before)


def latents_back(live, latents, hidden_grad, grads, matrices, gain, first, crops, previous):
    count, width = latents.shape
    block = lambda size: pl.BlockSpec((CROP, size), lambda i, live: (i + first, 0))
    rows = tuple(tuple(block(array.shape[1]) for array in kind) for kind in grads)
    flat = tuple(tuple(fixed(*array.shape) for array in kind) for kind in matrices)
    operands = (live, latents, hidden_grad, grads, matrices, gain)
    before = len(jax.tree.leaves(operands))
    return run(
        partial(latents_kernel, first),
        "latents_back",
        crops,
        (block(width), block(width), rows, flat, fixed(1, width))
        + (tuple(pl.BlockSpec(memory_space=pl.ANY) for _ in previous),),
        block(width),
        shaped((count, width), jnp.float32),
        2 * crops * CROP * width * width * 3,
        crops * CROP * width * 16,
        (),
        {before + i: i for i in range(len(previous))},
    )(*operands, previous)


def place_pieces(kernel, name, places, operands, out_shape):
    return pl.pallas_call(
        kernel,
        name=name,
        out_shape=out_shape,
        grid_spec=pltpu.PrefetchScalarGridSpec(
            num_scalar_prefetch=1,
            grid=(1,),
            in_specs=jax.tree.map(
                lambda array: pl.BlockSpec(array.shape, lambda i, places: (0, 0)), operands
            ),
            out_specs=jax.tree.map(
                lambda array: pl.BlockSpec(array.shape, lambda i, places: (0, 0)), out_shape
            ),
        ),
        compiler_params=pltpu.CompilerParams(
            dimension_semantics=("arbitrary",), vmem_limit_bytes=VMEM_LIMIT
        ),
    )(places, *operands)


def pair_perm(size, bit):
    return [(i, i ^ bit) for i in range(size)]


def after(value, *needed):
    return lax.optimization_barrier((value, needed))[0]


class Links:
    def __init__(self):
        self.wide = lax.axis_size("wide")
        self.narrow = lax.axis_size("narrow")
        self.paired = self.narrow == 2 and self.wide == 16
        self.index = lax.axis_index("wide")
        self.core = self.index % 2
        self.across = (self.index // 2) % 2
        self.along = self.index // 4
        self.token = ()
        self.sent = ()

    def slot(self, token):
        self.token = token
        self.sent = ()

    def swap(self, array, bit):
        return lax.ppermute(array, "wide", pair_perm(self.wide, bit))

    def swap_narrow(self, array):
        return lax.ppermute(array, "narrow", [(0, 1), (1, 0)])

    def others(self, weight, axis):
        whole = lax.all_gather(weight, "narrow", axis=0, tiled=False)
        whole = jnp.roll(whole, -lax.axis_index("narrow"), axis=0)[1:]
        return jnp.concatenate([whole[i] for i in range(self.narrow - 1)], axis=axis)

    def joined(self, near, far, index, count, side=None):
        rows = near.shape[0] // count
        columns = slice(None)
        if side is not None:
            width = near.shape[1] // 2
            columns = slice(side * width, (side + 1) * width)
        near, far = (array[index * rows : (index + 1) * rows, columns] for array in (near, far))
        return jnp.concatenate(
            [jnp.where(self.core == 0, near, far), jnp.where(self.core == 0, far, near)], axis=0
        )

    def places(self):
        return jnp.stack(
            [
                (self.core ^ core) * 8 + (self.across ^ across) * 4 + (self.along ^ along)
                for core in range(2)
                for across in range(2)
                for along in (0, 2, 1, 3)
            ]
        ).astype(jnp.int32)

    def reduce_plain(self, own, other, axis):
        width = own.shape[axis]
        parts = jnp.stack(
            [own]
            + [
                lax.slice_in_dim(other, i * width, (i + 1) * width, axis=axis)
                for i in range(self.narrow - 1)
            ]
        )
        parts = jnp.roll(parts, lax.axis_index("narrow"), axis=0)
        mine = lax.psum_scatter(parts, "narrow", scatter_dimension=0, tiled=True)[0]
        return lax.psum(mine, "wide").astype(jnp.float32)


def total(terms, size):
    parts = [
        lax.dynamic_slice_in_dim(array, start, size, 0).astype(jnp.float32)
        for array, start in terms
    ]
    return sum(parts[1:], parts[0]).astype(jnp.bfloat16)


def moved(terms, rows):
    return [(array, start + rows) for array, start in terms]


class Exchange:
    def __init__(self, links):
        self.links = links

    def waiting(self, terms):
        return [(after(array, self.links.token), start) for array, start in terms]

    def exchange(self, arrays, *sends):
        arrays = tuple(after(array, self.links.token) for array in arrays)
        self.links.sent += arrays
        return tuple(send(array) for send, array in zip(sends, arrays))


class Reduction(Exchange):
    def __init__(self, links, keep, give):
        super().__init__(links)
        self.rows = keep.shape[0] // 2
        self.own = [(keep, 0)]
        self.other = [(keep, self.rows)]
        self.give = give

    def cores(self):
        (got,) = self.exchange([self.give], lambda array: self.links.swap(array, 1))
        self.own += [(got, 0)]
        self.other += [(got, self.rows)]

    def narrows(self):
        give = total(self.waiting(self.other), self.rows)
        (got,) = self.exchange([give], self.links.swap_narrow)
        self.own += [(got, 0)]
        self.other = []
        self.got = got

    def acrosses(self):
        size = self.rows // 2
        across = self.links.across
        parts = [self.waiting(terms) for terms in (self.own, self.other) if terms]
        gives = [total(moved(terms, (1 - across) * size), size) for terms in parts]
        give = jnp.concatenate(gives, axis=0) if len(gives) > 1 else gives[0]
        (got,) = self.exchange([give], lambda array: self.links.swap(array, 2))
        self.own = moved(self.own, across * size) + [(got, 0)]
        if self.other:
            self.other = moved(self.other, across * size) + [(got, size)]
        self.rows = size
        self.got = got


class Ending(Exchange):
    def __init__(self, links, groups):
        super().__init__(links)
        self.groups = groups
        self.swaps = [
            lambda array: links.swap(array, 4),
            lambda array: links.swap(array, 8),
            lambda array: links.swap(array, 12),
        ]

    def alongs(self):
        size = self.groups[0].rows // 4
        for group in self.groups:
            group.own = self.waiting(group.own)
        terms = lambda group, bit: moved(group.own, (self.links.along ^ bit) * size)
        gives = [
            jnp.concatenate([total(terms(group, bit), size) for group in self.groups], axis=1)
            for bit in range(1, 4)
        ]
        got = self.exchange(gives, *self.swaps)
        self.parts = [terms(group, 0) for group in self.groups]
        self.size = size
        self.got = got

    def piece(self):
        got = [after(array, self.links.token) for array in self.got]
        pieces = []
        column = 0
        for terms in self.parts:
            width = terms[0][0].shape[1]
            mine = [
                (lax.slice_in_dim(array, column, column + width, axis=1), 0) for array in got
            ]
            pieces.append(total(self.waiting(terms) + mine, self.size))
            column += width
        return jnp.concatenate(pieces, axis=1)

    def along_back(self):
        piece = self.piece()
        self.got = self.exchange([piece] * 3, *self.swaps)
        near, far, opposite = self.got
        self.column = (piece, far, near, opposite)

    def far_back(self):
        piece = self.piece()
        self.got = self.exchange([piece], self.swaps[1])
        self.column = (piece, *self.got)

    def near_back(self):
        column = self.whole_column()
        self.got = self.exchange([column], self.swaps[0])
        self.columns = (column, *self.got)

    def whole_column(self):
        return jnp.concatenate([after(array, self.links.token) for array in self.column], axis=0)

    def across_back(self, columns=None):
        columns = columns or (self.whole_column(),)
        self.got = self.exchange(columns, *(len(columns) * (lambda array: self.links.swap(array, 2),)))
        return (*columns, *self.got)

    def core_back(self, columns):
        swap = lambda array: self.links.swap(array, 1)
        got = self.exchange(columns, *(len(columns) * (swap,)))
        self.result = (*columns, *got)


class SmallSum(Exchange):
    def __init__(self, links, rows):
        super().__init__(links)
        self.rows = rows
        self.left = [
            lambda rows: links.swap(rows, 2),
            lambda rows: links.swap(rows, 1),
            links.swap_narrow,
            lambda rows: links.swap(rows, 4),
            lambda rows: links.swap(rows, 8),
        ]

    def step(self):
        (got,) = self.exchange([self.rows], self.left.pop(0))
        self.rows = self.rows + got


def on_device(
    latents,
    cotangent,
    crop_counts,
    image_device,
    query_weight,
    key_weight,
    value_weight,
    out_weight,
    up_weight,
    down_weight,
    query_bias,
    value_bias,
    up_bias,
    out_bias,
    down_bias,
    first_gain,
    first_shift,
    second_gain,
    second_shift,
):
    links = Links()
    paired = links.paired
    count = latents.shape[0]
    crops = count // CROP
    width = latents.shape[1]
    narrow = links.narrow
    place = lax.axis_index("narrow")
    owned = jnp.sum(jnp.where(image_device == lax.axis_index("wide"), crop_counts, 0))
    live = jnp.stack([owned - place * crops, links.core]).astype(jnp.int32)
    units = query_weight.shape[1]
    biases = jnp.stack([query_bias, value_bias, up_bias])
    if paired:
        rest_biases = links.swap_narrow(biases)
    else:
        rest_biases = lax.all_gather(biases, "narrow", axis=0)
        rest_biases = jnp.roll(rest_biases, -place, axis=0).transpose(1, 0, 2).reshape(3, -1)
        rest_biases = rest_biases[:, units:]
    vector = lambda array: array.reshape(1, -1)
    bias_pair = lambda own, row: (
        vector(own).astype(jnp.float32),
        rest_biases[row : row + 1].astype(jnp.float32),
    )
    query_biases = bias_pair(query_bias, 0)
    value_biases = bias_pair(value_bias, 1)
    up_biases = bias_pair(up_bias, 2)
    norm = (vector(first_gain), vector(first_shift))
    own_weights = (query_weight, key_weight, value_weight)
    if paired:
        half = lambda weight: lax.dynamic_slice_in_dim(
            weight, links.core * (weight.shape[0] // 2), weight.shape[0] // 2, 0
        )
        attend_half = jnp.concatenate([half(weight) for weight in own_weights], axis=0)
        attend_near = links.swap_narrow(attend_half)
    first, *saved_own = attend(
        after(live, attend_half) if paired else live,
        latents,
        norm,
        own_weights,
        (query_biases[0], value_biases[0]),
    )
    if paired:
        up_half = half(after(up_weight, first))
        rows = up_half.shape[0] // 2
        feed_half = jnp.concatenate(
            [
                half(after(out_weight, first)),
                half(after(down_weight, first)),
                jnp.concatenate([up_half[:rows], up_half[rows:]], axis=1),
            ],
            axis=0,
        )
        feed_near = links.swap_narrow(feed_half)
        attend_far = links.swap(after(attend_near, first), 1)
        rest_weights = tuple(links.joined(attend_near, attend_far, i, 3) for i in range(3))
    else:
        rest_weights = tuple(links.others(weight, 1) for weight in own_weights)
    saved_rest = attend(
        after(live, feed_half) if paired else live,
        first,
        None,
        rest_weights,
        (query_biases[1], value_biases[1]),
    )
    if paired:
        feed_near = after(feed_near, saved_rest[0])
        feed_far = links.swap(feed_near, 1)
        rest_out, rest_down = (links.joined(feed_near, feed_far, i, 3) for i in range(2))
        sides = [links.joined(feed_near, feed_far, 2, 3, side) for side in range(2)]
        rest_up = jnp.concatenate(
            [side[start : start + rows] for start in (0, rows) for side in sides], axis=0
        )
    else:
        rest_out = links.others(out_weight, 0)
        rest_up = links.others(up_weight, 1)
        rest_down = links.others(down_weight, 0)
    matrices = tuple(zip(own_weights, rest_weights))
    outs = (out_weight, rest_out)
    ups = (up_weight, rest_up)
    downs = (down_weight, rest_down)
    saved = tuple(zip(saved_own, saved_rest))
    (
        block_output,
        hidden_grad,
        attended_grads,
        feed_packed,
        up_bias_grads,
        feed_vectors,
    ) = feed(
        live,
        latents,
        cotangent,
        saved[4],
        outs,
        ups,
        downs,
        up_biases,
        [vector(array) for array in (out_bias, down_bias, second_gain, second_shift)],
        paired,
    )

    def back(live, phase, widths, previous, packed_before):
        return attend_back(
            live,
            first,
            saved,
            attended_grads,
            matrices,
            widths,
            phase,
            previous,
            packed_before,
            paired,
        )

    def latents_step(live, grads, start, size, previous):
        return latents_back(
            live, latents, hidden_grad, grads, matrices, norm[0], start, size, previous
        )

    if paired:
        phases = units // HS
        widths = (HS, (width - units) // phases)
        ready = lambda: after(live, links.sent)
        tall, flat = (Reduction(links, keep, give) for keep, give in zip(*feed_packed))
        links.slot(feed_vectors)
        tall.cores()
        flat.cores()
        a = back(ready(), 0, widths, (), ())
        links.slot(a[3])
        tall.narrows()
        flat.acrosses()
        b = back(ready(), 1, widths, a[0], a[1])
        early = Reduction(links, *b[1])
        links.slot(b[3])
        flat.narrows()
        early.cores()
        c = back(ready(), 2, widths, b[0], ())
        links.slot(c[3])
        tall.acrosses()
        early.narrows()
        d = back(ready(), 3, widths, c[0], c[1])
        late = Reduction(links, *d[1])
        rows = place_pieces(
            rows_kernel,
            "vector_rows",
            place.astype(jnp.int32).reshape(1),
            (
                tuple(step[3] for step in (a, b, c, d)),
                tuple(step[4] for step in (a, b, c, d)),
                tuple(step[2] for step in (a, b, c, d)),
                feed_vectors,
                up_bias_grads,
                *norm,
            ),
            shaped((16, width), jnp.float32),
        )
        feeds = Ending(links, (tall, flat))
        earlies = Ending(links, (early,))
        lates = Ending(links, (late,))
        small = SmallSum(links, rows)
        top = crops // 2
        links.slot(d[3])
        feeds.alongs()
        early.acrosses()
        late.cores()
        upper = latents_step(ready(), d[0], 0, top, ())
        links.slot(upper)
        feeds.far_back()
        earlies.alongs()
        late.narrows()
        latents_gradient = latents_step(ready(), d[0], top, crops - top, (upper,))
        places = links.places()
        links.slot((latents_gradient, feeds.got, earlies.got))
        late.acrosses()
        feeds.near_back()
        earlies.far_back()
        small.step()
        links.slot((late.got, feeds.got, earlies.got, small.rows, places))
        lates.alongs()
        near_column, far_column = feeds.columns
        near_columns = feeds.across_back((near_column,))
        earlies.near_back()
        links.slot((lates.got, earlies.got, feeds.got))
        lates.along_back()
        far_columns = feeds.across_back((far_column,))
        early_columns = earlies.across_back((jnp.concatenate(earlies.columns, axis=0),))
        small.step()
        links.slot((lates.got, feeds.got, small.rows))
        late_columns = lates.across_back()
        feeds.core_back(
            tuple(column for pair in zip(near_columns, far_columns) for column in pair)
        )
        small.step()
        small.step()
        square = (
            shaped((width, units), jnp.float32),
            shaped((units, width), jnp.float32),
        )
        down_grad, out_grad, up_grad = place_pieces(
            finish_feed_kernel,
            "feed_places",
            places,
            (feeds.result,),
            (square[1], square[1], square[0]),
        )
        links.slot((lates.got, small.rows, up_grad))
        lates.core_back(late_columns)
        earlies.core_back(early_columns)
        small.step()
        rowwise = small.rows
        attend_matrix_grads = place_pieces(
            finish_kernel,
            "attend_places",
            places,
            ((earlies.result, lates.result),),
            (square[0],) * 3,
        )
    else:
        widths = (units, width - units)
        step = back(live, 0, widths, (), ())
        latents_gradient = latents_step(live, step[0], 0, crops, ())
        together = lambda own, rest: jnp.roll(
            jnp.concatenate([own, rest]).reshape(narrow, units), place, axis=0
        ).reshape(-1)
        shift_grad = step[4].sum(axis=0)
        rows = jnp.stack(
            [
                (step[3].sum(axis=1) - first_shift * shift_grad) / first_gain,
                shift_grad,
                *(feed_vectors[row] for row in range(4)),
                together(step[2][0][0], step[2][1][0]),
                together(step[2][0][2], step[2][1][2]),
                together(up_bias_grads[0][0], up_bias_grads[1][0]),
            ]
        )
        rowwise = lax.psum(rows, ("wide", "narrow"))
        joined = step[1][0]
        attend_matrix_grads = tuple(
            links.reduce_plain(
                joined[:, kind * units : (kind + 1) * units],
                lax.slice_in_dim(
                    joined,
                    3 * units + kind * widths[1],
                    3 * units + (kind + 1) * widths[1],
                    axis=1,
                ),
                1,
            )
            for kind in range(3)
        )
        down_grad, out_grad, up_grad = (
            links.reduce_plain(*grads, axis) for grads, axis in zip(feed_packed, (0, 0, 1))
        )
    own = lax.dynamic_slice_in_dim(rowwise[6:9], place * units, units, 1)
    return (
        block_output,
        latents_gradient,
        *attend_matrix_grads,
        out_grad,
        up_grad,
        down_grad,
        own[0],
        own[1],
        own[2],
        rowwise[4],
        rowwise[5],
        rowwise[0],
        rowwise[1],
        rowwise[2],
        rowwise[3],
    )


def solution(mesh):
    rows = P(("wide", "narrow"), None)
    columns = P(None, "narrow")
    units = P("narrow", None)
    vector = P("narrow")
    whole = P()
    return jax.shard_map(
        on_device,
        mesh=mesh,
        in_specs=(
            rows,
            rows,
            whole,
            whole,
            columns,
            columns,
            columns,
            units,
            columns,
            units,
            vector,
            vector,
            vector,
            whole,
            whole,
            whole,
            whole,
            whole,
            whole,
        ),
        out_specs=(
            rows,
            rows,
            columns,
            columns,
            columns,
            units,
            columns,
            units,
            vector,
            vector,
            vector,
            whole,
            whole,
            whole,
            whole,
            whole,
            whole,
        ),
        check_vma=False,
    )
```

time: 469 us -> 369 us (0.79)
  waiting for transfers between devices: 151 us -> 70.3 us
  Pallas kernels: 177 us -> 145 us
  starting transfers between devices: 67.7 us -> 88.3 us
  local copies, waits for them, and re-layouts: 30.4 us -> 10.8 us
  other arithmetic: 31.5 us -> 45.5 us
    ppermute x14 -> x8, waiting for transfers between devices: 96.2 us -> 44.2 us  [swap_narrow(): return lax.ppermute(array, 'narrow', [(0, 1), (1, 0)])]
    ppermute x64 -> x42, waiting for transfers between devices: 55.1 us -> 26.1 us  [swap(): return lax.ppermute(array, 'wide', pair_perm(self.wide, bit))]
    ppermute x64 -> x42, starting transfers between devices: 55.4 us -> 81.3 us  [swap(): return lax.ppermute(array, 'wide', pair_perm(self.wide, bit))]
    pallas_call x4 -> x10, Pallas kernels: 138 us -> 116 us  [the longest x4 51.6 us: attend_back(): run(partial(attend_back_kernel, crops, split), 'attend_back', crops, (row...]
    dynamic_slice x36 -> x4, local copies, waits for them, and re-layouts: 19.9 us -> 4.51 us  [on_device(): lax.dynamic_slice_in_dim(weight, links.core * (weight.shape[0] // 2), wei...]
    convert_element_type x37 -> x19, other arithmetic: 16.4 us -> 27.6 us  [the longest x16 25.8 us: total(): return sum(parts[1:], parts[0]).astype(jnp.bfloat16)]
    pallas_call x2, Pallas kernels: 38.6 us -> 28.8 us  [attend(): run(partial(attend_kernel, first), 'attend_first' if first else 'attend_r...]
    concatenate x22 -> x14, other arithmetic: 5.44 us -> 11.8 us  [the longest x5 5.26 us: joined(): jnp.concatenate([jnp.where(self.core == 0, near, far), jnp.where(self.cor...]
  transfers between devices with their start and end apart: 78 -> 50, of which waited for: 36 -> 18; matrix products, arithmetic and copies ran while one was open for 10% -> 13% of each run, Pallas kernels for 10% -> 30%
where the time goes in v3:
time: 369 us; the launch traced here: 362 us
  Pallas kernels  145 us (39%)
  starting transfers between devices  88.3 us (24%)
  waiting for transfers between devices  70.3 us (19%)
  other arithmetic  45.5 us (12%)
  local copies, waits for them, and re-layouts  10.8 us (3%)
    ppermute x42, starting transfers between devices, swap(): return lax.ppermute(array, 'wide', pair_perm(self.wide, bit))  81.3 us
    pallas_call x4, Pallas kernels, attend_back(): run(partial(attend_back_kernel, crops, split), 'attend_back', crops, (row...  51.6 us
    ppermute x8, waiting for transfers between devices, swap_narrow(): return lax.ppermute(array, 'narrow', [(0, 1), (1, 0)])  44.2 us
    pallas_call x1, Pallas kernels, feed(): run(partial(feed_kernel, crops, split), 'feed', crops, (row_block(width),...  29.4 us
    pallas_call x2, Pallas kernels, attend(): run(partial(attend_kernel, first), 'attend_first' if first else 'attend_r...  28.8 us
    ppermute x42, waiting for transfers between devices, swap(): return lax.ppermute(array, 'wide', pair_perm(self.wide, bit))  26.1 us
    convert_element_type x16, other arithmetic, total(): return sum(parts[1:], parts[0]).astype(jnp.bfloat16)  25.8 us
    pallas_call x2, Pallas kernels, latents_back(): run(partial(latents_kernel, first), 'latents_back', crops, (block(width),...  21.1 us
  transfers between devices with their start and end apart: 50, of which 18 were waited for; matrix products, arithmetic and copies ran while one was open for 13% of the time, Pallas kernels for 30%

profile of v3, /device:TPU:0, one launch (start us, length us, event | category | flops | bytes accessed | tf_op | source)
XLA Modules:
  0.0 362.0 jit_solution(9066726267144094272)
XLA Ops:
  4.3 3.0 collective-permute-start
  9.9 15.4 %attend_first.1 = (bf16[2048,1024]{1,0:T(8,128)(2,1)}, bf16[2048,512]{1,0:T(8,128)(2,1)}, bf16[2048,512]{1,0:T(8,128)(2,1)}, bf16[2048,512]{1,0:T(8,128)(2,1)}, ...) custom-call(s32[2]{0:T(128)} %pad_add_fusion.live_ref, ...), custom_call_target="tpu_custom_call" | custom-call | flops 68719476736 | bytes 234881024 | tf_op jit(solution)/shard_map/attend_first/pallas_call | solution.py:428
  25.2 16.8 %collective-permute-done = bf16[1536,512]{1,0:T(8,128)(2,1)} collective-permute-done((bf16[1536,512]{1,0:T(8,128)(2,1)}, bf16[1536,512]{1,0:T(8,128)(2,1)}, u32[]{:S(2)}, u32[]{:S(2)}) %collective-permute-start) | collective-permute-done | bytes 1572896 | tf_op jit(solution)/shard_map/ppermute | solution.py:627
  53.0 13.4 %attend_rest.1 = (bf16[2048,512]{1,0:T(8,128)(2,1)}, bf16[2048,512]{1,0:T(8,128)(2,1)}, bf16[2048,512]{1,0:T(8,128)(2,1)}, bf16[4,4,512,512]{3,2,1,0:T(8,128)(2,...) custom-call(s32[2]{0:T(128)} %pad_add_fusion.live_ref, bf16[2048,1024]{1,0:T(8,128)(2,1)} %get-tuple-element.222.source_ref.normed_ref, ...), custom_call_target="tpu_custom_call" | custom-call | flops 68719476736 | bytes 234881024 | tf_op jit(solution)/shard_map/attend_rest/pallas_call | solution.py:428
  66.4 17.8 %collective-permute-done.3 = bf16[768,1024]{1,0:T(8,128)(2,1)} collective-permute-done((bf16[768,1024]{1,0:T(8,128)(2,1)}, bf16[768,1024]{1,0:T(8,128)(2,1)}, u32[]{:S(2)}, u32[]{:S(2)}) %collective-permute-start.3) | collective-permute-done | bytes 1572896 | tf_op jit(solution)/shard_map/ppermute | solution.py:627
  84.8 3.0 collective-permute-done.4
  93.5 29.4 %feed.1 = (bf16[2048,1024]{1,0:T(8,128)(2,1)}, f32[2048,1024]{1,0:T(8,128)}, bf16[2048,512]{1,0:T(8,128)(2,1)}, bf16[2048,512]{1,0:T(8,128)(2,1)}, bf16[1024,102...) custom-call(s32[2]{0:T(128)} %pad_add_fusion.live_ref, ...), custom_call_target="tpu_custom_call" | custom-call | flops 309237645312 | bytes 234881024 | tf_op jit(solution)/shard_map/feed/pallas_call | solution.py:465
  122.9 17.7 %collective-permute-start.5 = (bf16[1024,1024]{1,0:T(8,128)(2,1)}, bf16[1024,1024]{1,0:T(8,128)(2,1)}, u32[]{:S(2)}, u32[]{:S(2)}) collective-permute-start(bf16[1024,1024]{1,0:T(8,128)(2,1)} %get-tuple-element.236), channel_id=1, source_target_pairs={{0,2},{2,0},{4,6},{6,4},{8,10},{10,8},{12,14},{14,12},{16,18},{18,... | collective-permute-start | bytes 6291464 | tf_op jit(solution)/shard_map/ppermute | solution.py:624
  140.6 13.0 %attend_back.4 = (bf16[2048,512]{1,0:T(8,128)(2,1)}, bf16[2048,512]{1,0:T(8,128)(2,1)}, bf16[2048,512]{1,0:T(8,128)(2,1)}, bf16[2048,512]{1,0:T(8,128)(2,1)}, bf...) custom-call(s32[2]{0:T(128)} %pad_add_fusion.live_ref, ...), custom_call_target="tpu_custom_call" | custom-call | flops 42949672960 | bytes 142606336 | tf_op jit(solution)/shard_map/attend_back/pallas_call | solution.py:526
  155.9 15.7 %collective-permute-start.7 = (bf16[512,512]{1,0:T(8,128)(2,1)}, bf16[512,512]{1,0:T(8,128)(2,1)S(1)}, u32[]{:S(2)}, u32[]{:S(2)}) collective-permute-start(bf16[512,512]{1,0:T(8,128)(2,1)} %pad_maximum_fusion.7), channel_id=1, source_target_pairs={{0,4},{2,6},{4,0},{6,2},{8,12},{10,14},{12,8},{14,10},{16,20},{18,... | collective-permute-start | bytes 1572872 | tf_op jit(solution)/shard_map/ppermute | solution.py:624
  171.6 2.6 add_convert_fusion
  174.8 12.8 %attend_back.5 = (bf16[2048,512]{1,0:T(8,128)(2,1)}, bf16[2048,512]{1,0:T(8,128)(2,1)}, bf16[2048,512]{1,0:T(8,128)(2,1)}, bf16[2048,512]{1,0:T(8,128)(2,1)}, bf...) custom-call(s32[2]{0:T(128)} %pad_add_fusion.live_ref, ...), custom_call_target="tpu_custom_call", output_to_operand_aliasing={{0}: (22, {}), {1}: (23, {}), {2}: (24, {}), {3}: (25, {}),... | custom-call | flops 42949672960 | bytes 142606336 | tf_op jit(solution)/shard_map/attend_back/pallas_call | solution.py:526
  189.6 13.0 %attend_back.6 = (bf16[2048,512]{1,0:T(8,128)(2,1)}, bf16[2048,512]{1,0:T(8,128)(2,1)}, bf16[2048,512]{1,0:T(8,128)(2,1)}, bf16[2048,512]{1,0:T(8,128)(2,1)}, bf...) custom-call(s32[2]{0:T(128)} %pad_add_fusion.live_ref, ...), custom_call_target="tpu_custom_call", output_to_operand_aliasing={{0}: (22, {}), {1}: (23, {}), {2}: (24, {}), {3}: (25, {}),... | custom-call | flops 42949672960 | bytes 142606336 | tf_op jit(solution)/shard_map/attend_back/pallas_call | solution.py:526
  202.7 2.5 add_convert_fusion.3
  205.3 6.9 %collective-permute-start.10 = (bf16[256,1024]{1,0:T(8,128)(2,1)}, bf16[256,1024]{1,0:T(8,128)(2,1)}, u32[]{:S(2)}, u32[]{:S(2)}) collective-permute-start(bf16[256,1024]{1,0:T(8,128)(2,1)} %add_convert_fusion.3), channel_id=1, source_target_pairs={{0,4},{2,6},{4,0},{6,2},{8,12},{10,14},{12,8},{14,10},{16,20},{18,... | collective-permute-start | bytes 1572872 | tf_op jit(solution)/shard_map/ppermute | solution.py:624
  214.0 12.8 %attend_back.7 = (bf16[2048,512]{1,0:T(8,128)(2,1)}, bf16[2048,512]{1,0:T(8,128)(2,1)}, bf16[2048,512]{1,0:T(8,128)(2,1)}, bf16[2048,512]{1,0:T(8,128)(2,1)}, bf...) custom-call(s32[2]{0:T(128)} %pad_add_fusion.live_ref, ...), custom_call_target="tpu_custom_call", output_to_operand_aliasing={{0}: (22, {}), {1}: (23, {}), {2}: (24, {}), {3}: (25, {}),... | custom-call | flops 42949672960 | bytes 142606336 | tf_op jit(solution)/shard_map/attend_back/pallas_call | solution.py:526
  232.4 6.0 %collective-permute-start.14 = (bf16[64,1536]{1,0:T(8,128)(2,1)}, bf16[64,1536]{1,0:T(8,128)(2,1)}, u32[]{:S(2)}, u32[]{:S(2)}) collective-permute-start(bf16[64,1536]{1,0:T(8,128)(2,1)} %pad_maximum_fusion.9), channel_id=1, source_target_pairs={{0,16},{2,18},{4,20},{6,22},{8,24},{10,26},{12,28},{14,30},{16,0},... | collective-permute-start | bytes 589832 | tf_op jit(solution)/shard_map/ppermute | solution.py:624
  241.8 12.3 %latents_back.2.previous_0_ = f32[2048,1024]{1,0:T(8,128)} custom-call(s32[2]{0:T(128)} %pad_add_fusion.live_ref, bf16[2048,1024]{1,0:T(8,128)(2,1)} %latents_ref.5, f32[2048,1024]{1,0:T(8,128)} %get-tuple-element.318.hidden_grad_ref, bf16[2048,512]{1,0:T(8,128)(2,1)} %get-tuple-element.319.grads_0__0_, bf16[2048,512]{1,0:T(8,128)(2,1)} %get-tuple-element.320.grads_0__1_, ...), custom_call_target="tpu_custom_call" | custom-call | flops 51539607552 | bytes 134217728 | tf_op jit(solution)/shard_map/latents_back/pallas_call | solution.py:563
  256.7 5.5 %collective-permute-start.18 = (bf16[64,1536]{1,0:T(8,128)(2,1)S(1)}, bf16[64,1536]{1,0:T(8,128)(2,1)S(1)}, u32[]{:S(2)}, u32[]{:S(2)}) collective-permute-start(bf16[64,1536]{1,0:T(8,128)(2,1)S(1)} %pad_maximum_fusion.11), channel_id=1, source_target_pairs={{0,16},{2,18},{4,20},{6,22},{8,24},{10,26},{12,28},{14,30},{16,0},... | collective-permute-start | bytes 589832 | tf_op jit(solution)/shard_map/ppermute | solution.py:624
  268.2 2.2 add_convert_fusion.1
  270.9 8.8 %latents_back.3 = f32[2048,1024]{1,0:T(8,128)} custom-call(s32[2]{0:T(128)} %pad_add_fusion.live_ref, bf16[2048,1024]{1,0:T(8,128)(2,1)} %latents_ref.5, f32[2048,1024]{1,0:T(8,128)} %get-tuple-element.318.hidden_grad_ref, bf16[2048,512]{1,0:T(8,128)(2,1)} %get-tuple-element.319.grads_0__0_, ...), custom_call_target="tpu_custom_call", output_to_operand_aliasing={{}: (16, {})} | custom-call | flops 51539607552 | bytes 134217728 | tf_op jit(solution)/shard_map/latents_back/pallas_call | solution.py:563
  280.9 7.5 %collective-permute-done.22 = bf16[512,768]{1,0:T(8,128)(2,1)} collective-permute-done((bf16[512,768]{1,0:T(8,128)(2,1)}, bf16[512,768]{1,0:T(8,128)(2,1)}, u32[]{:S(2)}, u32[]{:S(2)}) %collective-permute-start.22) | collective-permute-done | bytes 786464 | tf_op jit(solution)/shard_map/ppermute | solution.py:627
  293.8 2.5 vector_rows.1
  297.0 3.9 %collective-permute-done.26 = f32[16,1024]{1,0:T(8,128)S(1)} collective-permute-done((f32[16,1024]{1,0:T(8,128)}, f32[16,1024]{1,0:T(8,128)S(1)}, u32[]{:S(2)}, u32[]{:S(2)}) %collective-permute-start.26) | collective-permute-done | bytes 65568 | tf_op jit(solution)/shard_map/ppermute | solution.py:624
  304.5 3.0 collective-permute-start.30
  309.0 2.9 collective-permute-done.30
  332.9 2.6 collective-permute-done.40
  339.2 5.6 %feed_places.1 = (f32[512,1024]{1,0:T(8,128)}, f32[512,1024]{1,0:T(8,128)}, f32[1024,512]{1,0:T(8,128)}) custom-call(s32[16]{0:T(128)} %stack.89.places_ref, bf16[128,1536]{1,0:T(8,128)(2,1)} %copy-done.3, bf16[128,1536]{1,0:T(8,128)(2,1)} %collective-permute-done.24.sources_1_, bf16[128,1536]{1,0:T(8,128)(2,1)} %copy-done.6, bf16[128,1536]{1,0:T(8,128)(2,1)} %copy-done.7, ...), custom_call_target="tpu_custom_call" | custom-call | tf_op jit(solution)/shard_map/feed_places/pallas_call | solution.py:579
  344.8 3.0 collective-permute-done.38.groups_1__1_
  347.8 2.2 collective-permute-start.49
  350.5 2.6 collective-permute-done.32.groups_0__1_
  355.7 5.8 %attend_places.1 = (f32[1024,512]{1,0:T(8,128)}, f32[1024,512]{1,0:T(8,128)}, f32[1024,512]{1,0:T(8,128)}) custom-call(s32[16]{0:T(128)} %stack.89.places_ref, bf16[256,768]{1,0:T(8,128)(2,1)} %copy-done.4, bf16[256,768]{1,0:T(8,128)(2,1)} %collective-permute-done.32.groups_0__1_, bf16[256,768]{1,0:T(8,128)(2,1)} %collective-permute-done.45.groups_0__2_, ...), custom_call_target="tpu_custom_call" | custom-call | tf_op jit(solution)/shard_map/attend_places/pallas_call | solution.py:579
  (183 shorter events, 87.6 us)
Async XLA Ops:
  4.3 37.7 %collective-permute-start = (bf16[1536,512]{1,0:T(8,128)(2,1)}, bf16[1536,512]{1,0:T(8,128)(2,1)}, u32[]{:S(2)}, u32[]{:S(2)}) collective-permute-start(bf16[1536,512]{1,0:T(8,128)(2,1)} %pad_maximum_fusion), channel_id=1, source_target_pairs={{0,1},{1,0},{2,3},{3,2},{4,5},{5,4},{6,7},{7,6},{8,9},{9,8},{10,11... | collective-permute-start | bytes 4718600 | tf_op jit(solution)/shard_map/ppermute | solution.py:627
  47.4 36.8 %collective-permute-start.3 = (bf16[768,1024]{1,0:T(8,128)(2,1)}, bf16[768,1024]{1,0:T(8,128)(2,1)}, u32[]{:S(2)}, u32[]{:S(2)}) collective-permute-start(bf16[768,1024]{1,0:T(8,128)(2,1)} %maximum_maximum_fusion), channel_id=1, source_target_pairs={{0,1},{1,0},{2,3},{3,2},{4,5},{5,4},{6,7},{7,6},{8,9},{9,8},{10,11... | collective-permute-start | bytes 4718600 | tf_op jit(solution)/shard_map/ppermute | solution.py:627
  122.9 48.8 %collective-permute-start.5 = (bf16[1024,1024]{1,0:T(8,128)(2,1)}, bf16[1024,1024]{1,0:T(8,128)(2,1)}, u32[]{:S(2)}, u32[]{:S(2)}) collective-permute-start(bf16[1024,1024]{1,0:T(8,128)(2,1)} %get-tuple-element.236), channel_id=1, source_target_pairs={{0,2},{2,0},{4,6},{6,4},{8,10},{10,8},{12,14},{14,12},{16,18},{18,... | collective-permute-start | bytes 6291464 | tf_op jit(solution)/shard_map/ppermute | solution.py:624
  140.5 13.1 %collective-permute-start.6 = (bf16[1024,512]{1,0:T(8,128)(2,1)}, bf16[1024,512]{1,0:T(8,128)(2,1)}, u32[]{:S(2)}, u32[]{:S(2)}) collective-permute-start(bf16[1024,512]{1,0:T(8,128)(2,1)} %get-tuple-element.238), channel_id=1, source_target_pairs={{0,2},{2,0},{4,6},{6,4},{8,10},{10,8},{12,14},{14,12},{16,18},{18,... | collective-permute-start | bytes 3145736 | tf_op jit(solution)/shard_map/ppermute | solution.py:624
  155.9 31.6 %collective-permute-start.7 = (bf16[512,512]{1,0:T(8,128)(2,1)}, bf16[512,512]{1,0:T(8,128)(2,1)S(1)}, u32[]{:S(2)}, u32[]{:S(2)}) collective-permute-start(bf16[512,512]{1,0:T(8,128)(2,1)} %pad_maximum_fusion.7), channel_id=1, source_target_pairs={{0,4},{2,6},{4,0},{6,2},{8,12},{10,14},{12,8},{14,10},{16,20},{18,... | collective-permute-start | bytes 1572872 | tf_op jit(solution)/shard_map/ppermute | solution.py:624
  174.3 28.4 %collective-permute-start.8 = (bf16[512,1024]{1,0:T(8,128)(2,1)}, bf16[512,1024]{1,0:T(8,128)(2,1)}, u32[]{:S(2)}, u32[]{:S(2)}) collective-permute-start(bf16[512,1024]{1,0:T(8,128)(2,1)} %add_convert_fusion), channel_id=1, source_target_pairs={{0,1},{1,0},{2,3},{3,2},{4,5},{5,4},{6,7},{7,6},{8,9},{9,8},{10,11... | collective-permute-start | bytes 3145736 | tf_op jit(solution)/shard_map/ppermute | solution.py:627
  189.6 22.5 %collective-permute-start.9 = (bf16[1024,768]{1,0:T(8,128)(2,1)}, bf16[1024,768]{1,0:T(8,128)(2,1)}, u32[]{:S(2)}, u32[]{:S(2)}) collective-permute-start(bf16[1024,768]{1,0:T(8,128)(2,1)} %get-tuple-element.273), channel_id=1, source_target_pairs={{0,2},{2,0},{4,6},{6,4},{8,10},{10,8},{12,14},{14,12},{16,18},{18,... | collective-permute-start | bytes 4718600 | tf_op jit(solution)/shard_map/ppermute | solution.py:624
  189.6 37.2 %collective-permute-start.11 = (bf16[256,512]{1,0:T(8,128)(2,1)}, bf16[256,512]{1,0:T(8,128)(2,1)}, u32[]{:S(2)}, u32[]{:S(2)}) collective-permute-start(bf16[256,512]{1,0:T(8,128)(2,1)} %add_convert_fusion.6), channel_id=1, source_target_pairs={{0,1},{1,0},{2,3},{3,2},{4,5},{5,4},{6,7},{7,6},{8,9},{9,8},{10,11... | collective-permute-start | bytes 786440 | tf_op jit(solution)/shard_map/ppermute | solution.py:627
  205.3 21.6 %collective-permute-start.10 = (bf16[256,1024]{1,0:T(8,128)(2,1)}, bf16[256,1024]{1,0:T(8,128)(2,1)}, u32[]{:S(2)}, u32[]{:S(2)}) collective-permute-start(bf16[256,1024]{1,0:T(8,128)(2,1)} %add_convert_fusion.3), channel_id=1, source_target_pairs={{0,4},{2,6},{4,0},{6,2},{8,12},{10,14},{12,8},{14,10},{16,20},{18,... | collective-permute-start | bytes 1572872 | tf_op jit(solution)/shard_map/ppermute | solution.py:624
  213.5 25.0 %collective-permute-start.12 = (bf16[512,768]{1,0:T(8,128)(2,1)S(1)}, bf16[512,768]{1,0:T(8,128)(2,1)}, u32[]{:S(2)}, u32[]{:S(2)}) collective-permute-start(bf16[512,768]{1,0:T(8,128)(2,1)S(1)} %add_convert_fusion.2), channel_id=1, source_target_pairs={{0,1},{1,0},{2,3},{3,2},{4,5},{5,4},{6,7},{7,6},{8,9},{9,8},{10,11... | collective-permute-start | bytes 2359304 | tf_op jit(solution)/shard_map/ppermute | solution.py:627
  232.0 36.2 %collective-permute-start.17 = (bf16[1024,768]{1,0:T(8,128)(2,1)}, bf16[1024,768]{1,0:T(8,128)(2,1)}, u32[]{:S(2)}, u32[]{:S(2)}) collective-permute-start(bf16[1024,768]{1,0:T(8,128)(2,1)} %get-tuple-element.316), channel_id=1, source_target_pairs={{0,2},{2,0},{4,6},{6,4},{8,10},{10,8},{12,14},{14,12},{16,18},{18,... | collective-permute-start | bytes 4718600 | tf_op jit(solution)/shard_map/ppermute | solution.py:624
  232.0 22.2 %collective-permute-start.13 = (bf16[64,1536]{1,0:T(8,128)(2,1)}, bf16[64,1536]{1,0:T(8,128)(2,1)S(1)}, u32[]{:S(2)}, u32[]{:S(2)}) collective-permute-start(bf16[64,1536]{1,0:T(8,128)(2,1)} %pad_maximum_fusion.8), channel_id=1, source_target_pairs={{0,8},{2,10},{4,12},{6,14},{8,0},{10,2},{12,4},{14,6},{16,24},{18,... | collective-permute-start | bytes 589832 | tf_op jit(solution)/shard_map/ppermute | solution.py:624
  232.4 21.8 %collective-permute-start.14 = (bf16[64,1536]{1,0:T(8,128)(2,1)}, bf16[64,1536]{1,0:T(8,128)(2,1)}, u32[]{:S(2)}, u32[]{:S(2)}) collective-permute-start(bf16[64,1536]{1,0:T(8,128)(2,1)} %pad_maximum_fusion.9), channel_id=1, source_target_pairs={{0,16},{2,18},{4,20},{6,22},{8,24},{10,26},{12,28},{14,30},{16,0},... | collective-permute-start | bytes 589832 | tf_op jit(solution)/shard_map/ppermute | solution.py:624
  238.4 15.8 %collective-permute-start.15 = (bf16[64,1536]{1,0:T(8,128)(2,1)}, bf16[64,1536]{1,0:T(8,128)(2,1)}, u32[]{:S(2)}, u32[]{:S(2)}) collective-permute-start(bf16[64,1536]{1,0:T(8,128)(2,1)} %pad_maximum_fusion.10), channel_id=1, source_target_pairs={{0,24},{2,26},{4,28},{6,30},{8,16},{10,18},{12,20},{14,22},{16,8},... | collective-permute-start | bytes 589832 | tf_op jit(solution)/shard_map/ppermute | solution.py:624
  239.9 22.4 %collective-permute-start.16 = (bf16[256,768]{1,0:T(8,128)(2,1)S(1)}, bf16[256,768]{1,0:T(8,128)(2,1)}, u32[]{:S(2)}, u32[]{:S(2)}) collective-permute-start(bf16[256,768]{1,0:T(8,128)(2,1)S(1)} %add_convert_fusion.5), channel_id=1, source_target_pairs={{0,4},{2,6},{4,0},{6,2},{8,12},{10,14},{12,8},{14,10},{16,20},{18,... | collective-permute-start | bytes 1179656 | tf_op jit(solution)/shard_map/ppermute | solution.py:624
  256.7 22.9 %collective-permute-start.18 = (bf16[64,1536]{1,0:T(8,128)(2,1)S(1)}, bf16[64,1536]{1,0:T(8,128)(2,1)S(1)}, u32[]{:S(2)}, u32[]{:S(2)}) collective-permute-start(bf16[64,1536]{1,0:T(8,128)(2,1)S(1)} %pad_maximum_fusion.11), channel_id=1, source_target_pairs={{0,16},{2,18},{4,20},{6,22},{8,24},{10,26},{12,28},{14,30},{16,0},... | collective-permute-start | bytes 589832 | tf_op jit(solution)/shard_map/ppermute | solution.py:624
  263.7 15.9 %collective-permute-start.21 = (bf16[64,768]{1,0:T(8,128)(2,1)S(1)}, bf16[64,768]{1,0:T(8,128)(2,1)S(1)}, u32[]{:S(2)}, u32[]{:S(2)}) collective-permute-start(bf16[64,768]{1,0:T(8,128)(2,1)S(1)} %get-tuple-element.343), channel_id=1, source_target_pairs={{0,24},{2,26},{4,28},{6,30},{8,16},{10,18},{12,20},{14,22},{16,8},... | collective-permute-start | bytes 294920 | tf_op jit(solution)/shard_map/ppermute | solution.py:624
  265.7 14.6 %collective-permute-start.20 = (bf16[64,768]{1,0:T(8,128)(2,1)S(1)}, bf16[64,768]{1,0:T(8,128)(2,1)S(1)}, u32[]{:S(2)}, u32[]{:S(2)}) collective-permute-start(bf16[64,768]{1,0:T(8,128)(2,1)S(1)} %get-tuple-element.342), channel_id=1, source_target_pairs={{0,16},{2,18},{4,20},{6,22},{8,24},{10,26},{12,28},{14,30},{16,0},... | collective-permute-start | bytes 294920 | tf_op jit(solution)/shard_map/ppermute | solution.py:624
  267.7 12.6 %collective-permute-start.19 = (bf16[64,768]{1,0:T(8,128)(2,1)S(1)}, bf16[64,768]{1,0:T(8,128)(2,1)}, u32[]{:S(2)}, u32[]{:S(2)}) collective-permute-start(bf16[64,768]{1,0:T(8,128)(2,1)S(1)} %get-tuple-element.341), channel_id=1, source_target_pairs={{0,8},{2,10},{4,12},{6,14},{8,0},{10,2},{12,4},{14,6},{16,24},{18,... | collective-permute-start | bytes 294920 | tf_op jit(solution)/shard_map/ppermute | solution.py:624
  270.4 18.0 %collective-permute-start.22 = (bf16[512,768]{1,0:T(8,128)(2,1)}, bf16[512,768]{1,0:T(8,128)(2,1)}, u32[]{:S(2)}, u32[]{:S(2)}) collective-permute-start(bf16[512,768]{1,0:T(8,128)(2,1)} %add_convert_fusion.1), channel_id=1, source_target_pairs={{0,1},{1,0},{2,3},{3,2},{4,5},{5,4},{6,7},{7,6},{8,9},{9,8},{10,11... | collective-permute-start | bytes 2359304 | tf_op jit(solution)/shard_map/ppermute | solution.py:627
  280.4 21.4 %collective-permute-start.24 = (bf16[128,1536]{1,0:T(8,128)(2,1)S(1)}, bf16[128,1536]{1,0:T(8,128)(2,1)}, u32[]{:S(2)}, u32[]{:S(2)}) collective-permute-start(bf16[128,1536]{1,0:T(8,128)(2,1)S(1)} %constant_dynamic-update-slice_fusion.sources_0_), channel_id=1, source_target_pairs={{0,8},{2,10},{4,12},{6,14},{8,0},{10,2},{12,4},{14,6},{16,24},{18,... | collective-permute-start | bytes 1179656 | tf_op jit(solution)/shard_map/ppermute | solution.py:624
  289.8 12.0 %collective-permute-start.23 = (bf16[256,768]{1,0:T(8,128)(2,1)S(1)}, bf16[256,768]{1,0:T(8,128)(2,1)}, u32[]{:S(2)}, u32[]{:S(2)}) collective-permute-start(bf16[256,768]{1,0:T(8,128)(2,1)S(1)} %add_convert_fusion.4), channel_id=1, source_target_pairs={{0,4},{2,6},{4,0},{6,2},{8,12},{10,14},{12,8},{14,10},{16,20},{18,... | collective-permute-start | bytes 1179656 | tf_op jit(solution)/shard_map/ppermute | solution.py:624
  292.8 8.9 %collective-permute-start.25 = (bf16[64,768]{1,0:T(8,128)(2,1)S(1)}, bf16[64,768]{1,0:T(8,128)(2,1)S(1)}, u32[]{:S(2)}, u32[]{:S(2)}) collective-permute-start(bf16[64,768]{1,0:T(8,128)(2,1)S(1)} %add_convert_fusion.17), channel_id=1, source_target_pairs={{0,16},{2,18},{4,20},{6,22},{8,24},{10,26},{12,28},{14,30},{16,0},... | collective-permute-start | bytes 294920 | tf_op jit(solution)/shard_map/ppermute | solution.py:624
  301.8 12.1 %collective-permute-start.31 = (bf16[128,1536]{1,0:T(8,128)(2,1)S(1)}, bf16[128,1536]{1,0:T(8,128)(2,1)S(1)}, u32[]{:S(2)}, u32[]{:S(2)}) collective-permute-start(bf16[128,1536]{1,0:T(8,128)(2,1)S(1)} %constant_dynamic-update-slice_fusion.sources_0_), channel_id=1, source_target_pairs={{0,4},{2,6},{4,0},{6,2},{8,12},{10,14},{12,8},{14,10},{16,20},{18,... | collective-permute-start | bytes 1179656 | tf_op jit(solution)/shard_map/ppermute | solution.py:624
  301.9 12.0 %collective-permute-start.27 = (bf16[128,768]{1,0:T(8,128)(2,1)S(1)}, bf16[128,768]{1,0:T(8,128)(2,1)S(1)}, u32[]{:S(2)}, u32[]{:S(2)}) collective-permute-start(bf16[128,768]{1,0:T(8,128)(2,1)S(1)} %pad_maximum_fusion.12), channel_id=1, source_target_pairs={{0,8},{2,10},{4,12},{6,14},{8,0},{10,2},{12,4},{14,6},{16,24},{18,... | collective-permute-start | bytes 589832 | tf_op jit(solution)/shard_map/ppermute | solution.py:624
  313.9 12.0 %collective-permute-start.36 = (bf16[128,1536]{1,0:T(8,128)(2,1)}, bf16[128,1536]{1,0:T(8,128)(2,1)S(1)}, u32[]{:S(2)}, u32[]{:S(2)}) collective-permute-start(bf16[128,1536]{1,0:T(8,128)(2,1)} %collective-permute-done.24.sources_1_), channel_id=1, source_target_pairs={{0,4},{2,6},{4,0},{6,2},{8,12},{10,14},{12,8},{14,10},{16,20},{18,... | collective-permute-start | bytes 1179656 | tf_op jit(solution)/shard_map/ppermute | solution.py:624
  325.8 10.2 %collective-permute-start.44 = (bf16[128,1536]{1,0:T(8,128)(2,1)S(1)}, bf16[128,1536]{1,0:T(8,128)(2,1)S(1)}, u32[]{:S(2)}, u32[]{:S(2)}) collective-permute-start(bf16[128,1536]{1,0:T(8,128)(2,1)S(1)} %collective-permute-done.36.sources_3_), channel_id=1, source_target_pairs={{0,2},{2,0},{4,6},{6,4},{8,10},{10,8},{12,14},{14,12},{16,18},{18,... | collective-permute-start | bytes 1179656 | tf_op jit(solution)/shard_map/ppermute | solution.py:624
  325.9 11.8 %collective-permute-start.43 = (bf16[128,1536]{1,0:T(8,128)(2,1)S(1)}, bf16[128,1536]{1,0:T(8,128)(2,1)S(1)}, u32[]{:S(2)}, u32[]{:S(2)}) collective-permute-start(bf16[128,1536]{1,0:T(8,128)(2,1)S(1)} %collective-permute-done.31.sources_2_), channel_id=1, source_target_pairs={{0,2},{2,0},{4,6},{6,4},{8,10},{10,8},{12,14},{14,12},{16,18},{18,... | collective-permute-start | bytes 1179656 | tf_op jit(solution)/shard_map/ppermute | solution.py:624
  326.4 11.3 %collective-permute-start.42 = (bf16[128,1536]{1,0:T(8,128)(2,1)}, bf16[128,1536]{1,0:T(8,128)(2,1)S(1)}, u32[]{:S(2)}, u32[]{:S(2)}) collective-permute-start(bf16[128,1536]{1,0:T(8,128)(2,1)} %collective-permute-done.24.sources_1_), channel_id=1, source_target_pairs={{0,2},{2,0},{4,6},{6,4},{8,10},{10,8},{12,14},{14,12},{16,18},{18,... | collective-permute-start | bytes 1179656 | tf_op jit(solution)/shard_map/ppermute | solution.py:624
  326.4 12.7 %collective-permute-start.41 = (bf16[128,1536]{1,0:T(8,128)(2,1)S(1)}, bf16[128,1536]{1,0:T(8,128)(2,1)}, u32[]{:S(2)}, u32[]{:S(2)}) collective-permute-start(bf16[128,1536]{1,0:T(8,128)(2,1)S(1)} %constant_dynamic-update-slice_fusion.sources_0_), channel_id=1, source_target_pairs={{0,2},{2,0},{4,6},{6,4},{8,10},{10,8},{12,14},{14,12},{16,18},{18,... | collective-permute-start | bytes 1179656 | tf_op jit(solution)/shard_map/ppermute | solution.py:624
  335.5 12.3 %collective-permute-start.38 = (bf16[256,768]{1,0:T(8,128)(2,1)}, bf16[256,768]{1,0:T(8,128)(2,1)}, u32[]{:S(2)}, u32[]{:S(2)}) collective-permute-start(bf16[256,768]{1,0:T(8,128)(2,1)} %constant_dynamic-update-slice_fusion.5.groups_1__0_), channel_id=1, source_target_pairs={{0,4},{2,6},{4,0},{6,2},{8,12},{10,14},{12,8},{14,10},{16,20},{18,... | collective-permute-start | bytes 1179656 | tf_op jit(solution)/shard_map/ppermute | solution.py:624
  336.1 16.9 %collective-permute-start.32 = (bf16[256,768]{1,0:T(8,128)(2,1)S(1)}, bf16[256,768]{1,0:T(8,128)(2,1)}, u32[]{:S(2)}, u32[]{:S(2)}) collective-permute-start(bf16[256,768]{1,0:T(8,128)(2,1)S(1)} %constant_dynamic-update-slice_fusion.2.groups_0__0_), channel_id=1, source_target_pairs={{0,4},{2,6},{4,0},{6,2},{8,12},{10,14},{12,8},{14,10},{16,20},{18,... | collective-permute-start | bytes 1179656 | tf_op jit(solution)/shard_map/ppermute | solution.py:624
  (37 other events, 332.8 us)
